TPU v7x, 512 devices: a whole 4x8x8 slice. The times are simulated.
512 devices in a mesh: dp: 64 (over x, y, core), code: 8 (over z).
Axes of the slice: x: 4, y: 8, z: 8, core: 2. Of those that a mesh axis runs over, the one named last changes fastest.
Arguments:
- items: float32 [65536, 512], P(('dp', 'code')), may hold values from -6 to 6
- codewords: float32 [8192, 512], P('code'), may hold values from -6 to 6
- assign: int32 [65536], P('dp'), may hold values from 0 to 8191, as said below
Outputs:
- new_codewords: float32 [8192, 512], P('code', 'dp')
- residual: float32 [65536, 512], P(('dp', 'code'))
Inputs may be any that keep to these rules, and one draw needn't show every extreme that they name: `assign`: the items are laid out in aligned blocks of 128 (the items of one device). Splitting the codewords into equal ranges, one per index of code, the items of one block name codewords of exactly half of the ranges, 32 items for each such range.
All inputs are finite; a program needn't handle non-finite values.
Results may differ from a plain program's by a relative error of at most 0.0003.
Values sent between devices are 32-bit elements; how exact they have to be, the bound alone decides.
No kernel may reach another device: no remote copies, remote signals or barrier semaphores. Data moves between devices by JAX's collectives and lax.ppermute only.
A program may use at most 64 MiB of HBM per device.

v0:
```python
import jax
import jax.numpy as jnp
from jax import lax
from jax.sharding import PartitionSpec as P

K = 8192
ITERS = 3


epsilon = 1e-05
inverse_temp = 64.0


def unit_rows(values):
    return values * lax.rsqrt(jnp.mean(values * values, axis=-1, keepdims=True) + epsilon)


def kernel_of(rows_block, scaled):
    return jnp.exp(
        jnp.dot(
            unit_rows(rows_block),
            scaled.T,
            precision=lax.Precision.HIGHEST,
            preferred_element_type=jnp.float32,
        )
    )


def column_scale(col_part):
    summed = lax.psum(col_part, "dp")
    return 1.0 / (K * summed)


def row_scaling(row_part, total_items):
    summed = lax.psum(row_part, "code")
    return 1.0 / (total_items * summed)


def body(items, codewords, assign):
    code_count = lax.axis_size("code")
    dp_count = lax.axis_size("dp")
    local_codes = codewords.shape[0]
    width = items.shape[1]
    own_rows = items.shape[0]
    total_items = own_rows * code_count * dp_count
    scaled = unit_rows(codewords) * (inverse_temp / width)
    gathered = lax.all_gather(items, "code", axis=0, tiled=True)
    kernel_vals = kernel_of(gathered, scaled)
    col_part = jnp.sum(kernel_vals, axis=0)
    row_scale = jnp.ones((kernel_vals.shape[0],), jnp.float32)
    for sweep_index in range(ITERS):
        col_scale = column_scale(col_part)
        row_part = jnp.dot(
            kernel_vals,
            col_scale,
            precision=lax.Precision.HIGHEST,
            preferred_element_type=jnp.float32,
        )
        row_scale = row_scaling(row_part, total_items)
        col_part = jnp.dot(
            row_scale,
            kernel_vals,
            precision=lax.Precision.HIGHEST,
            preferred_element_type=jnp.float32,
        )
    mass = lax.psum(col_part, "dp")
    numerator = lax.dot_general(
        kernel_vals,
        row_scale[:, None] * gathered,
        (((0,), (0,)), ((), ())),
        precision=lax.Precision.HIGHEST,
        preferred_element_type=jnp.float32,
    )
    owned_sums = lax.psum_scatter(numerator, "dp", scatter_dimension=1, tiled=True)
    new_codewords = owned_sums / mass[:, None]
    my_code = lax.axis_index("code")
    offset = my_code * local_codes
    index_rows = assign - offset
    inside = (index_rows >= 0) & (index_rows < local_codes)
    picked = jnp.take(codewords, jnp.clip(index_rows, 0, local_codes - 1), axis=0)
    looked = lax.psum_scatter(
        jnp.where(inside[:, None], picked, jnp.float32(0.0)),
        "code",
        scatter_dimension=0,
        tiled=True,
    )
    residual = items - looked
    return (new_codewords, residual)


def solution(mesh):
    in_specs = (P(("dp", "code"), None), P("code", None), P("dp"))
    out_specs = (P("code", "dp"), P(("dp", "code"), None))
    return jax.shard_map(body, mesh=mesh, in_specs=in_specs, out_specs=out_specs, check_vma=False)
```

profile of v0, /device:TPU:1, one launch (start us, length us, event | category | flops | bytes accessed | tf_op | source)
XLA Modules:
  0.0 671.3 jit_solution(14707872022729318664)
XLA Ops:
  7.2 0.0 all-gather.2.cloned.1.call-start
  7.2 0.7 all-gather.2.cloned.1.call-update
  7.9 0.0 reduce-scatter.5.cloned.1.call-start
  7.9 0.7 fusion.23
  8.6 5.6 gather_fusion
  14.3 2.0 select_select_fusion
  16.3 0.0 reduce-scatter.5.cloned.1.call-update
  16.3 0.0 reduce-scatter.3.cloned.1.call-start
  16.4 1.5 copy-done
  17.9 0.2 multiply_reduce_fusion
  18.1 38.1 %all-gather.2.cloned.1.call-done = f32[1024,512]{1,0:T(8,128)} async-done(((f32[128,512]{1,0:T(8,128)}), f32[1024,512]{1,0:T(8,128)}) %all-gather.2.cloned.1.call-update) | async-done | bytes 2097168 | tf_op jit(solution)/shard_map/all_gather | solution.py:47
  56.2 2.0 multiply_reduce_fusion.1
  58.2 0.3 copy-done.1
  58.4 9.1 %exponential_reduce_fusion = (f32[1024]{0:T(1024)S(1)}, f32[1024,1024]{1,0:T(8,128)}) fusion(f32[1024,512]{1,0:T(8,128)S(1)} %copy-done, f32[1024]{0:T(1024)S(1)} %add_rsqrt_fusion, f32[1024,512]{1,0:T(8,128)S(1)} %copy-done.1, f32[1024]{0:T(1024)S(1)} %add_rsqrt_fusion.1), kind=kOutput, calls=%fused_computation.15 | convolution fusion | flops 6445071360 | bytes 8400896 | tf_op jit(solution)/shard_map/dot_general | solution.py:20
  67.5 128.1 %psum.49 = f32[1024]{0:T(1024)S(1)} all-reduce(f32[1024]{0:T(1024)S(1)} %get-tuple-element.4), channel_id=1, replica_groups=mesh['dp'=64,'code'=8] {'dp'}, use_global_device_ids=true, to_apply=%region_3.0 | all-reduce | flops 1024 | bytes 8192 | tf_op jit(solution)/shard_map/psum | solution.py:30
  195.6 6.2 fusion.12
  201.8 11.9 %psum.50 = f32[1024]{0:T(1024)S(1)} all-reduce(f32[1024]{0:T(1024)S(1)} %bitcast.21), channel_id=1, replica_groups=mesh['dp'=64,'code'=8] {'code'}, use_global_device_ids=true, to_apply=%region_4.0 | all-reduce | flops 1024 | bytes 8192 | tf_op jit(solution)/shard_map/psum | solution.py:35
  213.7 4.5 fusion.10
  218.2 128.7 %psum.51 = f32[1024]{0:T(1024)S(1)} all-reduce(f32[1024]{0:T(1024)S(1)} %bitcast.23), channel_id=1, replica_groups=mesh['dp'=64,'code'=8] {'dp'}, use_global_device_ids=true, to_apply=%region_5.0 | all-reduce | flops 1024 | bytes 8192 | tf_op jit(solution)/shard_map/psum | solution.py:30
  347.0 6.2 fusion.8
  353.1 10.7 %psum.52 = f32[1024]{0:T(1024)S(1)} all-reduce(f32[1024]{0:T(1024)S(1)} %bitcast.25), channel_id=1, replica_groups=mesh['dp'=64,'code'=8] {'code'}, use_global_device_ids=true, to_apply=%region_6.0 | all-reduce | flops 1024 | bytes 8192 | tf_op jit(solution)/shard_map/psum | solution.py:35
  363.8 4.5 fusion.6
  368.3 127.6 %psum.53 = f32[1024]{0:T(1024)S(1)} all-reduce(f32[1024]{0:T(1024)S(1)} %bitcast.27), channel_id=1, replica_groups=mesh['dp'=64,'code'=8] {'dp'}, use_global_device_ids=true, to_apply=%region_7.0 | all-reduce | flops 1024 | bytes 8192 | tf_op jit(solution)/shard_map/psum | solution.py:30
  495.9 6.3 fusion.4
  502.2 12.6 %psum.54 = f32[1024]{0:T(1024)S(1)} all-reduce(f32[1024]{0:T(1024)S(1)} %bitcast.29), channel_id=1, replica_groups=mesh['dp'=64,'code'=8] {'code'}, use_global_device_ids=true, to_apply=%region_8.0 | all-reduce | flops 1024 | bytes 8192 | tf_op jit(solution)/shard_map/psum | solution.py:35
  514.8 10.3 %fusion.2 = f32[1024,512]{0,1:T(8,128)} fusion(f32[1024,1024]{1,0:T(8,128)} %get-tuple-element.5, f32[1024,512]{1,0:T(8,128)S(1)} %copy-done.2, f32[1024]{0:T(1024)S(1)} %multiply_divide_fusion), kind=kOutput, calls=%fused_computation.3 | convolution fusion | flops 6442975232 | bytes 8392704 | tf_op jit(solution)/shard_map/dot_general | solution.py:67
  525.1 0.0 reduce-scatter.3.cloned.1.call-update
  525.2 4.5 fusion
  529.7 127.9 %psum.55 = f32[1024]{0:T(1024)S(1)} all-reduce(f32[1024]{0:T(1024)S(1)} %bitcast.20), channel_id=1, replica_groups=mesh['dp'=64,'code'=8] {'dp'}, use_global_device_ids=true, to_apply=%region_10.0 | all-reduce | flops 1024 | bytes 8192 | tf_op jit(solution)/shard_map/psum | solution.py:66
  657.7 1.7 sub.11
  659.4 4.0 reduce-scatter.3.cloned.1.call-done
  663.4 1.4 broadcast_divide_fusion
  (18 shorter events, 0.1 us)
Async XLA Ops:
  7.2 49.0 %all-gather.2.cloned.1.call-start = ((), (), s32[]{:S(2)}) async-start(), calls=%async_computation.2 | async-start | bytes 2359296 | tf_op jit(solution)/shard_map/all_gather | solution.py:47
  7.9 649.7 %reduce-scatter.5.cloned.1.call-start = ((), (), s32[]{:S(2)}) async-start(), calls=%async_computation.4 | async-start | bytes 2359296 | tf_op jit(solution)/shard_map/reduce_scatter | solution.py:81
  8.6 5.6 copy-start.4
  16.3 1.6 copy-start
  16.3 647.1 %reduce-scatter.3.cloned.1.call-start = ((), (), s32[]{:S(2)}) async-start(), calls=%async_computation.3 | async-start | bytes 2129920 | tf_op jit(solution)/shard_map/reduce_scatter | solution.py:74
  56.2 2.2 copy-start.1
  495.9 18.9 %copy-start.2 = (f32[1024,512]{1,0:T(8,128)S(1)}, f32[1024,512]{1,0:T(8,128)}, u32[]{:S(2)}) copy-start(f32[1024,512]{1,0:T(8,128)} %all-gather.2.cloned.1.call-done) | copy-start | bytes 6291460
  525.2 132.5 %copy-start.3 = (f32[128,512]{1,0:T(8,128)S(1)}, f32[128,512]{1,0:T(8,128)}, u32[]{:S(2)}) copy-start(f32[128,512]{1,0:T(8,128)} %param.3) | copy-start | bytes 786436
Sparse Core Ops, SparseCore 0:
  10.1 46.0 all-gather.1
  59.0 43.4 reduce-scatter.4
  525.3 138.0 reduce-scatter.2
where the time goes:
time: 676 us; the launch traced here: 671 us
  blocking collectives  548 us (81%)
  matrix products  51.6 us (8%)
  waiting for transfers between devices  42.8 us (6%)
  between operations  13.9 us (2%)
  other arithmetic  7.99 us (1%)
  local copies, waits for them, and re-layouts  7.4 us (1%)
    psum x3, blocking collectives, column_scale(): summed = lax.psum(col_part, 'dp')  384 us
    psum x1, blocking collectives, body(): mass = lax.psum(col_part, 'dp')  128 us
    all_gather x1, waiting for transfers between devices, body(): gathered = lax.all_gather(items, 'code', axis=0, tiled=True)  38.1 us
    psum x3, blocking collectives, row_scaling(): summed = lax.psum(row_part, 'code')  35.2 us
    dot_general x3, matrix products, body(): jnp.dot(kernel_vals, col_scale, precision=lax.Precision.HIGHEST, preferre...  18.7 us
  transfers between devices with their start and end apart: 3, of which 2 were waited for; matrix products, arithmetic and copies ran while one was open for 10% of the time, Pallas kernels for 0%

commit v1 on v0

v1 whole, which is shorter than its diff:
```python
import jax
import jax.numpy as jnp
from jax import lax
from jax.sharding import Mesh, PartitionSpec as P

K = 8192
ITERS = 3
DP = ("x", "y", "core")

epsilon = 1e-05
inverse_temp = 64.0


def unit_rows(values):
    return values * lax.rsqrt(jnp.mean(values * values, axis=-1, keepdims=True) + epsilon)


def exchange_sum(part, axes):
    count = lax.axis_size(axes)
    copies = jnp.broadcast_to(part[None], (count,) + part.shape)
    return jnp.sum(lax.all_to_all(copies, axes, 0, 0), axis=0)


def scatter_sum(blocks, axis):
    return jnp.sum(lax.all_to_all(blocks, axis, 0, 0), axis=0)


def body(items, codewords, assign):
    code_count = lax.axis_size("code")
    dp_count = lax.axis_size(DP)
    local_codes = codewords.shape[0]
    own_rows, width = items.shape
    total_items = own_rows * code_count * dp_count
    scaled = unit_rows(codewords) * (inverse_temp / width)
    gathered = lax.all_gather(items, "code", axis=0, tiled=True)
    logits = lax.dot_general(
        unit_rows(gathered),
        scaled,
        (((1,), (1,)), ((), ())),
        precision=lax.Precision.HIGH,
        preferred_element_type=jnp.float32,
    )
    kernel_vals = jnp.exp(logits)
    col_part = jnp.sum(kernel_vals, axis=0)
    for _ in range(ITERS):
        col_scale = 1.0 / (K * exchange_sum(col_part, DP))
        row_part = jnp.sum(kernel_vals * col_scale[None, :], axis=1)
        row_scale = 1.0 / (total_items * exchange_sum(row_part, "code"))
        col_part = jnp.sum(kernel_vals * row_scale[:, None], axis=0)
    mass = exchange_sum(col_part, DP)

    nx, ny, nc = lax.axis_size("x"), lax.axis_size("y"), lax.axis_size("core")
    cols = width // dp_count
    numerator = lax.dot_general(
        row_scale[:, None] * gathered,
        kernel_vals,
        (((0,), (0,)), ((), ())),
        precision=lax.Precision.HIGH,
        preferred_element_type=jnp.float32,
    )
    halves = numerator.reshape(nx * ny, nc, cols, local_codes)
    core = lax.axis_index("core")
    mine = lax.dynamic_index_in_dim(halves, core, 1, keepdims=False)
    other = lax.dynamic_index_in_dim(halves, 1 - core, 1, keepdims=False)
    chip = mine + lax.ppermute(other, "core", [(0, 1), (1, 0)])
    owned = scatter_sum(chip.reshape(nx, ny, cols, local_codes), "x")
    owned = scatter_sum(owned, "y")
    new_codewords = (owned / mass[None, :]).T

    my_code = lax.axis_index("code")
    offset = my_code * local_codes
    index_rows = assign - offset
    inside = (index_rows >= 0) & (index_rows < local_codes)
    picked = jnp.take(codewords, jnp.clip(index_rows, 0, local_codes - 1), axis=0)
    looked = lax.psum_scatter(
        jnp.where(inside[:, None], picked, jnp.float32(0.0)),
        "code",
        scatter_dimension=0,
        tiled=True,
    )
    residual = items - looked
    return (new_codewords, residual)


def solution(mesh):
    cores = 2
    ny = 8
    dp, code = mesh.devices.shape
    fine = Mesh(
        mesh.devices.reshape(dp // (ny * cores), ny, cores, code),
        ("x", "y", "core", "code"),
    )
    in_specs = (P(DP + ("code",), None), P("code", None), P(DP))
    out_specs = (P("code", DP), P(DP + ("code",), None))
    return jax.shard_map(body, mesh=fine, in_specs=in_specs, out_specs=out_specs, check_vma=False)
```

time: 676 us -> 256 us (0.38)
  blocking collectives: 548 us -> 36.8 us
  waiting for transfers between devices: 42.8 us -> 112 us
  matrix products: 51.6 us -> 11.6 us
  starting transfers between devices: 0.12 us -> 39.9 us
  other arithmetic: 7.99 us -> 29.7 us
    psum x7 -> x0, blocking collectives: 548 us -> none  [the longest x3 384 us: column_scale(): summed = lax.psum(col_part, 'dp')]
    all_to_all x0 -> x7, waiting for transfers between devices: none -> 62.9 us  [the longest x5 42.1 us: exchange_sum(): return jnp.sum(lax.all_to_all(copies, axes, 0, 0), axis=0)]
    dot_general x8 -> x2, matrix products: 51.6 us -> 11.6 us  [the longest x1 6.03 us: body(): lax.dot_general(row_scale[:, None] * gathered, kernel_vals, (((0,), (0,))...]
    all_to_all x0 -> x2, blocking collectives: none -> 36.8 us  [exchange_sum(): return jnp.sum(lax.all_to_all(copies, axes, 0, 0), axis=0)]
    all_to_all x0 -> x7, starting transfers between devices: none -> 36 us  [the longest x5 28.3 us: exchange_sum(): return jnp.sum(lax.all_to_all(copies, axes, 0, 0), axis=0)]
    reduce_sum x0 -> x15, other arithmetic: none -> 18.9 us  [the longest x3 8.8 us: body(): row_part = jnp.sum(kernel_vals * col_scale[None, :], axis=1)]
    all_gather x1, waiting for transfers between devices: 38.1 us -> 46.3 us  [body(): gathered = lax.all_gather(items, 'code', axis=0, tiled=True)]
  transfers between devices with their start and end apart: 3 -> 10, of which waited for: 2 -> 9; matrix products, arithmetic and copies ran while one was open for 10% -> 11% of each run, Pallas kernels for 0% -> 0%
where the time goes in v1:
time: 256 us; the launch traced here: 255 us
  waiting for transfers between devices  112 us (44%)
  starting transfers between devices  39.9 us (16%)
  blocking collectives  36.8 us (14%)
  other arithmetic  29.7 us (12%)
  between operations  14.3 us (6%)
  matrix products  11.6 us (5%)
  local copies, waits for them, and re-layouts  10.5 us (4%)
    all_gather x1, waiting for transfers between devices, body(): gathered = lax.all_gather(items, 'code', axis=0, tiled=True)  46.3 us
    all_to_all x5, waiting for transfers between devices, exchange_sum(): return jnp.sum(lax.all_to_all(copies, axes, 0, 0), axis=0)  42.1 us
    all_to_all x2, blocking collectives, exchange_sum(): return jnp.sum(lax.all_to_all(copies, axes, 0, 0), axis=0)  36.8 us
    all_to_all x5, starting transfers between devices, exchange_sum(): return jnp.sum(lax.all_to_all(copies, axes, 0, 0), axis=0)  28.3 us
    all_to_all x2, waiting for transfers between devices, scatter_sum(): return jnp.sum(lax.all_to_all(blocks, axis, 0, 0), axis=0)  20.8 us
    reduce_sum x3, other arithmetic, body(): row_part = jnp.sum(kernel_vals * col_scale[None, :], axis=1)  8.8 us
    reduce_sum x3, other arithmetic, body(): col_part = jnp.sum(kernel_vals * row_scale[:, None], axis=0)  8.49 us
    all_to_all x2, starting transfers between devices, scatter_sum(): return jnp.sum(lax.all_to_all(blocks, axis, 0, 0), axis=0)  7.73 us
  transfers between devices with their start and end apart: 10, of which 9 were waited for; matrix products, arithmetic and copies ran while one was open for 11% of the time, Pallas kernels for 0%

profile of v1, /device:TPU:1, one launch (start us, length us, event | category | flops | bytes accessed | tf_op | source)
XLA Modules:
  0.0 254.8 jit_solution(13360606303036772084)
XLA Ops:
  7.9 2.0 multiply_reduce_fusion.6
  9.9 46.3 %all-gather.2.cloned.1.call-done = f32[1024,512]{1,0:T(8,128)} async-done(((f32[128,512]{1,0:T(8,128)}), f32[1024,512]{1,0:T(8,128)}) %all-gather.2.cloned.1.call-update) | async-done | bytes 2097168 | tf_op jit(solution)/shard_map/all_gather | solution.py:35
  56.2 2.0 multiply_reduce_fusion.7
  58.4 5.6 %exponential_reduce_fusion = (f32[1024]{0:T(1024)S(1)}, f32[1024,1024]{1,0:T(8,128)}) fusion(f32[1024,512]{1,0:T(8,128)S(1)} %copy-done, f32[1024]{0:T(1024)S(1)} %add_rsqrt_fusion, f32[1024,512]{1,0:T(8,128)S(1)} %copy-done.1, f32[1024]{0:T(1024)S(1)} %add_rsqrt_fusion.1), kind=kOutput, calls=%fused_computation.9 | convolution fusion | flops 3223845888 | bytes 8400896 | tf_op jit(solution)/shard_map/dot_general | solution.py:36
  64.1 26.2 %all_to_all.52 = f32[64,1,1024]{2,1,0:T(1,128)S(1)} all-to-all(f32[64,1,1024]{2,1,0:T(1,128)S(1)} %broadcast_in_dim.31), channel_id=1, replica_groups=mesh['x'=4,'y'=8,'core'=2,'code'=8] {'x','y','core'}, dimensions={0} | all-to-all | bytes 524288 | tf_op jit(solution)/shard_map/all_to_all | solution.py:21
  90.5 2.9 %multiply_reduce_fusion.5 = f32[1024]{0:T(1024)S(1)} fusion(f32[1024,1024]{1,0:T(8,128)} %get-tuple-element.5, f32[1024]{0:T(1024)S(1)} %multiply_divide_fusion.5), kind=kLoop, calls=%fused_computation.6 | loop fusion | flops 2096128 | bytes 4202496 | tf_op jit(solution)/shard_map/reduce_sum | solution.py:47
  93.4 10.5 %all_to_all.53 = f32[8,1,1024]{2,1,0:T(1,128)S(1)} all-to-all(f32[8,1,1024]{2,1,0:T(1,128)S(1)} %broadcast_in_dim.32), channel_id=1, replica_groups=mesh['x'=4,'y'=8,'core'=2,'code'=8] {'code'}, dimensions={0} | all-to-all | bytes 65536 | tf_op jit(solution)/shard_map/all_to_all | solution.py:21
  104.0 2.8 %multiply_reduce_fusion.4 = f32[1024]{0:T(1024)S(1)} fusion(f32[1024,1024]{1,0:T(8,128)} %get-tuple-element.5, f32[1024]{0:T(1024)S(1)} %multiply_divide_fusion.4), kind=kLoop, calls=%fused_computation.5 | loop fusion | flops 2096128 | bytes 4202496 | tf_op jit(solution)/shard_map/reduce_sum | solution.py:49
  107.7 7.5 %all-to-all-start.2 = ((f32[64,1,1024]{2,1,0:T(1,128)}), f32[64,1,1024]{2,1,0:T(1,128)S(1)}, u32[]{:S(2)}, u32[]{:S(2)}) async-start(f32[64,1,1024]{2,1,0:T(1,128)} %broadcast_in_dim.33), calls=%async_computation.2 | async-start | bytes 524288 | tf_op jit(solution)/shard_map/all_to_all | solution.py:21
  115.1 12.0 %all-to-all-done.2 = f32[64,1,1024]{2,1,0:T(1,128)S(1)} async-done(((f32[64,1,1024]{2,1,0:T(1,128)}), f32[64,1,1024]{2,1,0:T(1,128)S(1)}, u32[]{:S(2)}, u32[]{:S(2)}) %all-to-all-start.2) | async-done | bytes 262176 | tf_op jit(solution)/shard_map/all_to_all | solution.py:21
  127.3 2.9 %multiply_reduce_fusion.3 = f32[1024]{0:T(1024)S(1)} fusion(f32[1024,1024]{1,0:T(8,128)} %get-tuple-element.5, f32[1024]{0:T(1024)S(1)} %multiply_divide_fusion.3), kind=kLoop, calls=%fused_computation.4 | loop fusion | flops 2096128 | bytes 4202496 | tf_op jit(solution)/shard_map/reduce_sum | solution.py:47
  130.8 3.3 %all-to-all-start.3 = ((f32[8,1,1024]{2,1,0:T(1,128)}), f32[8,1,1024]{2,1,0:T(1,128)S(1)}, u32[]{:S(2)}, u32[]{:S(2)}) async-start(f32[8,1,1024]{2,1,0:T(1,128)} %broadcast_in_dim.34), calls=%async_computation.3 | async-start | bytes 65536 | tf_op jit(solution)/shard_map/all_to_all | solution.py:21
  134.2 4.9 %gather_fusion = f32[1024,512]{1,0:T(8,128)} fusion(f32[1024,512]{1,0:T(8,128)S(1)} %copy-done, s32[1024]{0:T(1024)S(1)} %fusion.11), kind=kCustom, calls=%fused_computation | custom fusion | bytes 4198400 | tf_op jit(solution)/shard_map/jit(_take)/gather | solution.py:74
  139.1 1.9 all-to-all-done.3
  141.0 2.9 %multiply_reduce_fusion.2 = f32[1024]{0:T(1024)S(1)} fusion(f32[1024,1024]{1,0:T(8,128)} %get-tuple-element.5, f32[1024]{0:T(1024)S(1)} %multiply_divide_fusion.2), kind=kLoop, calls=%fused_computation.3 | loop fusion | flops 2096128 | bytes 4202496 | tf_op jit(solution)/shard_map/reduce_sum | solution.py:49
  144.8 7.2 %all-to-all-start.4 = ((f32[64,1,1024]{2,1,0:T(1,128)}), f32[64,1,1024]{2,1,0:T(1,128)S(1)}, u32[]{:S(2)}, u32[]{:S(2)}) async-start(f32[64,1,1024]{2,1,0:T(1,128)} %broadcast_in_dim.35), calls=%async_computation.4 | async-start | bytes 524288 | tf_op jit(solution)/shard_map/all_to_all | solution.py:21
  152.1 2.0 select_select_fusion
  154.1 9.9 %all-to-all-done.4 = f32[64,1,1024]{2,1,0:T(1,128)S(1)} async-done(((f32[64,1,1024]{2,1,0:T(1,128)}), f32[64,1,1024]{2,1,0:T(1,128)S(1)}, u32[]{:S(2)}, u32[]{:S(2)}) %all-to-all-start.4) | async-done | bytes 262176 | tf_op jit(solution)/shard_map/all_to_all | solution.py:21
  164.2 3.0 %multiply_reduce_fusion.1 = f32[1024]{0:T(1024)S(1)} fusion(f32[1024,1024]{1,0:T(8,128)} %get-tuple-element.5, f32[1024]{0:T(1024)S(1)} %multiply_divide_fusion.1), kind=kLoop, calls=%fused_computation.2 | loop fusion | flops 2096128 | bytes 4202496 | tf_op jit(solution)/shard_map/reduce_sum | solution.py:47
  167.9 3.8 %all-to-all-start.5 = ((f32[8,1,1024]{2,1,0:T(1,128)}), f32[8,1,1024]{2,1,0:T(1,128)S(1)}, u32[]{:S(2)}, u32[]{:S(2)}) async-start(f32[8,1,1024]{2,1,0:T(1,128)} %broadcast_in_dim.36), calls=%async_computation.5 | async-start | bytes 65536 | tf_op jit(solution)/shard_map/all_to_all | solution.py:21
  171.7 7.1 %all-to-all-done.5 = f32[8,1,1024]{2,1,0:T(1,128)S(1)} async-done(((f32[8,1,1024]{2,1,0:T(1,128)}), f32[8,1,1024]{2,1,0:T(1,128)S(1)}, u32[]{:S(2)}, u32[]{:S(2)}) %all-to-all-start.5) | async-done | bytes 32800 | tf_op jit(solution)/shard_map/all_to_all | solution.py:21
  178.9 6.0 %fusion = f32[512,1024]{1,0:T(8,128)S(1)} fusion(f32[1024,1024]{1,0:T(8,128)} %get-tuple-element.5, f32[1024,512]{1,0:T(8,128)S(1)} %copy-done.2, f32[1024]{0:T(1024)S(1)} %multiply_divide_fusion), kind=kOutput, calls=%fused_computation.7 | convolution fusion | flops 3221749760 | bytes 8392704 | tf_op jit(solution)/shard_map/dot_general | solution.py:54
  186.3 3.8 %collective-permute-start = (f32[32,8,1024]{2,1,0:T(8,128)S(1)}, f32[32,8,1024]{2,1,0:T(8,128)S(1)}, u32[]{:S(2)}, u32[]{:S(2)}) collective-permute-start(f32[32,8,1024]{2,1,0:T(8,128)S(1)} %dynamic-slice_bitcast_fusion), channel_id=1, source_target_pairs={{0,8},{8,0},{1,9},{9,1},{2,10},{10,2},{3,11},{11,3},{4,12},{12,4},... | collective-permute-start | bytes 3145736 | tf_op jit(solution)/shard_map/ppermute | solution.py:65
  190.1 2.3 collective-permute-done
  192.4 2.4 bitcast_add_fusion
  194.8 3.9 %all-to-all-start.6 = ((f32[4,8,8,1024]{3,2,1,0:T(8,128)}), f32[4,8,8,1024]{3,2,1,0:T(8,128)S(1)}, u32[]{:S(2)}, u32[]{:S(2)}) async-start(f32[4,8,8,1024]{3,2,1,0:T(8,128)} %bitcast.3), calls=%async_computation.6 | async-start | bytes 2097152 | tf_op jit(solution)/shard_map/all_to_all | solution.py:25
  198.7 2.8 %multiply_reduce_fusion = f32[1024]{0:T(1024)S(1)} fusion(f32[1024,1024]{1,0:T(8,128)} %get-tuple-element.5, f32[1024]{0:T(1024)S(1)} %multiply_divide_fusion), kind=kLoop, calls=%fused_computation.1 | loop fusion | flops 2096128 | bytes 4202496 | tf_op jit(solution)/shard_map/reduce_sum | solution.py:49
  201.5 11.7 %all-to-all-done.6 = f32[4,8,8,1024]{3,2,1,0:T(8,128)S(1)} async-done(((f32[4,8,8,1024]{3,2,1,0:T(8,128)}), f32[4,8,8,1024]{3,2,1,0:T(8,128)S(1)}, u32[]{:S(2)}, u32[]{:S(2)}) %all-to-all-start.6) | async-done | bytes 1048608 | tf_op jit(solution)/shard_map/all_to_all | solution.py:25
  214.1 6.5 %all-to-all-start.8 = ((f32[64,1,1024]{2,1,0:T(1,128)}), f32[64,1,1024]{2,1,0:T(1,128)S(1)}, u32[]{:S(2)}, u32[]{:S(2)}) async-start(f32[64,1,1024]{2,1,0:T(1,128)} %broadcast_in_dim.37), calls=%async_computation.8 | async-start | bytes 524288 | tf_op jit(solution)/shard_map/all_to_all | solution.py:21
  221.3 11.2 %all-to-all-done.8 = f32[64,1,1024]{2,1,0:T(1,128)S(1)} async-done(((f32[64,1,1024]{2,1,0:T(1,128)}), f32[64,1,1024]{2,1,0:T(1,128)S(1)}, u32[]{:S(2)}, u32[]{:S(2)}) %all-to-all-start.8) | async-done | bytes 262176 | tf_op jit(solution)/shard_map/all_to_all | solution.py:21
  232.5 3.9 %all-to-all-start.7 = ((f32[8,8,1024]{2,1,0:T(8,128)}), f32[8,8,1024]{2,1,0:T(8,128)S(1)}, u32[]{:S(2)}, u32[]{:S(2)}) async-start(f32[8,8,1024]{2,1,0:T(8,128)} %reduce_sum.176), calls=%async_computation.7 | async-start | bytes 524288 | tf_op jit(solution)/shard_map/all_to_all | solution.py:25
  238.3 9.0 %all-to-all-done.7 = f32[8,8,1024]{2,1,0:T(8,128)S(1)} async-done(((f32[8,8,1024]{2,1,0:T(8,128)}), f32[8,8,1024]{2,1,0:T(8,128)S(1)}, u32[]{:S(2)}, u32[]{:S(2)}) %all-to-all-start.7) | async-done | bytes 262176 | tf_op jit(solution)/shard_map/all_to_all | solution.py:25
  (48 shorter events, 10.4 us)
Async XLA Ops:
  7.2 49.0 %all-gather.2.cloned.1.call-start = ((), (), s32[]{:S(2)}) async-start(), calls=%async_computation.10 | async-start | bytes 2359296 | tf_op jit(solution)/shard_map/all_gather | solution.py:35
  7.9 50.3 %copy-start = (f32[1024,512]{1,0:T(8,128)S(1)}, f32[1024,512]{1,0:T(8,128)}, u32[]{:S(2)}) copy-start(f32[1024,512]{1,0:T(8,128)} %param.4) | copy-start | bytes 6291460
  56.2 2.2 copy-start.1
  107.7 19.5 %all-to-all-start.2 = ((f32[64,1,1024]{2,1,0:T(1,128)}), f32[64,1,1024]{2,1,0:T(1,128)S(1)}, u32[]{:S(2)}, u32[]{:S(2)}) async-start(f32[64,1,1024]{2,1,0:T(1,128)} %broadcast_in_dim.33), calls=%async_computation.2 | async-start | bytes 524288 | tf_op jit(solution)/shard_map/all_to_all | solution.py:21
  127.3 6.9 %copy-start.6 = (s32[1024]{0:T(1024)S(1)}, s32[1024]{0:T(1024)}, u32[]{:S(2)}) copy-start(s32[1024]{0:T(1024)} %param.5) | copy-start | bytes 12292
  130.8 10.1 %all-to-all-start.3 = ((f32[8,1,1024]{2,1,0:T(1,128)}), f32[8,1,1024]{2,1,0:T(1,128)S(1)}, u32[]{:S(2)}, u32[]{:S(2)}) async-start(f32[8,1,1024]{2,1,0:T(1,128)} %broadcast_in_dim.34), calls=%async_computation.3 | async-start | bytes 65536 | tf_op jit(solution)/shard_map/all_to_all | solution.py:21
  141.0 11.0 %copy-start.3 = (f32[1024,512]{1,0:T(8,128)S(1)}, f32[1024,512]{1,0:T(8,128)}, u32[]{:S(2)}) copy-start(f32[1024,512]{1,0:T(8,128)} %gather_fusion) | copy-start | bytes 6291460
  144.8 19.2 %all-to-all-start.4 = ((f32[64,1,1024]{2,1,0:T(1,128)}), f32[64,1,1024]{2,1,0:T(1,128)S(1)}, u32[]{:S(2)}, u32[]{:S(2)}) async-start(f32[64,1,1024]{2,1,0:T(1,128)} %broadcast_in_dim.35), calls=%async_computation.4 | async-start | bytes 524288 | tf_op jit(solution)/shard_map/all_to_all | solution.py:21
  152.0 84.4 %reduce-scatter.2.cloned.1.call-start = ((), (), s32[]{:S(2)}) async-start(), calls=%async_computation.11 | async-start | bytes 2359296 | tf_op jit(solution)/shard_map/reduce_scatter | solution.py:75
  164.2 14.7 %copy-start.2 = (f32[1024,512]{1,0:T(8,128)S(1)}, f32[1024,512]{1,0:T(8,128)}, u32[]{:S(2)}) copy-start(f32[1024,512]{1,0:T(8,128)} %all-gather.2.cloned.1.call-done) | copy-start | bytes 6291460
  167.9 10.9 %all-to-all-start.5 = ((f32[8,1,1024]{2,1,0:T(1,128)}), f32[8,1,1024]{2,1,0:T(1,128)S(1)}, u32[]{:S(2)}, u32[]{:S(2)}) async-start(f32[8,1,1024]{2,1,0:T(1,128)} %broadcast_in_dim.36), calls=%async_computation.5 | async-start | bytes 65536 | tf_op jit(solution)/shard_map/all_to_all | solution.py:21
  184.9 1.3 copy-start.4
  186.3 6.1 %collective-permute-start = (f32[32,8,1024]{2,1,0:T(8,128)S(1)}, f32[32,8,1024]{2,1,0:T(8,128)S(1)}, u32[]{:S(2)}, u32[]{:S(2)}) collective-permute-start(f32[32,8,1024]{2,1,0:T(8,128)S(1)} %dynamic-slice_bitcast_fusion), channel_id=1, source_target_pairs={{0,8},{8,0},{1,9},{9,1},{2,10},{10,2},{3,11},{11,3},{4,12},{12,4},... | collective-permute-start | bytes 3145736 | tf_op jit(solution)/shard_map/ppermute | solution.py:65
  194.8 18.4 %all-to-all-start.6 = ((f32[4,8,8,1024]{3,2,1,0:T(8,128)}), f32[4,8,8,1024]{3,2,1,0:T(8,128)S(1)}, u32[]{:S(2)}, u32[]{:S(2)}) async-start(f32[4,8,8,1024]{3,2,1,0:T(8,128)} %bitcast.3), calls=%async_computation.6 | async-start | bytes 2097152 | tf_op jit(solution)/shard_map/all_to_all | solution.py:25
  201.5 35.0 %copy-start.5 = (f32[128,512]{1,0:T(8,128)S(1)}, f32[128,512]{1,0:T(8,128)}, u32[]{:S(2)}) copy-start(f32[128,512]{1,0:T(8,128)} %param.3) | copy-start | bytes 786436
  214.1 18.5 %all-to-all-start.8 = ((f32[64,1,1024]{2,1,0:T(1,128)}), f32[64,1,1024]{2,1,0:T(1,128)S(1)}, u32[]{:S(2)}, u32[]{:S(2)}) async-start(f32[64,1,1024]{2,1,0:T(1,128)} %broadcast_in_dim.37), calls=%async_computation.8 | async-start | bytes 524288 | tf_op jit(solution)/shard_map/all_to_all | solution.py:21
  232.5 14.8 %all-to-all-start.7 = ((f32[8,8,1024]{2,1,0:T(8,128)}), f32[8,8,1024]{2,1,0:T(8,128)S(1)}, u32[]{:S(2)}, u32[]{:S(2)}) async-start(f32[8,8,1024]{2,1,0:T(8,128)} %reduce_sum.176), calls=%async_computation.7 | async-start | bytes 524288 | tf_op jit(solution)/shard_map/all_to_all | solution.py:25
Sparse Core Ops, SparseCore 0:
  10.1 46.0 all-gather.1
  155.7 39.9 reduce-scatter.1

commit v2 on v1

v2 whole, which is shorter than its diff:
```python
import functools

import jax
import jax.numpy as jnp
from jax import lax
from jax.experimental import pallas as pl
from jax.experimental.pallas import tpu as pltpu
from jax.sharding import Mesh, PartitionSpec as P

K = 8192
ITERS = 3
DP = ("x", "y", "core")
LANES = 128
SUB = 8

epsilon = 1e-05
inverse_temp = 64.0

VMEM = pl.BlockSpec(memory_space=pltpu.VMEM)
SMEM = pl.BlockSpec(memory_space=pltpu.SMEM)
MIB = 1024 * 1024


def call(body, out_shape, ins, scratch=(), grant=8):
    return pl.pallas_call(
        body,
        out_shape=out_shape,
        in_specs=ins,
        out_specs=jax.tree.map(lambda _: VMEM, out_shape),
        scratch_shapes=list(scratch),
        compiler_params=pltpu.CompilerParams(vmem_limit_bytes=grant * MIB),
    )


def split(values):
    high = values.astype(jnp.bfloat16)
    return high, (values - high.astype(jnp.float32)).astype(jnp.bfloat16)


def unit_rows(values):
    return values * lax.rsqrt(jnp.mean(values * values, axis=-1, keepdims=True) + epsilon)


def dot_nt(a, b):
    return lax.dot_general(a, b, (((1,), (1,)), ((), ())), preferred_element_type=jnp.float32)


def lane_sums(block):
    return jnp.sum(block.T, axis=0, keepdims=True)


def scale_kernel(codes_ref, high_ref, low_ref):
    width = codes_ref.shape[1]
    high, low = split(unit_rows(codes_ref[...]) * (inverse_temp / width))
    high_ref[...] = high
    low_ref[...] = low


def chunk_kernel(count, high_ref, low_ref, *refs):
    item_refs, (out_ref, sums_ref, th_ref, tl_ref) = refs[:count], refs[count:]
    rows = item_refs[0].shape[0]
    width = item_refs[0].shape[1]
    highs, lows = [], []
    for j, ref in enumerate(item_refs):
        values = ref[...]
        high, low = split(unit_rows(values))
        highs.append(high)
        lows.append(low)
        turned = values.T.reshape(width // (2 * SUB), 2, SUB, rows)
        for core in range(2):
            half_high, half_low = split(turned[:, core].reshape(width // 2, rows))
            th_ref[core, :, j * rows:(j + 1) * rows] = half_high
            tl_ref[core, :, j * rows:(j + 1) * rows] = half_low
    item_high = jnp.concatenate(highs, axis=0) if count > 1 else highs[0]
    item_low = jnp.concatenate(lows, axis=0) if count > 1 else lows[0]
    codes = high_ref.shape[0]
    step = 256
    for start in range(0, codes, step):
        code_high = high_ref[start:start + step]
        code_low = low_ref[start:start + step]
        logits = dot_nt(code_high, item_high) + (dot_nt(code_high, item_low) + dot_nt(code_low, item_high))
        values = jnp.exp(logits)
        out_ref[start:start + step] = values
        folded = values[:, :rows]
        for j in range(1, count):
            folded = folded + values[:, j * rows:(j + 1) * rows]
        for part in range(step // LANES):
            row = start // LANES + part
            sums_ref[row:row + 1] = lane_sums(folded[part * LANES:(part + 1) * LANES])


def load_blocks(refs):
    return [(ref, j * LANES) for ref in refs for j in range(ref.shape[1] // LANES)]


def row_kernel(order, z_ref, got_ref, *refs):
    blocks, out_ref = load_blocks(refs[:-1]), refs[-1]
    scale = 1.0 / (K * jnp.sum(got_ref[...], axis=0))
    totals = [jnp.zeros((SUB, LANES), jnp.float32) for _ in blocks]
    for b in range(scale.shape[0]):
        column = jnp.broadcast_to(scale[b:b + 1], (LANES, LANES)).T
        for j, (ref, lane) in enumerate(blocks):
            product = ref[b * LANES:(b + 1) * LANES, lane:lane + LANES] * column
            totals[j] = totals[j] + jnp.sum(product.reshape(LANES // SUB, SUB, LANES), axis=0)
    rows = [None] * len(blocks)
    for j, offset in enumerate(order):
        rows[offset] = jnp.sum(totals[j], axis=0, keepdims=True)
    tile = pltpu.roll(jnp.concatenate(rows, axis=0), z_ref[0], 0)
    for peer in range(out_ref.shape[0]):
        out_ref[peer] = tile


def row_scales(order, total_items, z_ref, got_ref):
    scale = 1.0 / (total_items * jnp.sum(got_ref[...], axis=0))
    tile = pltpu.roll(scale, z_ref[1], 0)
    return [tile[offset:offset + 1] for offset in order]


def col_kernel(order, total_items, z_ref, got_ref, *refs):
    blocks, out_ref = load_blocks(refs[:-1]), refs[-1]
    scales = row_scales(order, total_items, z_ref, got_ref)
    for b in range(out_ref.shape[0]):
        folded = jnp.zeros((LANES, LANES), jnp.float32)
        for (ref, lane), scale in zip(blocks, scales):
            folded = folded + ref[b * LANES:(b + 1) * LANES, lane:lane + LANES] * scale
        out_ref[b:b + 1] = lane_sums(folded)


def numer_kernel(order, total_items, count, nx, ny, z_ref, got_ref, *refs):
    blocks = load_blocks(refs[:count])
    high_refs, low_refs = refs[count:2 * count], refs[2 * count:3 * count]
    out_ref, wh_ref, wl_ref, xh_ref, xl_ref = refs[3 * count:]
    scales = row_scales(order, total_items, z_ref, got_ref)
    lane, half = 0, xh_ref.shape[0] // 2
    for high, low in zip(high_refs, low_refs):
        size = high.shape[2]
        for core in range(2):
            xh_ref[core * half:(core + 1) * half, lane:lane + size] = high[core]
            xl_ref[core * half:(core + 1) * half, lane:lane + size] = low[core]
        lane += size
    codes = refs[0].shape[0]
    step = 256
    mass = []
    for start in range(0, codes, step):
        for part in range(step // LANES):
            top = start + part * LANES
            folded = jnp.zeros((LANES, LANES), jnp.float32)
            for j, ((ref, lane), scale) in enumerate(zip(blocks, scales)):
                weights = ref[top:top + LANES, lane:lane + LANES] * scale
                folded = folded + weights
                high, low = split(weights)
                wh_ref[part * LANES:(part + 1) * LANES, j * LANES:(j + 1) * LANES] = high
                wl_ref[part * LANES:(part + 1) * LANES, j * LANES:(j + 1) * LANES] = low
            mass.append(lane_sums(folded))
        weight_high, weight_low = wh_ref[...], wl_ref[...]
        sums = dot_nt(xh_ref[...], weight_high) + (dot_nt(xh_ref[...], weight_low) + dot_nt(xl_ref[...], weight_high))
        for core in range(2):
            slot = jnp.where(z_ref[2] == core, 0, 1)
            for part in range(step // LANES):
                col = start // LANES + part
                for x in range(nx):
                    for y in range(ny):
                        row = core * half + (x * ny + y) * SUB
                        out_ref[slot, x, y * SUB + col] = sums[row:row + SUB, part * LANES:(part + 1) * LANES]
    tile = jnp.concatenate(mass, axis=0)
    for core in range(2):
        for x in range(nx):
            out_ref[core, x, ny * SUB] = tile


def repack_kernel(got_ref, out_ref):
    summed = got_ref[0]
    for x in range(1, got_ref.shape[0]):
        summed = summed + got_ref[x]
    ny, count = out_ref.shape[0], out_ref.shape[1]
    for y in range(ny):
        out_ref[y, :count - 1] = summed[y * (count - 1):(y + 1) * (count - 1)]
        out_ref[y, count - 1] = summed[ny * (count - 1)]


def finish_kernel(got_ref, out_ref):
    summed = jnp.sum(got_ref[...], axis=0)
    count = summed.shape[0] - 1
    for b in range(count):
        out_ref[:, b * LANES:(b + 1) * LANES] = summed[b] / summed[count][b:b + 1]


def body(items, codewords, assign):
    f32 = jnp.float32
    code_count = lax.axis_size("code")
    nx, ny, nc = lax.axis_size("x"), lax.axis_size("y"), lax.axis_size("core")
    local_codes, width = codewords.shape
    own_rows = items.shape[0]
    total_items = own_rows * code_count * nx * ny * nc
    my_code = lax.axis_index("code")
    z_info = jnp.stack([my_code, lax.rem(code_count - my_code, code_count), lax.axis_index("core")]).astype(jnp.int32)

    items, z_info = lax.optimization_barrier((items, z_info))

    half = jax.ShapeDtypeStruct((local_codes, width), jnp.bfloat16)
    code_high, code_low = call(scale_kernel, (half, half), [VMEM])(codewords)

    def chunk(*arrived):
        count = len(arrived)
        lanes = count * own_rows
        turned = jax.ShapeDtypeStruct((2, width // 2, lanes), jnp.bfloat16)
        shapes = (
            jax.ShapeDtypeStruct((local_codes, lanes), f32),
            jax.ShapeDtypeStruct((local_codes // LANES, LANES), f32),
            turned,
            turned,
        )
        return call(functools.partial(chunk_kernel, count), shapes, [VMEM] * (2 + count))(code_high, code_low, *arrived)

    index_rows = assign - my_code * local_codes
    inside = (index_rows >= 0) & (index_rows < local_codes)
    picked = jnp.take(codewords, jnp.clip(index_rows, 0, local_codes - 1), axis=0)
    named = jnp.where(inside[:, None], picked, jnp.float32(0.0))

    up = [(i, (i + 1) % code_count) for i in range(code_count)]
    down = [(i, (i - 1) % code_count) for i in range(code_count)]
    chunks, order = [chunk(items)], [0]
    right = left = items
    for step in range(1, code_count // 2 + 1):
        right = lax.ppermute(right, "code", up)
        if step < code_count // 2:
            if step == 2:
                named, left = lax.optimization_barrier((named, left))
            left, chunks[step - 1] = lax.optimization_barrier((left, chunks[step - 1]))
            left = lax.ppermute(left, "code", down)
            chunks.append(chunk(right, left))
            order += [code_count - step, step]
        else:
            chunks.append(chunk(right))
            order += [code_count - step]
    blocks = [c[0] for c in chunks]
    count = len(blocks)
    col_tile = sum(c[1] for c in chunks)

    def over_items(tile):
        chip = tile + lax.ppermute(tile, "core", [(0, 1), (1, 0)])
        return lax.all_to_all(jnp.broadcast_to(chip[None], (nx * ny,) + chip.shape), ("x", "y"), 0, 0)

    row_shape = jax.ShapeDtypeStruct((code_count, SUB, LANES), f32)
    col_shape = jax.ShapeDtypeStruct((local_codes // LANES, LANES), f32)
    operands = [SMEM, VMEM] + [VMEM] * count
    for turn in range(ITERS):
        got = over_items(col_tile)
        rows = call(functools.partial(row_kernel, order), row_shape, operands)(z_info, got, *blocks)
        if turn == 0:
            named, rows = lax.optimization_barrier((named, rows))
            looked = lax.psum_scatter(named, "code", scatter_dimension=0, tiled=True)
        got = lax.all_to_all(rows, "code", 0, 0)
        if turn < ITERS - 1:
            col_tile = call(functools.partial(col_kernel, order, total_items), col_shape, operands)(z_info, got, *blocks)

    tiles = jax.ShapeDtypeStruct((nc, nx, ny * SUB + 1, SUB, LANES), f32)
    numer = call(
        functools.partial(numer_kernel, order, total_items, count, nx, ny),
        tiles,
        operands + [VMEM] * (2 * count),
        [pltpu.VMEM((256, own_rows * code_count), jnp.bfloat16)] * 2
        + [pltpu.VMEM((width, own_rows * code_count), jnp.bfloat16)] * 2,
        grant=16,
    )(z_info, got, *blocks, *[c[2] for c in chunks], *[c[3] for c in chunks])
    partner = lax.ppermute(numer[1], "core", [(0, 1), (1, 0)])
    partner, residual = lax.optimization_barrier((partner, items - looked))
    chip = numer[0] + partner
    got = lax.all_to_all(chip, "x", 0, 0)
    packed = call(repack_kernel, jax.ShapeDtypeStruct((ny, SUB + 1, SUB, LANES), f32), [VMEM])(got)
    got = lax.all_to_all(packed, "y", 0, 0)
    turned = call(finish_kernel, jax.ShapeDtypeStruct((width // (nx * ny * nc), local_codes), f32), [VMEM])(got)
    new_codewords = turned.T

    return (new_codewords, residual)


def solution(mesh):
    cores = 2
    ny = 8
    dp, code = mesh.devices.shape
    fine = Mesh(
        mesh.devices.reshape(dp // (ny * cores), ny, cores, code),
        ("x", "y", "core", "code"),
    )
    in_specs = (P(DP + ("code",), None), P("code", None), P(DP))
    out_specs = (P("code", DP), P(DP + ("code",), None))
    return jax.shard_map(body, mesh=fine, in_specs=in_specs, out_specs=out_specs, check_vma=False)
```

time: 256 us -> 227 us (0.89)
  waiting for transfers between devices: 112 us -> 9.25 us
  blocking collectives: 36.8 us -> 103 us
  other arithmetic: 29.7 us -> 6.45 us
  Pallas kernels: 0 us -> 20 us
  matrix products: 11.6 us -> 0 us
  local copies, waits for them, and re-layouts: 10.5 us -> 21.4 us
  starting transfers between devices: 39.9 us -> 50.3 us
    all_to_all x2 -> x8, blocking collectives: 36.8 us -> 103 us  [the longest x3 43.4 us: over_items(): lax.all_to_all(jnp.broadcast_to(chip[None], (nx * ny,) + chip.shape), ('x...]
    all_to_all x7 -> x0, waiting for transfers between devices: 62.9 us -> none  [the longest x5 42.1 us: exchange_sum(): return jnp.sum(lax.all_to_all(copies, axes, 0, 0), axis=0)]
    ppermute x1 -> x11, starting transfers between devices: 3.8 us -> 50.3 us  [the longest x3 18.4 us: body(): left = lax.ppermute(left, 'code', down)]
    all_gather x1 -> x0, waiting for transfers between devices: 46.3 us -> none  [body(): gathered = lax.all_gather(items, 'code', axis=0, tiled=True)]
    all_to_all x7 -> x0, starting transfers between devices: 36 us -> none  [the longest x5 28.3 us: exchange_sum(): return jnp.sum(lax.all_to_all(copies, axes, 0, 0), axis=0)]
    reduce_sum x17 -> x0, other arithmetic: 22.8 us -> none  [the longest x3 8.8 us: body(): row_part = jnp.sum(kernel_vals * col_scale[None, :], axis=1)]
    pallas_call x0 -> x14, Pallas kernels: none -> 20 us  [the longest x5 9.46 us: chunk(): call(functools.partial(chunk_kernel, count), shapes, [VMEM] * (2 + count))]
    unnamed x14 -> x72, local copies, waits for them, and re-layouts: 1.6 us -> 16.4 us
  transfers between devices with their start and end apart: 10 -> 12, of which waited for: 9 -> 7; matrix products, arithmetic and copies ran while one was open for 11% -> 4% of each run, Pallas kernels for 0% -> 8%
where the time goes in v2:
time: 227 us; the launch traced here: 225 us
  blocking collectives  103 us (45%)
  starting transfers between devices  50.3 us (22%)
  local copies, waits for them, and re-layouts  21.4 us (9%)
  Pallas kernels  20 us (9%)
  between operations  14.4 us (6%)
  waiting for transfers between devices  9.25 us (4%)
  other arithmetic  6.45 us (3%)
    all_to_all x3, blocking collectives, over_items(): lax.all_to_all(jnp.broadcast_to(chip[None], (nx * ny,) + chip.shape), ('x...  43.4 us
    all_to_all x3, blocking collectives, body(): got = lax.all_to_all(rows, 'code', 0, 0)  29.3 us
    ppermute x3, starting transfers between devices, body(): left = lax.ppermute(left, 'code', down)  18.4 us
    all_to_all x1, blocking collectives, body(): got = lax.all_to_all(chip, 'x', 0, 0)  17.3 us
    unnamed x72, local copies, waits for them, and re-layouts  16.4 us
    ppermute x3, starting transfers between devices, over_items(): chip = tile + lax.ppermute(tile, 'core', [(0, 1), (1, 0)])  16.1 us
    all_to_all x1, blocking collectives, body(): got = lax.all_to_all(packed, 'y', 0, 0)  12.9 us
    ppermute x4, starting transfers between devices, body(): right = lax.ppermute(right, 'code', up)  10.6 us
  transfers between devices with their start and end apart: 12, of which 7 were waited for; matrix products, arithmetic and copies ran while one was open for 4% of the time, Pallas kernels for 8%

profile of v2, /device:TPU:1, one launch (start us, length us, event | category | flops | bytes accessed | tf_op | source)
XLA Modules:
  0.0 224.8 jit_solution(3520956312502693790)
XLA Ops:
  7.3 4.8 %collective-permute-start.1 = (f32[128,512]{1,0:T(8,128)}, f32[128,512]{1,0:T(8,128)}, u32[]{:S(2)}, u32[]{:S(2)}) collective-permute-start(f32[128,512]{1,0:T(8,128)} %refs_0_), channel_id=1, source_target_pairs={{0,1},{1,2},{2,3},{3,4},{4,5},{5,6},{6,7},{7,0},{8,9},{9,10},{10,1... | collective-permute-start | bytes 786440 | tf_op jit(solution)/shard_map/ppermute | solution.py:225
  12.1 1.6 copy-done
  14.3 2.6 %shard_map.51 = (f32[1024,128]{1,0:T(8,128)S(1)}, f32[8,128]{1,0:T(8,128)S(1)}, bf16[2,256,128]{2,1,0:T(8,128)(2,1)S(1)}, bf16[2,256,128]{2,1,0:T(8,128)(2,1)S(1)}) custom-call(bf16[1024,512]{1,0:T(8,128)(2,1)S(1)} %get-tuple-element.49.high_ref, bf16[1024,512]{1,0:T(8,128)(2,1)S(1)} %get-tuple-element.50.low_ref, f32[128,512]{1,0:T(8,128)} %refs_0_), custom_call_target="tpu_custom_call" | custom-call | tf_op jit(solution)/shard_map/pallas_call | solution.py:213
  19.3 8.6 %collective-permute-start = (f32[128,512]{1,0:T(8,128)}, f32[128,512]{1,0:T(8,128)S(1)}, u32[]{:S(2)}, u32[]{:S(2)}) collective-permute-start(f32[128,512]{1,0:T(8,128)} %refs_0_), channel_id=1, source_target_pairs={{0,7},{1,0},{2,1},{3,2},{4,3},{5,4},{6,5},{7,6},{8,15},{9,8},{10,9... | collective-permute-start | bytes 786440 | tf_op jit(solution)/shard_map/ppermute | solution.py:230
  27.9 4.9 %gather_fusion = f32[1024,512]{1,0:T(8,128)} fusion(f32[1024,512]{1,0:T(8,128)S(1)} %copy-done.1, s32[1024]{0:T(1024)S(1)} %fusion.1), kind=kCustom, calls=%fused_computation | custom fusion | bytes 4198400 | tf_op jit(solution)/shard_map/jit(_take)/gather | solution.py:217
  32.8 1.9 collective-permute-start.3
  34.7 3.2 %select_select_fusion = f32[1024,512]{1,0:T(8,128)} fusion(f32[1024,512]{1,0:T(8,128)} %gather_fusion, pred[1024]{0:T(1024)(128)(4,1)S(1)} %get-tuple-element.93, pred[1024]{0:T(1024)(128)(4,1)S(1)} %get-tuple-element.92), kind=kLoop, calls=%fused_computation.1 | loop fusion | flops 1048576 | bytes 4196352 | tf_op jit(solution)/shard_map/jit(_where)/select_n | solution.py:218
  39.6 2.2 shard_map.52
  42.5 4.6 %collective-permute-start.2 = (f32[128,512]{1,0:T(8,128)S(1)}, f32[128,512]{1,0:T(8,128)S(1)}, u32[]{:S(2)}, u32[]{:S(2)}) collective-permute-start(f32[128,512]{1,0:T(8,128)S(1)} %copy-done.27), channel_id=1, source_target_pairs={{0,7},{1,0},{2,1},{3,2},{4,3},{5,4},{6,5},{7,6},{8,15},{9,8},{10,9... | collective-permute-start | bytes 786440 | tf_op jit(solution)/shard_map/ppermute | solution.py:230
  47.1 1.9 collective-permute-start.4
  49.0 2.4 %collective-permute-done.2.refs_1_ = f32[128,512]{1,0:T(8,128)S(1)} collective-permute-done((f32[128,512]{1,0:T(8,128)S(1)}, f32[128,512]{1,0:T(8,128)S(1)}, u32[]{:S(2)}, u32[]{:S(2)}) %collective-permute-start.2) | collective-permute-done | bytes 262176 | tf_op jit(solution)/shard_map/ppermute | solution.py:230
  52.7 2.3 %shard_map.53 = (f32[1024,256]{1,0:T(8,128)S(1)}, f32[8,128]{1,0:T(8,128)S(1)}, bf16[2,256,256]{2,1,0:T(8,128)(2,1)S(1)}, bf16[2,256,256]{2,1,0:T(8,128)(2,1)S(1)}) custom-call(bf16[1024,512]{1,0:T(8,128)(2,1)S(1)} %get-tuple-element.49.high_ref, bf16[1024,512]{1,0:T(8,128)(2,1)S(1)} %copy-done.6, f32[128,512]{1,0:T(8,128)} %collective-permute-done.3.refs_0_, ...), custom_call_target="tpu_custom_call" | custom-call | tf_op jit(solution)/shard_map/pallas_call | solution.py:213
  56.4 5.3 %collective-permute-start.5 = (f32[128,512]{1,0:T(8,128)S(1)}, f32[128,512]{1,0:T(8,128)S(1)}, u32[]{:S(2)}, u32[]{:S(2)}) collective-permute-start(f32[128,512]{1,0:T(8,128)S(1)} %collective-permute-done.2.refs_1_), channel_id=1, source_target_pairs={{0,7},{1,0},{2,1},{3,2},{4,3},{5,4},{6,5},{7,6},{8,15},{9,8},{10,9... | collective-permute-start | bytes 786440 | tf_op jit(solution)/shard_map/ppermute | solution.py:230
  61.7 1.9 collective-permute-start.6
  63.6 1.4 collective-permute-done.5.refs_1_
  67.5 2.5 %collective-permute-done.6.refs_0_ = f32[128,512]{1,0:T(8,128)S(1)} collective-permute-done((f32[128,512]{1,0:T(8,128)S(1)}, f32[128,512]{1,0:T(8,128)S(1)}, u32[]{:S(2)}, u32[]{:S(2)}) %collective-permute-start.6) | collective-permute-done | bytes 262176 | tf_op jit(solution)/shard_map/ppermute | solution.py:225
  72.5 5.5 %collective-permute-start.7 = (f32[8,128]{1,0:T(8,128)S(1)}, f32[8,128]{1,0:T(8,128)S(1)}, u32[]{:S(2)}, u32[]{:S(2)}) collective-permute-start(f32[8,128]{1,0:T(8,128)S(1)} %add_add_fusion), channel_id=1, source_target_pairs={{0,8},{8,0},{1,9},{9,1},{2,10},{10,2},{3,11},{11,3},{4,12},{12,4},... | collective-permute-start | bytes 12296 | tf_op jit(solution)/shard_map/ppermute | solution.py:241
  78.8 18.6 %all_to_all.40.got_ref = f32[32,8,128]{2,1,0:T(8,128)S(1)} all-to-all(f32[32,8,128]{2,1,0:T(8,128)S(1)} %broadcast_in_dim.48), channel_id=1, replica_groups=mesh['x'=4,'y'=8,'core'=2,'code'=8] {'x','y'}, dimensions={0} | all-to-all | bytes 262144 | tf_op jit(solution)/shard_map/all_to_all | solution.py:242
  99.9 10.8 %all_to_all.41.got_ref = f32[8,8,128]{2,1,0:T(8,128)S(1)} all-to-all(f32[8,8,128]{2,1,0:T(8,128)} %copy-done.34), channel_id=1, replica_groups=mesh['x'=4,'y'=8,'core'=2,'code'=8] {'code'}, dimensions={0} | all-to-all | bytes 65536 | tf_op jit(solution)/shard_map/all_to_all | solution.py:253
  113.7 5.5 %collective-permute-start.8 = (f32[8,128]{1,0:T(8,128)S(1)}, f32[8,128]{1,0:T(8,128)S(1)}, u32[]{:S(2)}, u32[]{:S(2)}) collective-permute-start(f32[8,128]{1,0:T(8,128)S(1)} %shard_map.57), channel_id=1, source_target_pairs={{0,8},{8,0},{1,9},{9,1},{2,10},{10,2},{3,11},{11,3},{4,12},{12,4},... | collective-permute-start | bytes 12296 | tf_op jit(solution)/shard_map/ppermute | solution.py:241
  120.0 12.4 %all_to_all.42.got_ref = f32[32,8,128]{2,1,0:T(8,128)S(1)} all-to-all(f32[32,8,128]{2,1,0:T(8,128)S(1)} %broadcast_in_dim.49), channel_id=1, replica_groups=mesh['x'=4,'y'=8,'core'=2,'code'=8] {'x','y'}, dimensions={0} | all-to-all | bytes 262144 | tf_op jit(solution)/shard_map/all_to_all | solution.py:242
  133.3 9.2 %all_to_all.43.got_ref = f32[8,8,128]{2,1,0:T(8,128)S(1)} all-to-all(f32[8,8,128]{2,1,0:T(8,128)S(1)} %shard_map.58), channel_id=1, replica_groups=mesh['x'=4,'y'=8,'core'=2,'code'=8] {'code'}, dimensions={0} | all-to-all | bytes 65536 | tf_op jit(solution)/shard_map/all_to_all | solution.py:253
  143.4 5.2 %collective-permute-start.9 = (f32[8,128]{1,0:T(8,128)S(1)}, f32[8,128]{1,0:T(8,128)S(1)}, u32[]{:S(2)}, u32[]{:S(2)}) collective-permute-start(f32[8,128]{1,0:T(8,128)S(1)} %shard_map.59), channel_id=1, source_target_pairs={{0,8},{8,0},{1,9},{9,1},{2,10},{10,2},{3,11},{11,3},{4,12},{12,4},... | collective-permute-start | bytes 12296 | tf_op jit(solution)/shard_map/ppermute | solution.py:241
  149.4 12.4 %all_to_all.44.got_ref = f32[32,8,128]{2,1,0:T(8,128)S(1)} all-to-all(f32[32,8,128]{2,1,0:T(8,128)S(1)} %broadcast_in_dim.50), channel_id=1, replica_groups=mesh['x'=4,'y'=8,'core'=2,'code'=8] {'x','y'}, dimensions={0} | all-to-all | bytes 262144 | tf_op jit(solution)/shard_map/all_to_all | solution.py:242
  162.8 9.2 %all_to_all.45.got_ref = f32[8,8,128]{2,1,0:T(8,128)S(1)} all-to-all(f32[8,8,128]{2,1,0:T(8,128)S(1)} %shard_map.60), channel_id=1, replica_groups=mesh['x'=4,'y'=8,'core'=2,'code'=8] {'code'}, dimensions={0} | all-to-all | bytes 65536 | tf_op jit(solution)/shard_map/all_to_all | solution.py:253
  172.1 4.7 %shard_map.61 = f32[2,4,65,8,128]{4,3,2,1,0:T(8,128)S(1)} custom-call(s32[3]{0:T(128)S(1)} %pad_add_fusion.z_ref, f32[8,8,128]{2,1,0:T(8,128)S(1)} %all_to_all.45.got_ref, f32[1024,128]{1,0:T(8,128)S(1)} %copy-done.11, f32[1024,256]{1,0:T(8,128)S(1)} %get-tuple-element.74.refs_1_, f32[1024,256]{1,0:T(8,128)S(1)} %get-tuple-element.75.refs_2_, ...), custom_call_target="tpu_custom_call" | custom-call | tf_op jit(solution)/shard_map/pallas_call | solution.py:258
  176.8 1.3 copy-done.15
  178.3 5.2 %collective-permute-start.10 = (f32[4,65,8,128]{3,2,1,0:T(8,128)S(1)}, f32[4,65,8,128]{3,2,1,0:T(8,128)S(1)}, u32[]{:S(2)}, u32[]{:S(2)}) collective-permute-start(f32[4,65,8,128]{3,2,1,0:T(8,128)S(1)} %slice_bitcast_fusion), channel_id=1, source_target_pairs={{0,8},{8,0},{1,9},{9,1},{2,10},{10,2},{3,11},{11,3},{4,12},{12,4},... | collective-permute-start | bytes 3194888 | tf_op jit(solution)/shard_map/ppermute | solution.py:266
  183.5 1.8 sub.15
  185.7 1.3 fusion
  187.1 17.3 %all_to_all.46.got_ref = f32[4,65,8,128]{3,2,1,0:T(8,128)S(1)} all-to-all(f32[4,65,8,128]{3,2,1,0:T(8,128)S(1)} %fusion), channel_id=1, replica_groups=mesh['x'=4,'y'=8,'core'=2,'code'=8] {'x'}, dimensions={0} | all-to-all | bytes 2129920 | tf_op jit(solution)/shard_map/all_to_all | solution.py:269
  204.5 12.9 %all_to_all.47.got_ref = f32[8,9,8,128]{3,2,1,0:T(8,128)S(1)} all-to-all(f32[8,9,8,128]{3,2,1,0:T(8,128)S(1)} %shard_map.62), channel_id=1, replica_groups=mesh['x'=4,'y'=8,'core'=2,'code'=8] {'y'}, dimensions={0} | all-to-all | bytes 589824 | tf_op jit(solution)/shard_map/all_to_all | solution.py:271
  (102 shorter events, 25.0 us)
Async XLA Ops:
  7.2 176.3 %reduce-scatter.2.cloned.1.call-start = ((), (), s32[]{:S(2)}) async-start(), calls=%async_computation.9 | async-start | bytes 2359296 | tf_op jit(solution)/shard_map/reduce_scatter | solution.py:252
  7.3 25.5 %collective-permute-start.1 = (f32[128,512]{1,0:T(8,128)}, f32[128,512]{1,0:T(8,128)}, u32[]{:S(2)}, u32[]{:S(2)}) collective-permute-start(f32[128,512]{1,0:T(8,128)} %refs_0_), channel_id=1, source_target_pairs={{0,1},{1,2},{2,3},{3,4},{4,5},{5,6},{6,7},{7,0},{8,9},{9,10},{10,1... | collective-permute-start | bytes 786440 | tf_op jit(solution)/shard_map/ppermute | solution.py:225
  12.1 1.6 copy-start
  13.7 14.2 %copy-start.35 = (s32[1024]{0:T(1024)S(1)}, s32[1024]{0:T(1024)}, u32[]{:S(2)}) copy-start(s32[1024]{0:T(1024)} %param.5) | copy-start | bytes 12292
  13.7 14.2 %copy-start.1 = (f32[1024,512]{1,0:T(8,128)S(1)}, f32[1024,512]{1,0:T(8,128)}, u32[]{:S(2)}) copy-start(f32[1024,512]{1,0:T(8,128)} %codes_ref.1) | copy-start | bytes 6291460
  14.3 37.2 %copy-start.2 = (bf16[1024,512]{1,0:T(8,128)(2,1)}, bf16[1024,512]{1,0:T(8,128)(2,1)S(1)}, u32[]{:S(2)}) copy-start(bf16[1024,512]{1,0:T(8,128)(2,1)S(1)} %get-tuple-element.49.high_ref) | copy-start | bytes 3145732
  19.3 18.7 %collective-permute-start = (f32[128,512]{1,0:T(8,128)}, f32[128,512]{1,0:T(8,128)S(1)}, u32[]{:S(2)}, u32[]{:S(2)}) collective-permute-start(f32[128,512]{1,0:T(8,128)} %refs_0_), channel_id=1, source_target_pairs={{0,7},{1,0},{2,1},{3,2},{4,3},{5,4},{6,5},{7,6},{8,15},{9,8},{10,9... | collective-permute-start | bytes 786440 | tf_op jit(solution)/shard_map/ppermute | solution.py:230
  32.8 14.3 %collective-permute-start.3 = (f32[128,512]{1,0:T(8,128)}, f32[128,512]{1,0:T(8,128)}, u32[]{:S(2)}, u32[]{:S(2)}) collective-permute-start(f32[128,512]{1,0:T(8,128)} %collective-permute-done.1.refs_0_), channel_id=1, source_target_pairs={{0,1},{1,2},{2,3},{3,4},{4,5},{5,6},{6,7},{7,0},{8,9},{9,10},{10,1... | collective-permute-start | bytes 786440 | tf_op jit(solution)/shard_map/ppermute | solution.py:225
  34.7 4.0 %copy-start.5 = (bf16[1024,512]{1,0:T(8,128)(2,1)S(1)}, bf16[1024,512]{1,0:T(8,128)(2,1)}, u32[]{:S(2)}) copy-start(bf16[1024,512]{1,0:T(8,128)(2,1)} %copy-done.4) | copy-start | bytes 3145732
  42.5 8.9 %collective-permute-start.2 = (f32[128,512]{1,0:T(8,128)S(1)}, f32[128,512]{1,0:T(8,128)S(1)}, u32[]{:S(2)}, u32[]{:S(2)}) collective-permute-start(f32[128,512]{1,0:T(8,128)S(1)} %copy-done.27), channel_id=1, source_target_pairs={{0,7},{1,0},{2,1},{3,2},{4,3},{5,4},{6,5},{7,6},{8,15},{9,8},{10,9... | collective-permute-start | bytes 786440 | tf_op jit(solution)/shard_map/ppermute | solution.py:230
  47.1 14.6 %collective-permute-start.4 = (f32[128,512]{1,0:T(8,128)}, f32[128,512]{1,0:T(8,128)S(1)}, u32[]{:S(2)}, u32[]{:S(2)}) collective-permute-start(f32[128,512]{1,0:T(8,128)} %collective-permute-done.3.refs_0_), channel_id=1, source_target_pairs={{0,1},{1,2},{2,3},{3,4},{4,5},{5,6},{6,7},{7,0},{8,9},{9,10},{10,1... | collective-permute-start | bytes 786440 | tf_op jit(solution)/shard_map/ppermute | solution.py:225
  52.7 17.4 %copy-start.7 = (bf16[1024,512]{1,0:T(8,128)(2,1)S(1)}, bf16[1024,512]{1,0:T(8,128)(2,1)}, u32[]{:S(2)}) copy-start(bf16[1024,512]{1,0:T(8,128)(2,1)} %copy-done.4) | copy-start | bytes 3145732
  56.4 8.6 %collective-permute-start.5 = (f32[128,512]{1,0:T(8,128)S(1)}, f32[128,512]{1,0:T(8,128)S(1)}, u32[]{:S(2)}, u32[]{:S(2)}) collective-permute-start(f32[128,512]{1,0:T(8,128)S(1)} %collective-permute-done.2.refs_1_), channel_id=1, source_target_pairs={{0,7},{1,0},{2,1},{3,2},{4,3},{5,4},{6,5},{7,6},{8,15},{9,8},{10,9... | collective-permute-start | bytes 786440 | tf_op jit(solution)/shard_map/ppermute | solution.py:230
  61.7 8.3 %collective-permute-start.6 = (f32[128,512]{1,0:T(8,128)S(1)}, f32[128,512]{1,0:T(8,128)S(1)}, u32[]{:S(2)}, u32[]{:S(2)}) collective-permute-start(f32[128,512]{1,0:T(8,128)S(1)} %collective-permute-done.4.refs_0_), channel_id=1, source_target_pairs={{0,1},{1,2},{2,3},{3,4},{4,5},{5,6},{6,7},{7,0},{8,9},{9,10},{10,1... | collective-permute-start | bytes 786440 | tf_op jit(solution)/shard_map/ppermute | solution.py:225
  66.2 31.3 %copy-start.9 = (f32[1024,128]{1,0:T(8,128)S(1)}, f32[1024,128]{1,0:T(8,128)}, u32[]{:S(2)}) copy-start(f32[1024,128]{1,0:T(8,128)} %copy-done.8) | copy-start | bytes 1572868
  67.4 3.8 %copy-start.22 = (bf16[2,256,256]{2,1,0:T(8,128)(2,1)}, bf16[2,256,256]{2,1,0:T(8,128)(2,1)S(1)}, u32[]{:S(2)}) copy-start(bf16[2,256,256]{2,1,0:T(8,128)(2,1)S(1)} %get-tuple-element.82.refs_8_) | copy-start | bytes 786436
  67.5 5.1 %copy-start.24 = (bf16[2,256,256]{2,1,0:T(8,128)(2,1)}, bf16[2,256,256]{2,1,0:T(8,128)(2,1)S(1)}, u32[]{:S(2)}) copy-start(bf16[2,256,256]{2,1,0:T(8,128)(2,1)S(1)} %get-tuple-element.87.refs_13_) | copy-start | bytes 786436
  72.5 6.3 %collective-permute-start.7 = (f32[8,128]{1,0:T(8,128)S(1)}, f32[8,128]{1,0:T(8,128)S(1)}, u32[]{:S(2)}, u32[]{:S(2)}) collective-permute-start(f32[8,128]{1,0:T(8,128)S(1)} %add_add_fusion), channel_id=1, source_target_pairs={{0,8},{8,0},{1,9},{9,1},{2,10},{10,2},{3,11},{11,3},{4,12},{12,4},... | collective-permute-start | bytes 12296 | tf_op jit(solution)/shard_map/ppermute | solution.py:241
  112.8 19.6 %copy-start.11 = (f32[1024,128]{1,0:T(8,128)S(1)}, f32[1024,128]{1,0:T(8,128)}, u32[]{:S(2)}) copy-start(f32[1024,128]{1,0:T(8,128)} %copy-done.8) | copy-start | bytes 1572868
  112.8 19.6 %copy-start.14 = (f32[1024,128]{1,0:T(8,128)S(1)}, f32[1024,128]{1,0:T(8,128)}, u32[]{:S(2)}) copy-start(f32[1024,128]{1,0:T(8,128)} %copy-done.12) | copy-start | bytes 1572868
  113.7 6.3 %collective-permute-start.8 = (f32[8,128]{1,0:T(8,128)S(1)}, f32[8,128]{1,0:T(8,128)S(1)}, u32[]{:S(2)}, u32[]{:S(2)}) collective-permute-start(f32[8,128]{1,0:T(8,128)S(1)} %shard_map.57), channel_id=1, source_target_pairs={{0,8},{8,0},{1,9},{9,1},{2,10},{10,2},{3,11},{11,3},{4,12},{12,4},... | collective-permute-start | bytes 12296 | tf_op jit(solution)/shard_map/ppermute | solution.py:241
  143.4 6.0 %collective-permute-start.9 = (f32[8,128]{1,0:T(8,128)S(1)}, f32[8,128]{1,0:T(8,128)S(1)}, u32[]{:S(2)}, u32[]{:S(2)}) collective-permute-start(f32[8,128]{1,0:T(8,128)S(1)} %shard_map.59), channel_id=1, source_target_pairs={{0,8},{8,0},{1,9},{9,1},{2,10},{10,2},{3,11},{11,3},{4,12},{12,4},... | collective-permute-start | bytes 12296 | tf_op jit(solution)/shard_map/ppermute | solution.py:241
  161.8 10.2 %copy-start.17 = (bf16[2,256,256]{2,1,0:T(8,128)(2,1)S(1)}, bf16[2,256,256]{2,1,0:T(8,128)(2,1)}, u32[]{:S(2)}) copy-start(bf16[2,256,256]{2,1,0:T(8,128)(2,1)} %copy-done.16) | copy-start | bytes 786436
  161.9 10.2 %copy-start.19 = (bf16[2,256,256]{2,1,0:T(8,128)(2,1)S(1)}, bf16[2,256,256]{2,1,0:T(8,128)(2,1)}, u32[]{:S(2)}) copy-start(bf16[2,256,256]{2,1,0:T(8,128)(2,1)} %copy-done.18) | copy-start | bytes 786436
  161.9 10.2 %copy-start.21 = (bf16[2,256,256]{2,1,0:T(8,128)(2,1)S(1)}, bf16[2,256,256]{2,1,0:T(8,128)(2,1)}, u32[]{:S(2)}) copy-start(bf16[2,256,256]{2,1,0:T(8,128)(2,1)} %copy-done.20) | copy-start | bytes 786436
  161.9 10.2 %copy-start.23 = (bf16[2,256,256]{2,1,0:T(8,128)(2,1)S(1)}, bf16[2,256,256]{2,1,0:T(8,128)(2,1)}, u32[]{:S(2)}) copy-start(bf16[2,256,256]{2,1,0:T(8,128)(2,1)} %copy-done.22) | copy-start | bytes 786436
  161.9 10.2 %copy-start.25 = (bf16[2,256,256]{2,1,0:T(8,128)(2,1)S(1)}, bf16[2,256,256]{2,1,0:T(8,128)(2,1)}, u32[]{:S(2)}) copy-start(bf16[2,256,256]{2,1,0:T(8,128)(2,1)} %copy-done.24) | copy-start | bytes 786436
  161.9 10.2 %copy-start.29 = (bf16[2,256,128]{2,1,0:T(8,128)(2,1)S(1)}, bf16[2,256,128]{2,1,0:T(8,128)(2,1)}, u32[]{:S(2)}) copy-start(bf16[2,256,128]{2,1,0:T(8,128)(2,1)} %copy-done.28) | copy-start | bytes 393220
  161.9 10.2 %copy-start.31 = (bf16[2,256,128]{2,1,0:T(8,128)(2,1)S(1)}, bf16[2,256,128]{2,1,0:T(8,128)(2,1)}, u32[]{:S(2)}) copy-start(bf16[2,256,128]{2,1,0:T(8,128)(2,1)} %copy-done.30) | copy-start | bytes 393220
  161.9 10.2 %copy-start.33 = (bf16[2,256,128]{2,1,0:T(8,128)(2,1)S(1)}, bf16[2,256,128]{2,1,0:T(8,128)(2,1)}, u32[]{:S(2)}) copy-start(bf16[2,256,128]{2,1,0:T(8,128)(2,1)} %copy-done.32) | copy-start | bytes 393220
  176.8 1.3 copy-start.15
  178.3 7.5 %collective-permute-start.10 = (f32[4,65,8,128]{3,2,1,0:T(8,128)S(1)}, f32[4,65,8,128]{3,2,1,0:T(8,128)S(1)}, u32[]{:S(2)}, u32[]{:S(2)}) collective-permute-start(f32[4,65,8,128]{3,2,1,0:T(8,128)S(1)} %slice_bitcast_fusion), channel_id=1, source_target_pairs={{0,8},{8,0},{1,9},{9,1},{2,10},{10,2},{3,11},{11,3},{4,12},{12,4},... | collective-permute-start | bytes 3194888 | tf_op jit(solution)/shard_map/ppermute | solution.py:266
  (16 other events, 13.5 us)
Sparse Core Ops, SparseCore 0:
  100.0 35.4 reduce-scatter.1

commit v3 on v2

v3 whole, which is shorter than its diff:
```python
import functools

import jax
import jax.numpy as jnp
from jax import lax
from jax.experimental import pallas as pl
from jax.experimental.pallas import tpu as pltpu
from jax.sharding import Mesh, PartitionSpec as P

K = 8192
ITERS = 3
DP = ("x", "y", "core")
LANES = 128
SUB = 8

epsilon = 1e-05
inverse_temp = 64.0

VMEM = pl.BlockSpec(memory_space=pltpu.VMEM)
SMEM = pl.BlockSpec(memory_space=pltpu.SMEM)
MIB = 1024 * 1024


def call(body, out_shape, ins, scratch=(), grant=8):
    return pl.pallas_call(
        body,
        out_shape=out_shape,
        in_specs=ins,
        out_specs=jax.tree.map(lambda _: VMEM, out_shape),
        scratch_shapes=list(scratch),
        compiler_params=pltpu.CompilerParams(vmem_limit_bytes=grant * MIB),
    )


def split(values):
    high = values.astype(jnp.bfloat16)
    return high, (values - high.astype(jnp.float32)).astype(jnp.bfloat16)


def unit_rows(values):
    return values * lax.rsqrt(jnp.mean(values * values, axis=-1, keepdims=True) + epsilon)


def dot_nt(a, b):
    return lax.dot_general(a, b, (((1,), (1,)), ((), ())), preferred_element_type=jnp.float32)


def lane_sums(block):
    return jnp.sum(block.T, axis=0, keepdims=True)


def scale_kernel(z_ref, codes_ref, high_ref, low_ref):
    half, width = high_ref.shape
    codes = codes_ref[pl.ds(pl.multiple_of(z_ref[2] * half, half), half)]
    high, low = split(unit_rows(codes) * (inverse_temp / width))
    high_ref[...] = high
    low_ref[...] = low


def pair_kernel(z_ref, own_ref, other_ref, out_ref):
    out_ref[z_ref[2]] = own_ref[...]
    out_ref[1 - z_ref[2]] = other_ref[...]


def chunk_kernel(count, high_ref, low_ref, *refs):
    item_refs, (out_ref, sums_ref, xh_ref, xl_ref) = refs[:count], refs[count:]
    rows = item_refs[0].shape[0] * item_refs[0].shape[1]
    width = item_refs[0].shape[2]
    highs, lows = [], []
    for j, ref in enumerate(item_refs):
        values = ref[...].reshape(rows, width)
        high, low = split(unit_rows(values))
        highs.append(high)
        lows.append(low)
        xh_ref[j * rows:(j + 1) * rows], xl_ref[j * rows:(j + 1) * rows] = split(values)
    codes = high_ref.shape[0]
    step = 256
    for start in range(0, codes, step):
        code_high = high_ref[start:start + step]
        code_low = low_ref[start:start + step]
        folded = jnp.zeros((step, LANES), jnp.float32)
        for j, (item_high, item_low) in enumerate(zip(highs, lows)):
            logits = dot_nt(code_high, item_high) + (dot_nt(code_high, item_low) + dot_nt(code_low, item_high))
            values = jnp.exp(logits)
            out_ref[start:start + step, j * rows:(j + 1) * rows] = values
            for lane in range(0, rows, LANES):
                folded = folded + values[:, lane:lane + LANES]
        for part in range(step // LANES):
            row = start // LANES + part
            sums_ref[row:row + 1] = lane_sums(folded[part * LANES:(part + 1) * LANES])


def load_blocks(refs):
    return [(ref, j * LANES) for ref in refs for j in range(ref.shape[1] // LANES)]


def row_kernel(orders, z_ref, got_ref, *refs):
    blocks, out_ref = load_blocks(refs[:-1]), refs[-1]
    scale = 1.0 / (K * jnp.sum(got_ref[...], axis=0))
    totals = [jnp.zeros((SUB, LANES), jnp.float32) for _ in blocks]
    for b in range(scale.shape[0]):
        column = jnp.broadcast_to(scale[b:b + 1], (LANES, LANES)).T
        for j, (ref, lane) in enumerate(blocks):
            product = ref[b * LANES:(b + 1) * LANES, lane:lane + LANES] * column
            totals[j] = totals[j] + jnp.sum(product.reshape(LANES // SUB, SUB, LANES), axis=0)
    sums = [jnp.sum(total, axis=0, keepdims=True) for total in totals]
    tiles = []
    for order in orders:
        rows = [None] * len(blocks)
        for j, place in enumerate(order):
            rows[place] = sums[j]
        tiles.append(jnp.concatenate(rows, axis=0))
    tile = pltpu.roll(jnp.where(z_ref[2] == 0, tiles[0], tiles[1]), z_ref[0], 0)
    for peer in range(out_ref.shape[0]):
        out_ref[peer] = tile


def row_scales(orders, total_items, z_ref, got_ref):
    scale = 1.0 / (total_items * jnp.sum(got_ref[...], axis=0))
    tile = pltpu.roll(scale, z_ref[1], 0)
    return [jnp.where(z_ref[2] == 0, tile[a:a + 1], tile[b:b + 1]) for a, b in zip(*orders)]


def col_kernel(orders, total_items, z_ref, got_ref, *refs):
    blocks, out_ref = load_blocks(refs[:-1]), refs[-1]
    scales = row_scales(orders, total_items, z_ref, got_ref)
    rows = []
    for b in range(out_ref.shape[1]):
        folded = jnp.zeros((LANES, LANES), jnp.float32)
        for (ref, lane), scale in zip(blocks, scales):
            folded = folded + ref[b * LANES:(b + 1) * LANES, lane:lane + LANES] * scale
        rows.append(lane_sums(folded))
    tile = jnp.concatenate(rows, axis=0)
    for peer in range(out_ref.shape[0]):
        out_ref[peer] = tile


def numer_kernel(orders, total_items, count, z_ref, got_ref, *refs):
    high_refs, low_refs, out_ref = refs[count:2 * count], refs[2 * count:3 * count], refs[3 * count]
    scales = row_scales(orders, total_items, z_ref, got_ref)
    codes, width = refs[0].shape[0], high_refs[0].shape[1]
    nx = out_ref.shape[0]
    parts = codes // LANES
    step = 256
    mass = []
    for start in range(0, codes, step):
        folded = jnp.zeros((step, LANES), jnp.float32)
        sums, at = None, 0
        for ref, xh_ref, xl_ref in zip(refs[:count], high_refs, low_refs):
            highs, lows = [], []
            for lane in range(0, ref.shape[1], LANES):
                weights = ref[start:start + step, lane:lane + LANES] * scales[at]
                folded = folded + weights
                high, low = split(weights)
                highs.append(high)
                lows.append(low)
                at += 1
            high, low = jnp.concatenate(highs, axis=1), jnp.concatenate(lows, axis=1)
            xh, xl = xh_ref[...], xl_ref[...]
            more = jnp.dot(high, xh, preferred_element_type=jnp.float32) + (
                jnp.dot(low, xh, preferred_element_type=jnp.float32)
                + jnp.dot(high, xl, preferred_element_type=jnp.float32)
            )
            sums = more if sums is None else sums + more
        for part in range(step // LANES):
            mass.append(lane_sums(folded[part * LANES:(part + 1) * LANES]))
            col = start // LANES + part
            for x in range(nx):
                for lane in range(x * width // nx, (x + 1) * width // nx, LANES):
                    turned = sums[part * LANES:(part + 1) * LANES, lane:lane + LANES].T
                    for group in range(LANES // SUB):
                        row = (lane - x * width // nx) // SUB + group
                        out_ref[x, row * parts + col] = turned[group * SUB:(group + 1) * SUB]
    tile = jnp.concatenate(mass + [jnp.ones((SUB - parts, LANES), jnp.float32)], axis=0)
    for x in range(nx):
        out_ref[x, out_ref.shape[1] - 1] = tile


def repack_kernel(got_ref, out_ref):
    summed = got_ref[0]
    for x in range(1, got_ref.shape[0]):
        summed = summed + got_ref[x]
    ny, count = out_ref.shape[0], out_ref.shape[1]
    for y in range(ny):
        out_ref[y, :count - 1] = summed[y * (count - 1):(y + 1) * (count - 1)]
        out_ref[y, count - 1] = summed[ny * (count - 1)]


def lookup_kernel(first, z_ref, index_ref, codes_ref, *refs):
    out_ref, start = refs[-1], 0
    if len(refs) > 1:
        start = refs[0].shape[0]
        out_ref[:start] = refs[0][...]
    part0 = codes_ref[...].astype(jnp.bfloat16)
    rest = codes_ref[...] - part0.astype(jnp.float32)
    part1 = rest.astype(jnp.bfloat16)
    part2 = (rest - part1.astype(jnp.float32)).astype(jnp.bfloat16)
    codes = codes_ref.shape[0]
    for block in range((out_ref.shape[0] - start) // LANES):
        local = index_ref[first + block:first + block + 1] - z_ref[3]
        column = jnp.broadcast_to(local.astype(jnp.float32), (LANES, LANES)).T
        hits = []
        for b in range(codes // LANES):
            lane = lax.broadcasted_iota(jnp.int32, (LANES, LANES), 1) + b * LANES
            hits.append(jnp.where(column == lane.astype(jnp.float32), 1.0, 0.0).astype(jnp.bfloat16))
        chosen = jnp.concatenate(hits, axis=1)
        found = jnp.dot(chosen, part2, preferred_element_type=jnp.float32)
        found = jnp.dot(chosen, part1, preferred_element_type=jnp.float32) + found
        found = jnp.dot(chosen, part0, preferred_element_type=jnp.float32) + found
        out_ref[start + block * LANES:start + (block + 1) * LANES] = found


def finish_kernel(z_ref, got_ref, items_ref, looked_ref, out_ref, residual_ref):
    residual_ref[...] = items_ref[...] - looked_ref[...]
    summed = jnp.sum(got_ref[...], axis=0)
    count = summed.shape[0] - 1
    parts = count // 2
    for core in range(2):
        slot = jnp.where(z_ref[2] == core, 0, 1)
        for b in range(parts):
            out_ref[slot, :, b * LANES:(b + 1) * LANES] = summed[core * parts + b] / summed[count][b:b + 1]


def body(items, codewords, assign):
    f32 = jnp.float32
    n = lax.axis_size("code")
    nx, ny, nc = lax.axis_size("x"), lax.axis_size("y"), lax.axis_size("core")
    local_codes, width = codewords.shape
    own_rows = items.shape[0]
    pair_rows = nc * own_rows
    half = local_codes // nc
    total_items = pair_rows * n * nx * ny
    my_code = lax.axis_index("code")
    core = lax.axis_index("core")
    shift = nc * my_code
    z_info = jnp.stack([shift, lax.rem(nc * n - shift, nc * n), core, my_code * local_codes]).astype(jnp.int32)
    items, z_info = lax.optimization_barrier((items, z_info))
    swap = [(0, 1), (1, 0)]

    other = lax.ppermute(items, "core", swap)
    scaled = jax.ShapeDtypeStruct((half, width), jnp.bfloat16)
    code_high, code_low = call(scale_kernel, (scaled, scaled), [SMEM, VMEM])(z_info, codewords)
    pair = call(pair_kernel, jax.ShapeDtypeStruct((nc,) + items.shape, f32), [SMEM, VMEM, VMEM])(z_info, items, other)

    def chunk(*arrived):
        count = len(arrived)
        lanes = count * pair_rows
        parts = jax.ShapeDtypeStruct((lanes, width), jnp.bfloat16)
        shapes = (
            jax.ShapeDtypeStruct((half, lanes), f32),
            jax.ShapeDtypeStruct((half // LANES, LANES), f32),
            parts,
            parts,
        )
        return call(functools.partial(chunk_kernel, count), shapes, [VMEM] * (2 + count))(code_high, code_low, *arrived)

    index_tile = assign.reshape(-1, LANES)
    piece = index_tile.shape[0] // 2

    def lookup(first, *before):
        rows = piece * LANES * (1 + len(before))
        shape = jax.ShapeDtypeStruct((rows, width), f32)
        operands = [SMEM] + [VMEM] * (2 + len(before))
        return call(functools.partial(lookup_kernel, first), shape, operands, grant=12)(
            z_info, index_tile, codewords, *before
        )

    around = [(i, (i + 1) % n) for i in range(n)] + [(n + i, n + (i - 1) % n) for i in range(n)]
    last = n // 2
    chunks, places = [chunk(pair)], [0]
    came = pair
    named = None
    for step in range(1, last + 1):
        before = came
        came = lax.ppermute(came, ("core", "code"), around)
        if step > 1:
            handed = lax.ppermute(before, "core", swap)
            if step == 2:
                named = lookup(0)
                handed, named = lax.optimization_barrier((handed, named))
            elif step == 3:
                named = lookup(piece, named)
                handed, named = lax.optimization_barrier((handed, named))
            chunks.append(chunk(before, handed))
            places += [n - step + 1, step - 1]
        came, chunks[-1] = lax.optimization_barrier((came, chunks[-1]))
    chunks.append(chunk(came))
    places += [last]
    flipped = [(n - place) % n for place in places]
    orders = [[nc * place + c for place in order for c in range(nc)] for order in (places, flipped)]
    blocks = [c[0] for c in chunks]
    count = len(blocks)
    col_tile, named = lax.optimization_barrier((sum(c[1] for c in chunks), named))
    looked = lax.psum_scatter(named, "code", scatter_dimension=0, tiled=True)

    row_shape = jax.ShapeDtypeStruct((nc * n, nc * n, LANES), f32)
    col_shape = jax.ShapeDtypeStruct((nx * ny,) + col_tile.shape, f32)
    operands = [SMEM, VMEM] + [VMEM] * count
    cols = jnp.broadcast_to(col_tile[None], col_shape.shape)
    for turn in range(ITERS):
        got = lax.all_to_all(cols, ("x", "y"), 0, 0)
        rows = call(functools.partial(row_kernel, orders), row_shape, operands)(z_info, got, *blocks)
        got = lax.all_to_all(rows, ("core", "code"), 0, 0)
        if turn < ITERS - 1:
            cols = call(functools.partial(col_kernel, orders, total_items), col_shape, operands)(z_info, got, *blocks)

    per_owner = width // (nx * ny * nc)
    tiles = ny * nc * (per_owner // SUB) * (half // LANES)
    numer = call(
        functools.partial(numer_kernel, orders, total_items, count),
        jax.ShapeDtypeStruct((nx, tiles + 1, SUB, LANES), f32),
        operands + [VMEM] * (2 * count),
        grant=16,
    )(z_info, got, *blocks, *[c[2] for c in chunks], *[c[3] for c in chunks])
    got = lax.all_to_all(numer, "x", 0, 0)
    got, looked = lax.optimization_barrier((got, looked))
    packed = call(repack_kernel, jax.ShapeDtypeStruct((ny, tiles // ny + 1, SUB, LANES), f32), [VMEM])(got)
    got = lax.all_to_all(packed, "y", 0, 0)
    shapes = (jax.ShapeDtypeStruct((nc, per_owner, half), f32), jax.ShapeDtypeStruct(items.shape, f32))
    turned, residual = call(finish_kernel, shapes, [SMEM] + [VMEM] * 3)(z_info, got, items, looked)
    mine, given = turned[0], lax.ppermute(turned[1], "core", swap)
    new_codewords = jnp.concatenate([jnp.where(core == 0, mine, given), jnp.where(core == 0, given, mine)], axis=1).T
    return (new_codewords, residual)


def solution(mesh):
    cores = 2
    ny = 8
    dp, code = mesh.devices.shape
    fine = Mesh(
        mesh.devices.reshape(dp // (ny * cores), ny, cores, code),
        ("x", "y", "core", "code"),
    )
    in_specs = (P(DP + ("code",), None), P("code", None), P(DP))
    out_specs = (P("code", DP), P(DP + ("code",), None))
    return jax.shard_map(body, mesh=fine, in_specs=in_specs, out_specs=out_specs, check_vma=False)
```

time: 227 us -> 217 us (0.956)
  starting transfers between devices: 50.3 us -> 39.9 us
  blocking collectives: 103 us -> 113 us
  other arithmetic: 6.45 us -> 0.71 us
  Pallas kernels: 20 us -> 24.7 us
  waiting for transfers between devices: 9.25 us -> 4.96 us
  local copies, waits for them, and re-layouts: 21.4 us -> 18.4 us
    all_to_all x7, blocking collectives: 90.1 us -> 101 us  [the longest x3 42.5 us: body(): got = lax.all_to_all(rows, ('core', 'code'), 0, 0)]
    ppermute x11 -> x9, starting transfers between devices: 50.3 us -> 39.9 us  [the longest x4 15.6 us: body(): came = lax.ppermute(came, ('core', 'code'), around)]
    pallas_call x9 -> x12, Pallas kernels: 10.5 us -> 17 us  [the longest x2 5.28 us: lookup(): call(functools.partial(lookup_kernel, first), shape, operands, grant=12)]
    gather x1 -> x0, local copies, waits for them, and re-layouts: 4.86 us -> none  [body(): jnp.take(codewords, jnp.clip(index_rows, 0, local_codes - 1), axis=0)]
    ppermute x11 -> x9, waiting for transfers between devices: 9.21 us -> 4.95 us  [the longest x4 2.78 us: body(): came = lax.ppermute(came, ('core', 'code'), around)]
    select_n x1, other arithmetic: 3.23 us -> 0.01 us  [body(): jnp.where(core == 0, mine, given)]
    unnamed x72 -> x74, local copies, waits for them, and re-layouts: 16.4 us -> 18.4 us
  transfers between devices with their start and end apart: 12 -> 10, of which waited for: 7 -> 5; matrix products, arithmetic and copies ran while one was open for 4% -> 0% of each run, Pallas kernels for 8% -> 10%
where the time goes in v3:
time: 217 us; the launch traced here: 216 us
  blocking collectives  113 us (52%)
  starting transfers between devices  39.9 us (18%)
  Pallas kernels  24.7 us (11%)
  local copies, waits for them, and re-layouts  18.4 us (8%)
  between operations  14.5 us (7%)
  waiting for transfers between devices  4.96 us (2%)
    all_to_all x3, blocking collectives, body(): got = lax.all_to_all(rows, ('core', 'code'), 0, 0)  42.5 us
    all_to_all x3, blocking collectives, body(): got = lax.all_to_all(cols, ('x', 'y'), 0, 0)  42.1 us
    unnamed x74, local copies, waits for them, and re-layouts  18.4 us
    all_to_all x1, blocking collectives, body(): got = lax.all_to_all(numer, 'x', 0, 0)  16.5 us
    ppermute x4, starting transfers between devices, body(): came = lax.ppermute(came, ('core', 'code'), around)  15.6 us
    all_to_all x1, blocking collectives, body(): got = lax.all_to_all(packed, 'y', 0, 0)  12 us
    ppermute x3, starting transfers between devices, body(): handed = lax.ppermute(before, 'core', swap)  9.6 us
    ppermute x1, starting transfers between devices, body(): other = lax.ppermute(items, 'core', swap)  8.78 us
  transfers between devices with their start and end apart: 10, of which 5 were waited for; matrix products, arithmetic and copies ran while one was open for 0% of the time, Pallas kernels for 10%

profile of v3, /device:TPU:1, one launch (start us, length us, event | category | flops | bytes accessed | tf_op | source)
XLA Modules:
  0.0 216.4 jit_solution(6060472948590190480)
XLA Ops:
  7.3 8.8 %collective-permute-start = (f32[128,512]{1,0:T(8,128)}, f32[128,512]{1,0:T(8,128)S(1)}, u32[]{:S(2)}, u32[]{:S(2)}) collective-permute-start(f32[128,512]{1,0:T(8,128)} %items_ref), channel_id=1, source_target_pairs={{0,8},{8,0},{1,9},{9,1},{2,10},{10,2},{3,11},{11,3},{4,12},{12,4},... | collective-permute-start | bytes 786440 | tf_op jit(solution)/shard_map/ppermute | solution.py:240
  16.1 1.4 collective-permute-done.other_ref
  19.0 5.3 %collective-permute-start.1 = (f32[2,128,512]{2,1,0:T(8,128)S(1)}, f32[2,128,512]{2,1,0:T(8,128)S(1)}, u32[]{:S(2)}, u32[]{:S(2)}) collective-permute-start(f32[2,128,512]{2,1,0:T(8,128)S(1)} %shard_map.50.refs_0_), channel_id=1, source_target_pairs={{0,1},{1,2},{2,3},{3,4},{4,5},{5,6},{6,7},{7,0},{8,15},{9,8},{10,9... | collective-permute-start | bytes 1572872 | tf_op jit(solution)/shard_map/ppermute | solution.py:275
  24.3 1.6 copy-done.6
  29.1 1.3 collective-permute-done.1.refs_0_
  30.4 3.6 %collective-permute-start.3 = (f32[2,128,512]{2,1,0:T(8,128)S(1)}, f32[2,128,512]{2,1,0:T(8,128)S(1)}, u32[]{:S(2)}, u32[]{:S(2)}) collective-permute-start(f32[2,128,512]{2,1,0:T(8,128)S(1)} %collective-permute-done.1.refs_0_), channel_id=1, source_target_pairs={{0,8},{8,0},{1,9},{9,1},{2,10},{10,2},{3,11},{11,3},{4,12},{12,4},... | collective-permute-start | bytes 1572872 | tf_op jit(solution)/shard_map/ppermute | solution.py:277
  34.0 3.6 %collective-permute-start.2 = (f32[2,128,512]{2,1,0:T(8,128)S(1)}, f32[2,128,512]{2,1,0:T(8,128)}, u32[]{:S(2)}, u32[]{:S(2)}) collective-permute-start(f32[2,128,512]{2,1,0:T(8,128)S(1)} %collective-permute-done.1.refs_0_), channel_id=1, source_target_pairs={{0,1},{1,2},{2,3},{3,4},{4,5},{5,6},{6,7},{7,0},{8,15},{9,8},{10,9... | collective-permute-start | bytes 1572872 | tf_op jit(solution)/shard_map/ppermute | solution.py:275
  37.6 2.6 %shard_map.53.refs_0_ = f32[512,512]{1,0:T(8,128)S(1)} custom-call(s32[4]{0:T(128)S(1)} %pad_add_fusion.z_ref, s32[8,128]{1,0:T(8,128)S(1)} %bitcast.12, f32[1024,512]{1,0:T(8,128)S(1)} %copy-done.7), custom_call_target="tpu_custom_call" | custom-call | tf_op jit(solution)/shard_map/pallas_call | solution.py:264
  40.3 1.3 shard_map.54
  43.2 1.1 collective-permute-done.2.refs_0_
  44.3 4.0 %collective-permute-start.5 = (f32[2,128,512]{2,1,0:T(8,128)}, f32[2,128,512]{2,1,0:T(8,128)S(1)}, u32[]{:S(2)}, u32[]{:S(2)}) collective-permute-start(f32[2,128,512]{2,1,0:T(8,128)} %collective-permute-done.2.refs_0_), channel_id=1, source_target_pairs={{0,8},{8,0},{1,9},{9,1},{2,10},{10,2},{3,11},{11,3},{4,12},{12,4},... | collective-permute-start | bytes 1572872 | tf_op jit(solution)/shard_map/ppermute | solution.py:277
  48.3 2.6 %collective-permute-start.4 = (f32[2,128,512]{2,1,0:T(8,128)}, f32[2,128,512]{2,1,0:T(8,128)}, u32[]{:S(2)}, u32[]{:S(2)}) collective-permute-start(f32[2,128,512]{2,1,0:T(8,128)} %collective-permute-done.2.refs_0_), channel_id=1, source_target_pairs={{0,1},{1,2},{2,3},{3,4},{4,5},{5,6},{6,7},{7,0},{8,15},{9,8},{10,9... | collective-permute-start | bytes 1572872 | tf_op jit(solution)/shard_map/ppermute | solution.py:275
  50.9 2.7 %shard_map.55 = f32[1024,512]{1,0:T(8,128)S(1)} custom-call(s32[4]{0:T(128)S(1)} %pad_add_fusion.z_ref, s32[8,128]{1,0:T(8,128)S(1)} %bitcast.13, f32[1024,512]{1,0:T(8,128)S(1)} %copy-done.7, f32[512,512]{1,0:T(8,128)S(1)} %shard_map.53.refs_0_), custom_call_target="tpu_custom_call" | custom-call | tf_op jit(solution)/shard_map/pallas_call | solution.py:264
  53.6 1.3 copy-done.12
  55.8 1.0 copy-done.28
  56.8 2.4 %shard_map.56 = (f32[512,512]{1,0:T(8,128)S(1)}, f32[4,128]{1,0:T(4,128)S(1)}, bf16[512,512]{1,0:T(8,128)(2,1)S(1)}, bf16[512,512]{1,0:T(8,128)(2,1)S(1)}) custom-call(bf16[512,512]{1,0:T(8,128)(2,1)S(1)} %get-tuple-element.58.high_ref, bf16[512,512]{1,0:T(8,128)(2,1)S(1)} %get-tuple-element.59.low_ref, f32[2,128,512]{2,1,0:T(8,128)} %collective-permute-done.2.refs_0_, ...), custom_call_target="tpu_custom_call" | custom-call | tf_op jit(solution)/shard_map/pallas_call | solution.py:255
  60.8 2.0 collective-permute-start.7
  62.8 4.0 %collective-permute-start.6 = (f32[2,128,512]{2,1,0:T(8,128)}, f32[2,128,512]{2,1,0:T(8,128)S(1)}, u32[]{:S(2)}, u32[]{:S(2)}) collective-permute-start(f32[2,128,512]{2,1,0:T(8,128)} %collective-permute-done.4.refs_0_), channel_id=1, source_target_pairs={{0,1},{1,2},{2,3},{3,4},{4,5},{5,6},{6,7},{7,0},{8,15},{9,8},{10,9... | collective-permute-start | bytes 1572872 | tf_op jit(solution)/shard_map/ppermute | solution.py:275
  68.9 2.4 %shard_map.57 = (f32[512,512]{1,0:T(8,128)S(1)}, f32[4,128]{1,0:T(4,128)S(1)}, bf16[512,512]{1,0:T(8,128)(2,1)S(1)}, bf16[512,512]{1,0:T(8,128)(2,1)S(1)}) custom-call(bf16[512,512]{1,0:T(8,128)(2,1)S(1)} %copy-done.9, bf16[512,512]{1,0:T(8,128)(2,1)S(1)} %copy-done.11, f32[2,128,512]{2,1,0:T(8,128)} %collective-permute-done.4.refs_0_, ...), custom_call_target="tpu_custom_call" | custom-call | tf_op jit(solution)/shard_map/pallas_call | solution.py:255
  76.3 18.3 %all_to_all.40.got_ref = f32[32,4,128]{2,1,0:T(4,128)S(1)} all-to-all(f32[32,4,128]{2,1,0:T(4,128)S(1)} %broadcast_in_dim.2), channel_id=1, replica_groups=mesh['x'=4,'y'=8,'core'=2,'code'=8] {'x','y'}, dimensions={0} | all-to-all | bytes 131072 | tf_op jit(solution)/shard_map/all_to_all | solution.py:301
  94.7 1.0 copy-done.1
  95.7 1.0 copy-done.4
  97.7 16.6 %all_to_all.41.got_ref = f32[16,16,128]{2,1,0:T(8,128)S(1)} all-to-all(f32[16,16,128]{2,1,0:T(8,128)S(1)} %shard_map.59), channel_id=1, replica_groups=mesh['x'=4,'y'=8,'core'=2,'code'=8] {'core','code'}, dimensions={0} | all-to-all | bytes 262144 | tf_op jit(solution)/shard_map/all_to_all | solution.py:303
  115.3 11.9 %all_to_all.42.got_ref = f32[32,4,128]{2,1,0:T(4,128)S(1)} all-to-all(f32[32,4,128]{2,1,0:T(4,128)S(1)} %shard_map.60), channel_id=1, replica_groups=mesh['x'=4,'y'=8,'core'=2,'code'=8] {'x','y'}, dimensions={0} | all-to-all | bytes 131072 | tf_op jit(solution)/shard_map/all_to_all | solution.py:301
  128.2 12.8 %all_to_all.43.got_ref = f32[16,16,128]{2,1,0:T(8,128)S(1)} all-to-all(f32[16,16,128]{2,1,0:T(8,128)S(1)} %shard_map.61), channel_id=1, replica_groups=mesh['x'=4,'y'=8,'core'=2,'code'=8] {'core','code'}, dimensions={0} | all-to-all | bytes 262144 | tf_op jit(solution)/shard_map/all_to_all | solution.py:303
  142.0 11.9 %all_to_all.44.got_ref = f32[32,4,128]{2,1,0:T(4,128)S(1)} all-to-all(f32[32,4,128]{2,1,0:T(4,128)S(1)} %shard_map.62), channel_id=1, replica_groups=mesh['x'=4,'y'=8,'core'=2,'code'=8] {'x','y'}, dimensions={0} | all-to-all | bytes 131072 | tf_op jit(solution)/shard_map/all_to_all | solution.py:301
  154.9 13.0 %all_to_all.45.got_ref = f32[16,16,128]{2,1,0:T(8,128)S(1)} all-to-all(f32[16,16,128]{2,1,0:T(8,128)S(1)} %shard_map.63), channel_id=1, replica_groups=mesh['x'=4,'y'=8,'core'=2,'code'=8] {'core','code'}, dimensions={0} | all-to-all | bytes 262144 | tf_op jit(solution)/shard_map/all_to_all | solution.py:303
  168.0 4.3 %shard_map.64 = f32[4,65,8,128]{3,2,1,0:T(8,128)S(1)} custom-call(s32[4]{0:T(128)S(1)} %pad_add_fusion.z_ref, f32[16,16,128]{2,1,0:T(8,128)S(1)} %all_to_all.45.got_ref, f32[512,256]{1,0:T(8,128)S(1)} %copy-done.2, f32[512,512]{1,0:T(8,128)S(1)} %get-tuple-element.91.refs_1_, f32[512,512]{1,0:T(8,128)S(1)} %get-tuple-element.92.refs_2_, ...), custom_call_target="tpu_custom_call" | custom-call | tf_op jit(solution)/shard_map/pallas_call | solution.py:309
  172.2 16.5 %all_to_all.46.got_ref = f32[4,65,8,128]{3,2,1,0:T(8,128)S(1)} all-to-all(f32[4,65,8,128]{3,2,1,0:T(8,128)S(1)} %shard_map.64), channel_id=1, replica_groups=mesh['x'=4,'y'=8,'core'=2,'code'=8] {'x'}, dimensions={0} | all-to-all | bytes 2129920 | tf_op jit(solution)/shard_map/all_to_all | solution.py:315
  188.8 12.0 %all_to_all.47.got_ref = f32[8,9,8,128]{3,2,1,0:T(8,128)S(1)} all-to-all(f32[8,9,8,128]{3,2,1,0:T(8,128)S(1)} %shard_map.65), channel_id=1, replica_groups=mesh['x'=4,'y'=8,'core'=2,'code'=8] {'y'}, dimensions={0} | all-to-all | bytes 589824 | tf_op jit(solution)/shard_map/all_to_all | solution.py:318
  200.9 1.3 shard_map.66
  202.2 5.9 %collective-permute-start.8 = (f32[8,512]{1,0:T(8,128)S(1)}, f32[8,512]{1,0:T(8,128)S(1)}, u32[]{:S(2)}, u32[]{:S(2)}) collective-permute-start(f32[8,512]{1,0:T(8,128)S(1)} %slice_bitcast_fusion), channel_id=1, source_target_pairs={{0,8},{8,0},{1,9},{9,1},{2,10},{10,2},{3,11},{11,3},{4,12},{12,4},... | collective-permute-start | bytes 49160 | tf_op jit(solution)/shard_map/ppermute | solution.py:321
  (94 shorter events, 22.2 us)
Async XLA Ops:
  7.2 181.6 %reduce-scatter.2.cloned.1.call-start = ((), (), s32[]{:S(2)}) async-start(), calls=%async_computation.9 | async-start | bytes 2359296 | tf_op jit(solution)/shard_map/reduce_scatter | solution.py:294
  7.3 10.1 %collective-permute-start = (f32[128,512]{1,0:T(8,128)}, f32[128,512]{1,0:T(8,128)S(1)}, u32[]{:S(2)}, u32[]{:S(2)}) collective-permute-start(f32[128,512]{1,0:T(8,128)} %items_ref), channel_id=1, source_target_pairs={{0,8},{8,0},{1,9},{9,1},{2,10},{10,2},{3,11},{11,3},{4,12},{12,4},... | collective-permute-start | bytes 786440 | tf_op jit(solution)/shard_map/ppermute | solution.py:240
  19.0 11.4 %collective-permute-start.1 = (f32[2,128,512]{2,1,0:T(8,128)S(1)}, f32[2,128,512]{2,1,0:T(8,128)S(1)}, u32[]{:S(2)}, u32[]{:S(2)}) collective-permute-start(f32[2,128,512]{2,1,0:T(8,128)S(1)} %shard_map.50.refs_0_), channel_id=1, source_target_pairs={{0,1},{1,2},{2,3},{3,4},{4,5},{5,6},{6,7},{7,0},{8,15},{9,8},{10,9... | collective-permute-start | bytes 1572872 | tf_op jit(solution)/shard_map/ppermute | solution.py:275
  24.3 1.6 copy-start.6
  25.9 11.8 %copy-start.7 = (f32[1024,512]{1,0:T(8,128)S(1)}, f32[1024,512]{1,0:T(8,128)}, u32[]{:S(2)}) copy-start(f32[1024,512]{1,0:T(8,128)} %codes_ref.5) | copy-start | bytes 6291460
  25.9 11.8 %copy-start.36 = (s32[1024]{0:T(1024)S(1)}, s32[1024]{0:T(1024)}, u32[]{:S(2)}) copy-start(s32[1024]{0:T(1024)} %param.5) | copy-start | bytes 12292
  26.7 28.2 %copy-start.8 = (bf16[512,512]{1,0:T(8,128)(2,1)}, bf16[512,512]{1,0:T(8,128)(2,1)S(1)}, u32[]{:S(2)}) copy-start(bf16[512,512]{1,0:T(8,128)(2,1)S(1)} %get-tuple-element.58.high_ref) | copy-start | bytes 1572868
  26.7 28.2 %copy-start.10 = (bf16[512,512]{1,0:T(8,128)(2,1)}, bf16[512,512]{1,0:T(8,128)(2,1)S(1)}, u32[]{:S(2)}) copy-start(bf16[512,512]{1,0:T(8,128)(2,1)S(1)} %get-tuple-element.59.low_ref) | copy-start | bytes 1572868
  30.4 9.9 %collective-permute-start.3 = (f32[2,128,512]{2,1,0:T(8,128)S(1)}, f32[2,128,512]{2,1,0:T(8,128)S(1)}, u32[]{:S(2)}, u32[]{:S(2)}) collective-permute-start(f32[2,128,512]{2,1,0:T(8,128)S(1)} %collective-permute-done.1.refs_0_), channel_id=1, source_target_pairs={{0,8},{8,0},{1,9},{9,1},{2,10},{10,2},{3,11},{11,3},{4,12},{12,4},... | collective-permute-start | bytes 1572872 | tf_op jit(solution)/shard_map/ppermute | solution.py:277
  34.0 10.3 %collective-permute-start.2 = (f32[2,128,512]{2,1,0:T(8,128)S(1)}, f32[2,128,512]{2,1,0:T(8,128)}, u32[]{:S(2)}, u32[]{:S(2)}) collective-permute-start(f32[2,128,512]{2,1,0:T(8,128)S(1)} %collective-permute-done.1.refs_0_), channel_id=1, source_target_pairs={{0,1},{1,2},{2,3},{3,4},{4,5},{5,6},{6,7},{7,0},{8,15},{9,8},{10,9... | collective-permute-start | bytes 1572872 | tf_op jit(solution)/shard_map/ppermute | solution.py:275
  44.3 10.6 %collective-permute-start.5 = (f32[2,128,512]{2,1,0:T(8,128)}, f32[2,128,512]{2,1,0:T(8,128)S(1)}, u32[]{:S(2)}, u32[]{:S(2)}) collective-permute-start(f32[2,128,512]{2,1,0:T(8,128)} %collective-permute-done.2.refs_0_), channel_id=1, source_target_pairs={{0,8},{8,0},{1,9},{9,1},{2,10},{10,2},{3,11},{11,3},{4,12},{12,4},... | collective-permute-start | bytes 1572872 | tf_op jit(solution)/shard_map/ppermute | solution.py:277
  48.3 12.5 %collective-permute-start.4 = (f32[2,128,512]{2,1,0:T(8,128)}, f32[2,128,512]{2,1,0:T(8,128)}, u32[]{:S(2)}, u32[]{:S(2)}) collective-permute-start(f32[2,128,512]{2,1,0:T(8,128)} %collective-permute-done.2.refs_0_), channel_id=1, source_target_pairs={{0,1},{1,2},{2,3},{3,4},{4,5},{5,6},{6,7},{7,0},{8,15},{9,8},{10,9... | collective-permute-start | bytes 1572872 | tf_op jit(solution)/shard_map/ppermute | solution.py:275
  53.6 1.3 copy-start.12
  60.8 6.1 %collective-permute-start.7 = (f32[2,128,512]{2,1,0:T(8,128)}, f32[2,128,512]{2,1,0:T(8,128)S(1)}, u32[]{:S(2)}, u32[]{:S(2)}) collective-permute-start(f32[2,128,512]{2,1,0:T(8,128)} %collective-permute-done.4.refs_0_), channel_id=1, source_target_pairs={{0,8},{8,0},{1,9},{9,1},{2,10},{10,2},{3,11},{11,3},{4,12},{12,4},... | collective-permute-start | bytes 1572872 | tf_op jit(solution)/shard_map/ppermute | solution.py:277
  62.8 10.5 %collective-permute-start.6 = (f32[2,128,512]{2,1,0:T(8,128)}, f32[2,128,512]{2,1,0:T(8,128)S(1)}, u32[]{:S(2)}, u32[]{:S(2)}) collective-permute-start(f32[2,128,512]{2,1,0:T(8,128)} %collective-permute-done.4.refs_0_), channel_id=1, source_target_pairs={{0,1},{1,2},{2,3},{3,4},{4,5},{5,6},{6,7},{7,0},{8,15},{9,8},{10,9... | collective-permute-start | bytes 1572872 | tf_op jit(solution)/shard_map/ppermute | solution.py:275
  66.8 1.0 copy-start.9
  94.7 1.0 copy-start.1
  95.7 1.0 copy-start.4
  141.0 26.8 %copy-start.32 = (bf16[256,512]{1,0:T(8,128)(2,1)S(1)}, bf16[256,512]{1,0:T(8,128)(2,1)}, u32[]{:S(2)}) copy-start(bf16[256,512]{1,0:T(8,128)(2,1)} %copy-done.31) | copy-start | bytes 786436
  141.0 26.8 %copy-start.34 = (bf16[256,512]{1,0:T(8,128)(2,1)S(1)}, bf16[256,512]{1,0:T(8,128)(2,1)}, u32[]{:S(2)}) copy-start(bf16[256,512]{1,0:T(8,128)(2,1)} %copy-done.33) | copy-start | bytes 786436
  153.9 14.0 %copy-start.2 = (f32[512,256]{1,0:T(8,128)S(1)}, f32[512,256]{1,0:T(8,128)}, u32[]{:S(2)}) copy-start(f32[512,256]{1,0:T(8,128)} %copy-done) | copy-start | bytes 1572868
  153.9 14.0 %copy-start.5 = (f32[512,256]{1,0:T(8,128)S(1)}, f32[512,256]{1,0:T(8,128)}, u32[]{:S(2)}) copy-start(f32[512,256]{1,0:T(8,128)} %copy-done.3) | copy-start | bytes 1572868
  153.9 14.0 %copy-start.16 = (bf16[512,512]{1,0:T(8,128)(2,1)S(1)}, bf16[512,512]{1,0:T(8,128)(2,1)}, u32[]{:S(2)}) copy-start(bf16[512,512]{1,0:T(8,128)(2,1)} %copy-done.15) | copy-start | bytes 1572868
  153.9 14.1 %copy-start.18 = (bf16[512,512]{1,0:T(8,128)(2,1)S(1)}, bf16[512,512]{1,0:T(8,128)(2,1)}, u32[]{:S(2)}) copy-start(bf16[512,512]{1,0:T(8,128)(2,1)} %copy-done.17) | copy-start | bytes 1572868
  153.9 14.1 %copy-start.20 = (bf16[512,512]{1,0:T(8,128)(2,1)S(1)}, bf16[512,512]{1,0:T(8,128)(2,1)}, u32[]{:S(2)}) copy-start(bf16[512,512]{1,0:T(8,128)(2,1)} %copy-done.19) | copy-start | bytes 1572868
  153.9 14.1 %copy-start.22 = (bf16[512,512]{1,0:T(8,128)(2,1)S(1)}, bf16[512,512]{1,0:T(8,128)(2,1)}, u32[]{:S(2)}) copy-start(bf16[512,512]{1,0:T(8,128)(2,1)} %copy-done.21) | copy-start | bytes 1572868
  153.9 14.1 %copy-start.24 = (bf16[512,512]{1,0:T(8,128)(2,1)S(1)}, bf16[512,512]{1,0:T(8,128)(2,1)}, u32[]{:S(2)}) copy-start(bf16[512,512]{1,0:T(8,128)(2,1)} %copy-done.23) | copy-start | bytes 1572868
  153.9 14.1 %copy-start.26 = (bf16[512,512]{1,0:T(8,128)(2,1)S(1)}, bf16[512,512]{1,0:T(8,128)(2,1)}, u32[]{:S(2)}) copy-start(bf16[512,512]{1,0:T(8,128)(2,1)} %copy-done.25) | copy-start | bytes 1572868
  153.9 14.1 %copy-start.30 = (bf16[256,512]{1,0:T(8,128)(2,1)S(1)}, bf16[256,512]{1,0:T(8,128)(2,1)}, u32[]{:S(2)}) copy-start(bf16[256,512]{1,0:T(8,128)(2,1)} %copy-done.29) | copy-start | bytes 786436
  172.2 28.6 %copy-start.14 = (f32[128,512]{1,0:T(8,128)S(1)}, f32[128,512]{1,0:T(8,128)}, u32[]{:S(2)}) copy-start(f32[128,512]{1,0:T(8,128)} %items_ref) | copy-start | bytes 786436
  188.8 12.1 %copy-start.35 = (f32[128,512]{1,0:T(8,128)S(1)}, f32[128,512]{1,0:T(8,128)}, u32[]{:S(2)}) copy-start(f32[128,512]{1,0:T(8,128)} %reduce-scatter.2.cloned.1.call-done.looked_ref) | copy-start | bytes 786436
  202.2 6.8 %collective-permute-start.8 = (f32[8,512]{1,0:T(8,128)S(1)}, f32[8,512]{1,0:T(8,128)S(1)}, u32[]{:S(2)}, u32[]{:S(2)}) collective-permute-start(f32[8,512]{1,0:T(8,128)S(1)} %slice_bitcast_fusion), channel_id=1, source_target_pairs={{0,8},{8,0},{1,9},{9,1},{2,10},{10,2},{3,11},{11,3},{4,12},{12,4},... | collective-permute-start | bytes 49160 | tf_op jit(solution)/shard_map/ppermute | solution.py:321
  (15 other events, 12.3 us)
Sparse Core Ops, SparseCore 0:
  76.4 44.2 reduce-scatter.1

commit v4 on v3

v4 whole, which is shorter than its diff:
```python
import functools

import jax
import jax.numpy as jnp
from jax import lax
from jax.experimental import pallas as pl
from jax.experimental.pallas import tpu as pltpu
from jax.sharding import Mesh, PartitionSpec as P

K = 8192
ITERS = 3
DP = ("x", "y", "core")
LANES = 128
SUB = 8

epsilon = 1e-05
inverse_temp = 64.0

VMEM = pl.BlockSpec(memory_space=pltpu.VMEM)
SMEM = pl.BlockSpec(memory_space=pltpu.SMEM)
MIB = 1024 * 1024


def call(body, out_shape, ins, scratch=(), grant=8):
    return pl.pallas_call(
        body,
        out_shape=out_shape,
        in_specs=ins,
        out_specs=jax.tree.map(lambda _: VMEM, out_shape),
        scratch_shapes=list(scratch),
        compiler_params=pltpu.CompilerParams(vmem_limit_bytes=grant * MIB),
    )


def split(values):
    high = values.astype(jnp.bfloat16)
    return high, (values - high.astype(jnp.float32)).astype(jnp.bfloat16)


def unit_rows(values):
    return values * lax.rsqrt(jnp.mean(values * values, axis=-1, keepdims=True) + epsilon)


def dot_nt(a, b):
    return lax.dot_general(a, b, (((1,), (1,)), ((), ())), preferred_element_type=jnp.float32)


def lane_sums(block):
    return jnp.sum(block.T, axis=0, keepdims=True)


def scale_kernel(z_ref, codes_ref, high_ref, low_ref):
    half, width = high_ref.shape
    codes = codes_ref[pl.ds(pl.multiple_of(z_ref[0] * half, half), half)]
    high, low = split(unit_rows(codes) * (inverse_temp / width))
    high_ref[...] = high
    low_ref[...] = low


def chunk_kernel(high_ref, low_ref, items_ref, out_ref, sums_ref, xh_ref, xl_ref):
    codes, step = high_ref.shape[0], 256
    folded = [jnp.zeros((step, LANES), jnp.float32) for _ in range(0, codes, step)]
    for first in range(0, items_ref.shape[0], step):
        values = items_ref[first:first + step]
        xh_ref[first:first + step], xl_ref[first:first + step] = split(values)
        item_high, item_low = split(unit_rows(values))
        for k, start in enumerate(range(0, codes, step)):
            code_high = high_ref[start:start + step]
            code_low = low_ref[start:start + step]
            logits = dot_nt(code_high, item_high) + (dot_nt(code_high, item_low) + dot_nt(code_low, item_high))
            values = jnp.exp(logits)
            out_ref[start:start + step, first:first + step] = values
            for lane in range(0, step, LANES):
                folded[k] = folded[k] + values[:, lane:lane + LANES]
    for k, total in enumerate(folded):
        for part in range(step // LANES):
            row = k * (step // LANES) + part
            sums_ref[row:row + 1] = lane_sums(total[part * LANES:(part + 1) * LANES])


def load_blocks(refs):
    return [(ref, j * LANES) for ref in refs for j in range(ref.shape[1] // LANES)]


def row_kernel(z_ref, got_ref, *refs):
    blocks, out_ref = load_blocks(refs[:-1]), refs[-1]
    scale = 1.0 / (K * jnp.sum(got_ref[...], axis=0))
    totals = [jnp.zeros((SUB, LANES), jnp.float32) for _ in blocks]
    for b in range(scale.shape[0]):
        column = jnp.broadcast_to(scale[b:b + 1], (LANES, LANES)).T
        for j, (ref, lane) in enumerate(blocks):
            product = ref[b * LANES:(b + 1) * LANES, lane:lane + LANES] * column
            totals[j] = totals[j] + jnp.sum(product.reshape(LANES // SUB, SUB, LANES), axis=0)
    sums = [jnp.sum(total, axis=0, keepdims=True) for total in totals]
    group = len(sums) // 2
    own, other = jnp.concatenate(sums[:group], axis=0), jnp.concatenate(sums[group:], axis=0)
    first = z_ref[0] == 0
    tile = jnp.concatenate([jnp.where(first, own, other), jnp.where(first, other, own)], axis=0)
    for peer in range(out_ref.shape[0]):
        out_ref[peer] = tile


def row_scales(total_items, z_ref, got_ref):
    scale = 1.0 / (total_items * jnp.sum(got_ref[...], axis=0))
    group = scale.shape[0] // 2
    first = z_ref[0] == 0
    own, other = scale[:group], scale[group:]
    tiles = jnp.where(first, own, other), jnp.where(first, other, own)
    return [tile[row:row + 1] for tile in tiles for row in range(group)]


def col_kernel(total_items, z_ref, got_ref, *refs):
    blocks, out_ref = load_blocks(refs[:-1]), refs[-1]
    scales = row_scales(total_items, z_ref, got_ref)
    rows = []
    for b in range(out_ref.shape[1]):
        folded = jnp.zeros((LANES, LANES), jnp.float32)
        for (ref, lane), scale in zip(blocks, scales):
            folded = folded + ref[b * LANES:(b + 1) * LANES, lane:lane + LANES] * scale
        rows.append(lane_sums(folded))
    tile = jnp.concatenate(rows, axis=0)
    for peer in range(out_ref.shape[0]):
        out_ref[peer] = tile


def numer_kernel(total_items, count, z_ref, got_ref, *refs):
    high_refs, low_refs, out_ref = refs[count:2 * count], refs[2 * count:3 * count], refs[3 * count]
    scales = row_scales(total_items, z_ref, got_ref)
    codes, width = refs[0].shape[0], high_refs[0].shape[1]
    nx = out_ref.shape[0]
    parts = codes // LANES
    step = 256
    mass = []
    for start in range(0, codes, step):
        folded = jnp.zeros((step, LANES), jnp.float32)
        sums, at = None, 0
        for ref, xh_ref, xl_ref in zip(refs[:count], high_refs, low_refs):
            highs, lows = [], []
            for lane in range(0, ref.shape[1], LANES):
                weights = ref[start:start + step, lane:lane + LANES] * scales[at]
                folded = folded + weights
                high, low = split(weights)
                highs.append(high)
                lows.append(low)
                at += 1
            high, low = jnp.concatenate(highs, axis=1), jnp.concatenate(lows, axis=1)
            xh, xl = xh_ref[...], xl_ref[...]
            more = jnp.dot(high, xh, preferred_element_type=jnp.float32) + (
                jnp.dot(low, xh, preferred_element_type=jnp.float32)
                + jnp.dot(high, xl, preferred_element_type=jnp.float32)
            )
            sums = more if sums is None else sums + more
        for part in range(step // LANES):
            mass.append(lane_sums(folded[part * LANES:(part + 1) * LANES]))
            col = start // LANES + part
            for x in range(nx):
                for lane in range(x * width // nx, (x + 1) * width // nx, LANES):
                    turned = sums[part * LANES:(part + 1) * LANES, lane:lane + LANES].T
                    for group in range(LANES // SUB):
                        row = (lane - x * width // nx) // SUB + group
                        out_ref[x, row * parts + col] = turned[group * SUB:(group + 1) * SUB]
    tile = jnp.concatenate(mass + [jnp.ones((SUB - parts, LANES), jnp.float32)], axis=0)
    for x in range(nx):
        out_ref[x, out_ref.shape[1] - 1] = tile


def repack_kernel(got_ref, out_ref):
    summed = got_ref[0]
    for x in range(1, got_ref.shape[0]):
        summed = summed + got_ref[x]
    peers, count = out_ref.shape[0], out_ref.shape[1] - 1
    for peer in range(peers):
        out_ref[peer, :count] = summed[peer * count:(peer + 1) * count]
        out_ref[peer, count] = summed[peers * count]


def lookup_kernel(z_ref, index_ref, codes_ref, out_ref):
    part0 = codes_ref[...].astype(jnp.bfloat16)
    rest = codes_ref[...] - part0.astype(jnp.float32)
    part1 = rest.astype(jnp.bfloat16)
    part2 = (rest - part1.astype(jnp.float32)).astype(jnp.bfloat16)
    codes = codes_ref.shape[0]
    for block in range(out_ref.shape[0] // LANES):
        local = index_ref[block:block + 1] - z_ref[1]
        column = jnp.broadcast_to(local.astype(jnp.float32), (LANES, LANES)).T
        hits = []
        for b in range(codes // LANES):
            lane = lax.broadcasted_iota(jnp.int32, (LANES, LANES), 1) + b * LANES
            hits.append(jnp.where(column == lane.astype(jnp.float32), 1.0, 0.0).astype(jnp.bfloat16))
        chosen = jnp.concatenate(hits, axis=1)
        found = jnp.dot(chosen, part2, preferred_element_type=jnp.float32)
        found = jnp.dot(chosen, part1, preferred_element_type=jnp.float32) + found
        found = jnp.dot(chosen, part0, preferred_element_type=jnp.float32) + found
        out_ref[block * LANES:(block + 1) * LANES] = found


def finish_kernel(cores, got_ref, items_ref, looked_ref, out_ref, residual_ref):
    residual_ref[...] = items_ref[...] - looked_ref[...]
    peers, parts = got_ref.shape[0], got_ref.shape[1] - 1
    for core in range(cores):
        summed = got_ref[core]
        for peer in range(core + cores, peers, cores):
            summed = summed + got_ref[peer]
        for b in range(parts):
            lane = (core * parts + b) * LANES
            out_ref[:, lane:lane + LANES] = summed[b] / summed[parts][b:b + 1]


def body(items, codewords, assign):
    f32 = jnp.float32
    n = lax.axis_size("code")
    nx, ny, nc = lax.axis_size("x"), lax.axis_size("y"), lax.axis_size("core")
    local_codes, width = codewords.shape
    own_rows = items.shape[0]
    half = local_codes // nc
    total_items = own_rows * nc * n * nx * ny
    core = lax.axis_index("core")
    z_info = jnp.stack([core, lax.axis_index("code") * local_codes]).astype(jnp.int32)

    own = lax.all_gather(items, "code", axis=0, tiled=True)
    scaled = jax.ShapeDtypeStruct((half, width), jnp.bfloat16)
    code_high, code_low = call(scale_kernel, (scaled, scaled), [SMEM, VMEM])(z_info, codewords)
    index_tile = assign.reshape(-1, LANES)
    named = call(lookup_kernel, jax.ShapeDtypeStruct((assign.shape[0], width), f32), [SMEM, VMEM, VMEM], grant=12)(
        z_info, index_tile, codewords
    )
    own, named, code_high, code_low = lax.optimization_barrier((own, named, code_high, code_low))
    looked = lax.psum_scatter(named, "code", scatter_dimension=0, tiled=True)
    other = lax.ppermute(own, "core", [(0, 1), (1, 0)])

    def chunk(group):
        rows = group.shape[0]
        parts = jax.ShapeDtypeStruct((rows, width), jnp.bfloat16)
        shapes = (
            jax.ShapeDtypeStruct((half, rows), f32),
            jax.ShapeDtypeStruct((half // LANES, LANES), f32),
            parts,
            parts,
        )
        return call(chunk_kernel, shapes, [VMEM] * 3)(code_high, code_low, group)

    chunks = [chunk(own), chunk(other)]
    blocks = [c[0] for c in chunks]
    count = len(blocks)
    col_tile = chunks[0][1] + chunks[1][1]

    row_shape = jax.ShapeDtypeStruct((nc * n, nc * n, LANES), f32)
    col_shape = jax.ShapeDtypeStruct((nx * ny,) + col_tile.shape, f32)
    operands = [SMEM, VMEM] + [VMEM] * count
    cols = jnp.broadcast_to(col_tile[None], col_shape.shape)
    for turn in range(ITERS):
        got = lax.all_to_all(cols, ("x", "y"), 0, 0)
        rows = call(row_kernel, row_shape, operands)(z_info, got, *blocks)
        got = lax.all_to_all(rows, ("core", "code"), 0, 0)
        if turn < ITERS - 1:
            cols = call(functools.partial(col_kernel, total_items), col_shape, operands)(z_info, got, *blocks)

    per_owner = width // (nx * ny * nc)
    tiles = ny * nc * (per_owner // SUB) * (half // LANES)
    numer = call(
        functools.partial(numer_kernel, total_items, count),
        jax.ShapeDtypeStruct((nx, tiles + 1, SUB, LANES), f32),
        operands + [VMEM] * (2 * count),
        grant=16,
    )(z_info, got, *blocks, *[c[2] for c in chunks], *[c[3] for c in chunks])
    got = lax.all_to_all(numer, "x", 0, 0)
    got, looked = lax.optimization_barrier((got, looked))
    peers = ny * nc
    packed = call(repack_kernel, jax.ShapeDtypeStruct((peers, tiles // peers + 1, SUB, LANES), f32), [VMEM])(got)
    got = lax.all_to_all(packed, ("y", "core"), 0, 0)
    shapes = (jax.ShapeDtypeStruct((per_owner, local_codes), f32), jax.ShapeDtypeStruct(items.shape, f32))
    turned, residual = call(functools.partial(finish_kernel, nc), shapes, [VMEM] * 3)(got, items, looked)
    new_codewords = turned.T
    return (new_codewords, residual)


def solution(mesh):
    cores = 2
    ny = 8
    dp, code = mesh.devices.shape
    fine = Mesh(
        mesh.devices.reshape(dp // (ny * cores), ny, cores, code),
        ("x", "y", "core", "code"),
    )
    in_specs = (P(DP + ("code",), None), P("code", None), P(DP))
    out_specs = (P("code", DP), P(DP + ("code",), None))
    return jax.shard_map(body, mesh=fine, in_specs=in_specs, out_specs=out_specs, check_vma=False)
```

time: 217 us -> 204 us (0.940)
  waiting for transfers between devices: 4.96 us -> 41.8 us
  starting transfers between devices: 39.9 us -> 6.71 us
  local copies, waits for them, and re-layouts: 18.4 us -> 3.92 us
  Pallas kernels: 24.7 us -> 20.5 us
  blocking collectives: 113 us -> 116 us
    all_gather x0 -> x1, waiting for transfers between devices: none -> 39.4 us  [body(): own = lax.all_gather(items, 'code', axis=0, tiled=True)]
    ppermute x9 -> x1, starting transfers between devices: 39.9 us -> 6.64 us  [body(): other = lax.ppermute(own, 'core', [(0, 1), (1, 0)])]
    unnamed x74 -> x12, local copies, waits for them, and re-layouts: 18.4 us -> 3.91 us
    all_to_all x1, blocking collectives: 12 us -> 17.8 us  [body(): got = lax.all_to_all(packed, ('y', 'core'), 0, 0)]
    pallas_call x16 -> x11, Pallas kernels: 23.9 us -> 19.6 us  [the longest x1 5.55 us: body(): call(lookup_kernel, jax.ShapeDtypeStruct((assign.shape[0], width), f32),...]
    ppermute x9 -> x1, waiting for transfers between devices: 4.95 us -> 1.68 us  [body(): other = lax.ppermute(own, 'core', [(0, 1), (1, 0)])]
    all_to_all x3, blocking collectives: 42.5 us -> 40.1 us  [body(): got = lax.all_to_all(rows, ('core', 'code'), 0, 0)]
  transfers between devices with their start and end apart: 10 -> 3, of which waited for: 5 -> 2; matrix products, arithmetic and copies ran while one was open for 0% -> 0% of each run, Pallas kernels for 10% -> 10%
where the time goes in v4:
time: 204 us; the launch traced here: 203 us
  blocking collectives  116 us (57%)
  waiting for transfers between devices  41.8 us (20%)
  Pallas kernels  20.5 us (10%)
  between operations  14.2 us (7%)
  starting transfers between devices  6.71 us (3%)
  local copies, waits for them, and re-layouts  3.92 us (2%)
    all_to_all x3, blocking collectives, body(): got = lax.all_to_all(cols, ('x', 'y'), 0, 0)  41.8 us
    all_to_all x3, blocking collectives, body(): got = lax.all_to_all(rows, ('core', 'code'), 0, 0)  40.1 us
    all_gather x1, waiting for transfers between devices, body(): own = lax.all_gather(items, 'code', axis=0, tiled=True)  39.4 us
    all_to_all x1, blocking collectives, body(): got = lax.all_to_all(packed, ('y', 'core'), 0, 0)  17.8 us
    all_to_all x1, blocking collectives, body(): got = lax.all_to_all(numer, 'x', 0, 0)  16.5 us
    ppermute x1, starting transfers between devices, body(): other = lax.ppermute(own, 'core', [(0, 1), (1, 0)])  6.64 us
    pallas_call x1, Pallas kernels, body(): call(lookup_kernel, jax.ShapeDtypeStruct((assign.shape[0], width), f32),...  5.55 us
    pallas_call x1, Pallas kernels, body(): call(functools.partial(numer_kernel, total_items, count), jax.ShapeDtypeS...  4.41 us
  transfers between devices with their start and end apart: 3, of which 2 were waited for; matrix products, arithmetic and copies ran while one was open for 0% of the time, Pallas kernels for 10%

profile of v4, /device:TPU:1, one launch (start us, length us, event | category | flops | bytes accessed | tf_op | source)
XLA Modules:
  0.0 203.4 jit_solution(15216732310748494602)
XLA Ops:
  7.2 0.0 all-gather.2.cloned.1.call-start
  7.2 0.7 all-gather.2.cloned.1.call-update
  7.9 0.0 reduce-scatter.2.cloned.1.call-start
  8.0 0.1 pad_add_fusion.z_ref
  8.0 1.6 copy-done
  9.6 0.8 shard_map.51
  10.5 0.7 copy-done.1
  11.2 5.6 %shard_map.50 = f32[1024,512]{1,0:T(8,128)} custom-call(s32[2]{0:T(128)S(1)} %pad_add_fusion.z_ref, s32[8,128]{1,0:T(8,128)S(1)} %bitcast.4, f32[1024,512]{1,0:T(8,128)S(1)} %copy-done.1), custom_call_target="tpu_custom_call" | custom-call | tf_op jit(solution)/shard_map/pallas_call | solution.py:224
  16.8 39.4 %all-gather.2.cloned.1.call-done.items_ref = f32[1024,512]{1,0:T(8,128)} async-done(((f32[128,512]{1,0:T(8,128)}), f32[1024,512]{1,0:T(8,128)}) %all-gather.2.cloned.1.call-update) | async-done | bytes 2097168 | tf_op jit(solution)/shard_map/all_gather | solution.py:220
  56.2 0.0 reduce-scatter.2.cloned.1.call-update
  56.2 1.6 copy-done.2
  57.8 6.6 %collective-permute-start = (f32[1024,512]{1,0:T(8,128)S(1)}, f32[1024,512]{1,0:T(8,128)S(1)}, u32[]{:S(2)}, u32[]{:S(2)}) collective-permute-start(f32[1024,512]{1,0:T(8,128)S(1)} %copy-done.2), channel_id=1, source_target_pairs={{0,8},{8,0},{1,9},{9,1},{2,10},{10,2},{3,11},{11,3},{4,12},{12,4},... | collective-permute-start | bytes 6291464 | tf_op jit(solution)/shard_map/ppermute | solution.py:229
  64.4 2.1 %shard_map.52 = (f32[512,1024]{1,0:T(8,128)S(1)}, f32[4,128]{1,0:T(4,128)S(1)}, bf16[1024,512]{1,0:T(8,128)(2,1)S(1)}, bf16[1024,512]{1,0:T(8,128)(2,1)S(1)}) custom-call(bf16[512,512]{1,0:T(8,128)(2,1)S(1)} %get-tuple-element.22.high_ref, bf16[512,512]{1,0:T(8,128)(2,1)S(1)} %get-tuple-element.23.low_ref, f32[1024,512]{1,0:T(8,128)S(1)} %copy-done.2), custom_call_target="tpu_custom_call" | custom-call | tf_op jit(solution)/shard_map/pallas_call | solution.py:240
  66.5 1.7 collective-permute-done.items_ref
  68.2 2.1 %shard_map.53 = (f32[512,1024]{1,0:T(8,128)S(1)}, f32[4,128]{1,0:T(4,128)S(1)}, bf16[1024,512]{1,0:T(8,128)(2,1)S(1)}, bf16[1024,512]{1,0:T(8,128)(2,1)S(1)}) custom-call(bf16[512,512]{1,0:T(8,128)(2,1)S(1)} %get-tuple-element.22.high_ref, bf16[512,512]{1,0:T(8,128)(2,1)S(1)} %get-tuple-element.23.low_ref, f32[1024,512]{1,0:T(8,128)S(1)} %collective-permute-done.items_ref), custom_call_target="tpu_custom_call" | custom-call | tf_op jit(solution)/shard_map/pallas_call | solution.py:240
  70.3 18.0 %all_to_all.40.got_ref = f32[32,4,128]{2,1,0:T(4,128)S(1)} all-to-all(f32[32,4,128]{2,1,0:T(4,128)S(1)} %broadcast_in_dim.2), channel_id=1, replica_groups=mesh['x'=4,'y'=8,'core'=2,'code'=8] {'x','y'}, dimensions={0} | all-to-all | bytes 131072 | tf_op jit(solution)/shard_map/all_to_all | solution.py:252
  88.3 1.0 shard_map.54
  89.3 14.6 %all_to_all.41.got_ref = f32[16,16,128]{2,1,0:T(8,128)S(1)} all-to-all(f32[16,16,128]{2,1,0:T(8,128)S(1)} %shard_map.54), channel_id=1, replica_groups=mesh['x'=4,'y'=8,'core'=2,'code'=8] {'core','code'}, dimensions={0} | all-to-all | bytes 262144 | tf_op jit(solution)/shard_map/all_to_all | solution.py:254
  103.9 0.9 shard_map.55
  104.8 11.9 %all_to_all.42.got_ref = f32[32,4,128]{2,1,0:T(4,128)S(1)} all-to-all(f32[32,4,128]{2,1,0:T(4,128)S(1)} %shard_map.55), channel_id=1, replica_groups=mesh['x'=4,'y'=8,'core'=2,'code'=8] {'x','y'}, dimensions={0} | all-to-all | bytes 131072 | tf_op jit(solution)/shard_map/all_to_all | solution.py:252
  116.8 1.0 shard_map.56
  117.7 12.6 %all_to_all.43.got_ref = f32[16,16,128]{2,1,0:T(8,128)S(1)} all-to-all(f32[16,16,128]{2,1,0:T(8,128)S(1)} %shard_map.56), channel_id=1, replica_groups=mesh['x'=4,'y'=8,'core'=2,'code'=8] {'core','code'}, dimensions={0} | all-to-all | bytes 262144 | tf_op jit(solution)/shard_map/all_to_all | solution.py:254
  130.4 0.9 shard_map.57
  131.3 11.9 %all_to_all.44.got_ref = f32[32,4,128]{2,1,0:T(4,128)S(1)} all-to-all(f32[32,4,128]{2,1,0:T(4,128)S(1)} %shard_map.57), channel_id=1, replica_groups=mesh['x'=4,'y'=8,'core'=2,'code'=8] {'x','y'}, dimensions={0} | all-to-all | bytes 131072 | tf_op jit(solution)/shard_map/all_to_all | solution.py:252
  143.2 1.0 shard_map.58
  144.2 12.9 %all_to_all.45.got_ref = f32[16,16,128]{2,1,0:T(8,128)S(1)} all-to-all(f32[16,16,128]{2,1,0:T(8,128)S(1)} %shard_map.58), channel_id=1, replica_groups=mesh['x'=4,'y'=8,'core'=2,'code'=8] {'core','code'}, dimensions={0} | all-to-all | bytes 262144 | tf_op jit(solution)/shard_map/all_to_all | solution.py:254
  157.0 4.4 %shard_map.59 = f32[4,65,8,128]{3,2,1,0:T(8,128)S(1)} custom-call(s32[2]{0:T(128)S(1)} %pad_add_fusion.z_ref, f32[16,16,128]{2,1,0:T(8,128)S(1)} %all_to_all.45.got_ref, f32[512,1024]{1,0:T(8,128)S(1)} %get-tuple-element.27.refs_0_, f32[512,1024]{1,0:T(8,128)S(1)} %get-tuple-element.28.refs_1_, bf16[1024,512]{1,0:T(8,128)(2,1)S(1)} %get-tuple-element.29.refs_2_, ...), custom_call_target="tpu_custom_call" | custom-call | tf_op jit(solution)/shard_map/pallas_call | solution.py:260
  161.4 0.0 copy-start.3
  161.4 16.5 %all_to_all.46.got_ref = f32[4,65,8,128]{3,2,1,0:T(8,128)S(1)} all-to-all(f32[4,65,8,128]{3,2,1,0:T(8,128)S(1)} %shard_map.59), channel_id=1, replica_groups=mesh['x'=4,'y'=8,'core'=2,'code'=8] {'x'}, dimensions={0} | all-to-all | bytes 2129920 | tf_op jit(solution)/shard_map/all_to_all | solution.py:266
  178.0 0.1 shard_map.60
  178.0 17.8 %all_to_all.47.got_ref = f32[16,5,8,128]{3,2,1,0:T(8,128)S(1)} all-to-all(f32[16,5,8,128]{3,2,1,0:T(8,128)S(1)} %shard_map.60), channel_id=1, replica_groups=mesh['x'=4,'y'=8,'core'=2,'code'=8] {'y','core'}, dimensions={0} | all-to-all | bytes 655360 | tf_op jit(solution)/shard_map/all_to_all | solution.py:270
  195.8 0.7 shard_map.61
  (11 shorter events, 0.0 us)
Async XLA Ops:
  7.2 3.3 %copy-start.5 = (s32[1024]{0:T(1024)S(1)}, s32[1024]{0:T(1024)}, u32[]{:S(2)}) copy-start(s32[1024]{0:T(1024)} %param.5) | copy-start | bytes 12292
  7.2 49.0 %all-gather.2.cloned.1.call-start = ((), (), s32[]{:S(2)}) async-start(), calls=%async_computation.9 | async-start | bytes 2359296 | tf_op jit(solution)/shard_map/all_gather | solution.py:220
  7.9 170.1 %reduce-scatter.2.cloned.1.call-start = ((), (), s32[]{:S(2)}) async-start(), calls=%async_computation.10 | async-start | bytes 2359296 | tf_op jit(solution)/shard_map/reduce_scatter | solution.py:228
  8.0 1.6 copy-start
  9.6 1.6 copy-start.1
  56.2 1.6 copy-start.2
  57.8 10.4 %collective-permute-start = (f32[1024,512]{1,0:T(8,128)S(1)}, f32[1024,512]{1,0:T(8,128)S(1)}, u32[]{:S(2)}, u32[]{:S(2)}) collective-permute-start(f32[1024,512]{1,0:T(8,128)S(1)} %copy-done.2), channel_id=1, source_target_pairs={{0,8},{8,0},{1,9},{9,1},{2,10},{10,2},{3,11},{11,3},{4,12},{12,4},... | collective-permute-start | bytes 6291464 | tf_op jit(solution)/shard_map/ppermute | solution.py:229
  161.4 34.4 %copy-start.3 = (f32[128,512]{1,0:T(8,128)S(1)}, f32[128,512]{1,0:T(8,128)}, u32[]{:S(2)}) copy-start(f32[128,512]{1,0:T(8,128)} %items_ref.1) | copy-start | bytes 786436
  178.0 17.9 %copy-start.4 = (f32[128,512]{1,0:T(8,128)S(1)}, f32[128,512]{1,0:T(8,128)}, u32[]{:S(2)}) copy-start(f32[128,512]{1,0:T(8,128)} %reduce-scatter.2.cloned.1.call-done.looked_ref) | copy-start | bytes 786436
Sparse Core Ops, SparseCore 0:
  10.1 46.0 all-gather.1
  59.0 45.9 reduce-scatter.1

commit v5 on v4

--- a/solution.py
+++ b/solution.py
@@ -72,17 +72,22 @@
             out_ref[start:start + step, first:first + step] = values
             for lane in range(0, step, LANES):
                 folded[k] = folded[k] + values[:, lane:lane + LANES]
-    for k, total in enumerate(folded):
-        for part in range(step // LANES):
-            row = k * (step // LANES) + part
-            sums_ref[row:row + 1] = lane_sums(total[part * LANES:(part + 1) * LANES])
+    rows = [lane_sums(total[at:at + LANES]) for total in folded for at in range(0, step, LANES)]
+
+    @pl.when(pl.program_id(0) == 0)
+    def _():
+        sums_ref[...] = jnp.concatenate(rows, axis=0)
+
+    @pl.when(pl.program_id(0) > 0)
+    def _():
+        sums_ref[...] += jnp.concatenate(rows, axis=0)
 
 
 def load_blocks(refs):
     return [(ref, j * LANES) for ref in refs for j in range(ref.shape[1] // LANES)]
 
 
-def row_kernel(z_ref, got_ref, *refs):
+def row_kernel(got_ref, *refs):
     blocks, out_ref = load_blocks(refs[:-1]), refs[-1]
     scale = 1.0 / (K * jnp.sum(got_ref[...], axis=0))
     totals = [jnp.zeros((SUB, LANES), jnp.float32) for _ in blocks]
@@ -92,26 +97,19 @@
             product = ref[b * LANES:(b + 1) * LANES, lane:lane + LANES] * column
             totals[j] = totals[j] + jnp.sum(product.reshape(LANES // SUB, SUB, LANES), axis=0)
     sums = [jnp.sum(total, axis=0, keepdims=True) for total in totals]
-    group = len(sums) // 2
-    own, other = jnp.concatenate(sums[:group], axis=0), jnp.concatenate(sums[group:], axis=0)
-    first = z_ref[0] == 0
-    tile = jnp.concatenate([jnp.where(first, own, other), jnp.where(first, other, own)], axis=0)
+    tile = jnp.concatenate(sums, axis=0)
     for peer in range(out_ref.shape[0]):
         out_ref[peer] = tile
 
 
-def row_scales(total_items, z_ref, got_ref):
+def row_scales(total_items, got_ref):
     scale = 1.0 / (total_items * jnp.sum(got_ref[...], axis=0))
-    group = scale.shape[0] // 2
-    first = z_ref[0] == 0
-    own, other = scale[:group], scale[group:]
-    tiles = jnp.where(first, own, other), jnp.where(first, other, own)
-    return [tile[row:row + 1] for tile in tiles for row in range(group)]
-
-
-def col_kernel(total_items, z_ref, got_ref, *refs):
+    return [scale[row:row + 1] for row in range(scale.shape[0])]
+
+
+def col_kernel(total_items, got_ref, *refs):
     blocks, out_ref = load_blocks(refs[:-1]), refs[-1]
-    scales = row_scales(total_items, z_ref, got_ref)
+    scales = row_scales(total_items, got_ref)
     rows = []
     for b in range(out_ref.shape[1]):
         folded = jnp.zeros((LANES, LANES), jnp.float32)
@@ -123,9 +121,9 @@
         out_ref[peer] = tile
 
 
-def numer_kernel(total_items, count, z_ref, got_ref, *refs):
+def numer_kernel(total_items, count, got_ref, *refs):
     high_refs, low_refs, out_ref = refs[count:2 * count], refs[2 * count:3 * count], refs[3 * count]
-    scales = row_scales(total_items, z_ref, got_ref)
+    scales = row_scales(total_items, got_ref)
     codes, width = refs[0].shape[0], high_refs[0].shape[1]
     nx = out_ref.shape[0]
     parts = codes // LANES
@@ -217,43 +215,51 @@
     core = lax.axis_index("core")
     z_info = jnp.stack([core, lax.axis_index("code") * local_codes]).astype(jnp.int32)
 
-    own = lax.all_gather(items, "code", axis=0, tiled=True)
+    gathered = lax.all_gather(items, ("core", "code"), axis=0, tiled=True)
     scaled = jax.ShapeDtypeStruct((half, width), jnp.bfloat16)
     code_high, code_low = call(scale_kernel, (scaled, scaled), [SMEM, VMEM])(z_info, codewords)
     index_tile = assign.reshape(-1, LANES)
     named = call(lookup_kernel, jax.ShapeDtypeStruct((assign.shape[0], width), f32), [SMEM, VMEM, VMEM], grant=12)(
         z_info, index_tile, codewords
     )
-    own, named, code_high, code_low = lax.optimization_barrier((own, named, code_high, code_low))
+    gathered, named, code_high, code_low = lax.optimization_barrier((gathered, named, code_high, code_low))
     looked = lax.psum_scatter(named, "code", scatter_dimension=0, tiled=True)
-    other = lax.ppermute(own, "core", [(0, 1), (1, 0)])
-
-    def chunk(group):
-        rows = group.shape[0]
-        parts = jax.ShapeDtypeStruct((rows, width), jnp.bfloat16)
-        shapes = (
-            jax.ShapeDtypeStruct((half, rows), f32),
+    group, block = gathered.shape[0], 256
+    part = jax.ShapeDtypeStruct((group, width), jnp.bfloat16)
+    kernel_vals, col_tile, item_high, item_low = pl.pallas_call(
+        chunk_kernel,
+        grid=(group // block,),
+        out_shape=(
+            jax.ShapeDtypeStruct((half, group), f32),
             jax.ShapeDtypeStruct((half // LANES, LANES), f32),
-            parts,
-            parts,
-        )
-        return call(chunk_kernel, shapes, [VMEM] * 3)(code_high, code_low, group)
-
-    chunks = [chunk(own), chunk(other)]
-    blocks = [c[0] for c in chunks]
-    count = len(blocks)
-    col_tile = chunks[0][1] + chunks[1][1]
+            part,
+            part,
+        ),
+        in_specs=[
+            pl.BlockSpec((half, width), lambda i: (0, 0)),
+            pl.BlockSpec((half, width), lambda i: (0, 0)),
+            pl.BlockSpec((block, width), lambda i: (i, 0)),
+        ],
+        out_specs=(
+            pl.BlockSpec((half, block), lambda i: (0, i)),
+            pl.BlockSpec((half // LANES, LANES), lambda i: (0, 0)),
+            pl.BlockSpec((block, width), lambda i: (i, 0)),
+            pl.BlockSpec((block, width), lambda i: (i, 0)),
+        ),
+        compiler_params=pltpu.CompilerParams(vmem_limit_bytes=16 * MIB),
+    )(code_high, code_low, pltpu.with_memory_space_constraint(gathered, pltpu.HBM))
+    blocks, count = [kernel_vals], 1
 
     row_shape = jax.ShapeDtypeStruct((nc * n, nc * n, LANES), f32)
     col_shape = jax.ShapeDtypeStruct((nx * ny,) + col_tile.shape, f32)
-    operands = [SMEM, VMEM] + [VMEM] * count
+    operands = [VMEM] * (1 + count)
     cols = jnp.broadcast_to(col_tile[None], col_shape.shape)
     for turn in range(ITERS):
         got = lax.all_to_all(cols, ("x", "y"), 0, 0)
-        rows = call(row_kernel, row_shape, operands)(z_info, got, *blocks)
+        rows = call(row_kernel, row_shape, operands)(got, *blocks)
         got = lax.all_to_all(rows, ("core", "code"), 0, 0)
         if turn < ITERS - 1:
-            cols = call(functools.partial(col_kernel, total_items), col_shape, operands)(z_info, got, *blocks)
+            cols = call(functools.partial(col_kernel, total_items), col_shape, operands)(got, *blocks)
 
     per_owner = width // (nx * ny * nc)
     tiles = ny * nc * (per_owner // SUB) * (half // LANES)
@@ -262,7 +268,7 @@
         jax.ShapeDtypeStruct((nx, tiles + 1, SUB, LANES), f32),
         operands + [VMEM] * (2 * count),
         grant=16,
-    )(z_info, got, *blocks, *[c[2] for c in chunks], *[c[3] for c in chunks])
+    )(got, *blocks, item_high, item_low)
     got = lax.all_to_all(numer, "x", 0, 0)
     got, looked = lax.optimization_barrier((got, looked))
     peers = ny * nc

time: 204 us -> 201 us (0.985)
  starting transfers between devices: 6.71 us -> 0.08 us
  waiting for transfers between devices: 41.8 us -> 45.7 us
    ppermute x1 -> x0, starting transfers between devices: 6.64 us -> none  [body(): other = lax.ppermute(own, 'core', [(0, 1), (1, 0)])]
    all_gather x1, waiting for transfers between devices: 39.4 us -> 45 us  [body(): gathered = lax.all_gather(items, ('core', 'code'), axis=0, tiled=True)]
    pallas_call x5 -> x4, Pallas kernels: 7.04 us -> 9.97 us  [the longest x1 8.72 us: body(): pl.pallas_call(chunk_kernel, grid=(group // block,), out_shape=(jax.Shape...]
  transfers between devices with their start and end apart: 3 -> 2, of which waited for: 2 -> 1; matrix products, arithmetic and copies ran while one was open for 0% -> 0% of each run, Pallas kernels for 10% -> 10%
where the time goes in v5:
time: 201 us; the launch traced here: 200 us
  blocking collectives  116 us (58%)
  waiting for transfers between devices  45.7 us (23%)
  Pallas kernels  21.6 us (11%)
  between operations  14.1 us (7%)
  local copies, waits for them, and re-layouts  2.35 us (1%)
    all_gather x1, waiting for transfers between devices, body(): gathered = lax.all_gather(items, ('core', 'code'), axis=0, tiled=True)  45 us
    all_to_all x3, blocking collectives, body(): got = lax.all_to_all(cols, ('x', 'y'), 0, 0)  41.8 us
    all_to_all x3, blocking collectives, body(): got = lax.all_to_all(rows, ('core', 'code'), 0, 0)  40 us
    all_to_all x1, blocking collectives, body(): got = lax.all_to_all(packed, ('y', 'core'), 0, 0)  17.8 us
    all_to_all x1, blocking collectives, body(): got = lax.all_to_all(numer, 'x', 0, 0)  16.5 us
    pallas_call x1, Pallas kernels, body(): pl.pallas_call(chunk_kernel, grid=(group // block,), out_shape=(jax.Shape...  8.72 us
    pallas_call x1, Pallas kernels, body(): call(lookup_kernel, jax.ShapeDtypeStruct((assign.shape[0], width), f32),...  5.56 us
  transfers between devices with their start and end apart: 2, of which 1 were waited for; matrix products, arithmetic and copies ran while one was open for 0% of the time, Pallas kernels for 10%

profile of v5, /device:TPU:1, one launch (start us, length us, event | category | flops | bytes accessed | tf_op | source)
XLA Modules:
  0.0 200.1 jit_solution(13153504569791379129)
XLA Ops:
  7.2 0.0 copy-start.4
  7.2 0.0 all-gather.2.cloned.1.call-start
  7.2 0.7 all-gather.2.cloned.1.call-update
  7.9 0.0 reduce-scatter.2.cloned.1.call-start
  8.0 0.1 pad_add_fusion.z_ref
  8.0 1.6 copy-done
  9.6 0.8 shard_map.51
  10.5 0.0 copy-done.4
  10.5 0.7 copy-done.1
  11.2 5.6 %shard_map.50 = f32[1024,512]{1,0:T(8,128)} custom-call(s32[2]{0:T(128)S(1)} %pad_add_fusion.z_ref, s32[8,128]{1,0:T(8,128)S(1)} %bitcast.4, f32[1024,512]{1,0:T(8,128)S(1)} %copy-done.1), custom_call_target="tpu_custom_call" | custom-call | tf_op jit(solution)/shard_map/pallas_call | solution.py:222
  16.8 45.0 %all-gather.2.cloned.1.call-done.items_ref = f32[2048,512]{1,0:T(8,128)} async-done(((f32[128,512]{1,0:T(8,128)}), f32[2048,512]{1,0:T(8,128)}) %all-gather.2.cloned.1.call-update) | async-done | bytes 4194320 | tf_op jit(solution)/shard_map/all_gather | solution.py:218
  61.7 0.0 reduce-scatter.2.cloned.1.call-update
  61.8 8.7 %shard_map.52 = (f32[512,2048]{1,0:T(8,128)S(1)}, f32[4,128]{1,0:T(4,128)S(1)}, bf16[2048,512]{1,0:T(8,128)(2,1)S(1)}, bf16[2048,512]{1,0:T(8,128)(2,1)S(1)}) custom-call(bf16[512,512]{1,0:T(8,128)(2,1)S(1)} %get-tuple-element.18.high_ref, bf16[512,512]{1,0:T(8,128)(2,1)S(1)} %get-tuple-element.19.low_ref, f32[2048,512]{1,0:T(8,128)} %all-gather.2.cloned.1.call-done.items_ref), custom_call_target="tpu_custom_call" | custom-call | tf_op jit(solution)/shard_map/pallas_call | solution.py:229
  70.5 18.0 %all_to_all.40.got_ref = f32[32,4,128]{2,1,0:T(4,128)S(1)} all-to-all(f32[32,4,128]{2,1,0:T(4,128)S(1)} %broadcast_in_dim.2), channel_id=1, replica_groups=mesh['x'=4,'y'=8,'core'=2,'code'=8] {'x','y'}, dimensions={0} | all-to-all | bytes 131072 | tf_op jit(solution)/shard_map/all_to_all | solution.py:258
  88.5 0.4 shard_map.53
  88.9 14.3 %all_to_all.41.got_ref = f32[16,16,128]{2,1,0:T(8,128)S(1)} all-to-all(f32[16,16,128]{2,1,0:T(8,128)S(1)} %shard_map.53), channel_id=1, replica_groups=mesh['x'=4,'y'=8,'core'=2,'code'=8] {'core','code'}, dimensions={0} | all-to-all | bytes 262144 | tf_op jit(solution)/shard_map/all_to_all | solution.py:260
  103.2 0.4 shard_map.54
  103.6 12.0 %all_to_all.42.got_ref = f32[32,4,128]{2,1,0:T(4,128)S(1)} all-to-all(f32[32,4,128]{2,1,0:T(4,128)S(1)} %shard_map.54), channel_id=1, replica_groups=mesh['x'=4,'y'=8,'core'=2,'code'=8] {'x','y'}, dimensions={0} | all-to-all | bytes 131072 | tf_op jit(solution)/shard_map/all_to_all | solution.py:258
  115.6 0.4 shard_map.55
  116.0 12.8 %all_to_all.43.got_ref = f32[16,16,128]{2,1,0:T(8,128)S(1)} all-to-all(f32[16,16,128]{2,1,0:T(8,128)S(1)} %shard_map.55), channel_id=1, replica_groups=mesh['x'=4,'y'=8,'core'=2,'code'=8] {'core','code'}, dimensions={0} | all-to-all | bytes 262144 | tf_op jit(solution)/shard_map/all_to_all | solution.py:260
  128.8 0.4 shard_map.56
  129.2 11.9 %all_to_all.44.got_ref = f32[32,4,128]{2,1,0:T(4,128)S(1)} all-to-all(f32[32,4,128]{2,1,0:T(4,128)S(1)} %shard_map.56), channel_id=1, replica_groups=mesh['x'=4,'y'=8,'core'=2,'code'=8] {'x','y'}, dimensions={0} | all-to-all | bytes 131072 | tf_op jit(solution)/shard_map/all_to_all | solution.py:258
  141.1 0.4 shard_map.57
  141.5 12.9 %all_to_all.45.got_ref = f32[16,16,128]{2,1,0:T(8,128)S(1)} all-to-all(f32[16,16,128]{2,1,0:T(8,128)S(1)} %shard_map.57), channel_id=1, replica_groups=mesh['x'=4,'y'=8,'core'=2,'code'=8] {'core','code'}, dimensions={0} | all-to-all | bytes 262144 | tf_op jit(solution)/shard_map/all_to_all | solution.py:260
  154.4 3.7 %shard_map.58 = f32[4,65,8,128]{3,2,1,0:T(8,128)S(1)} custom-call(f32[16,16,128]{2,1,0:T(8,128)S(1)} %all_to_all.45.got_ref, f32[512,2048]{1,0:T(8,128)S(1)} %get-tuple-element.22.refs_0_, bf16[2048,512]{1,0:T(8,128)(2,1)S(1)} %get-tuple-element.23.refs_1_, bf16[2048,512]{1,0:T(8,128)(2,1)S(1)} %get-tuple-element.24.refs_2_), custom_call_target="tpu_custom_call" | custom-call | tf_op jit(solution)/shard_map/pallas_call | solution.py:266
  158.1 0.0 copy-start.2
  158.1 16.5 %all_to_all.46.got_ref = f32[4,65,8,128]{3,2,1,0:T(8,128)S(1)} all-to-all(f32[4,65,8,128]{3,2,1,0:T(8,128)S(1)} %shard_map.58), channel_id=1, replica_groups=mesh['x'=4,'y'=8,'core'=2,'code'=8] {'x'}, dimensions={0} | all-to-all | bytes 2129920 | tf_op jit(solution)/shard_map/all_to_all | solution.py:272
  174.6 0.1 shard_map.59
  174.7 17.8 %all_to_all.47.got_ref = f32[16,5,8,128]{3,2,1,0:T(8,128)S(1)} all-to-all(f32[16,5,8,128]{3,2,1,0:T(8,128)S(1)} %shard_map.59), channel_id=1, replica_groups=mesh['x'=4,'y'=8,'core'=2,'code'=8] {'y','core'}, dimensions={0} | all-to-all | bytes 655360 | tf_op jit(solution)/shard_map/all_to_all | solution.py:276
  192.5 0.0 copy-done.2
  192.5 0.0 copy-done.3
  192.5 0.7 shard_map.60
  (5 shorter events, 0.0 us)
Async XLA Ops:
  7.2 3.3 %copy-start.4 = (s32[1024]{0:T(1024)S(1)}, s32[1024]{0:T(1024)}, u32[]{:S(2)}) copy-start(s32[1024]{0:T(1024)} %param.5) | copy-start | bytes 12292
  7.2 54.6 %all-gather.2.cloned.1.call-start = ((), (), s32[]{:S(2)}) async-start(), calls=%async_computation.9 | async-start | bytes 4456448 | tf_op jit(solution)/shard_map/all_gather | solution.py:218
  7.9 166.7 %reduce-scatter.2.cloned.1.call-start = ((), (), s32[]{:S(2)}) async-start(), calls=%async_computation.10 | async-start | bytes 2359296 | tf_op jit(solution)/shard_map/reduce_scatter | solution.py:226
  8.0 1.6 copy-start
  9.6 1.6 copy-start.1
  158.1 34.4 %copy-start.2 = (f32[128,512]{1,0:T(8,128)S(1)}, f32[128,512]{1,0:T(8,128)}, u32[]{:S(2)}) copy-start(f32[128,512]{1,0:T(8,128)} %items_ref.1) | copy-start | bytes 786436
  174.6 17.9 %copy-start.3 = (f32[128,512]{1,0:T(8,128)S(1)}, f32[128,512]{1,0:T(8,128)}, u32[]{:S(2)}) copy-start(f32[128,512]{1,0:T(8,128)} %reduce-scatter.2.cloned.1.call-done.looked_ref) | copy-start | bytes 786436
Sparse Core Ops, SparseCore 0:
  10.1 51.5 all-gather.1
  64.6 41.8 reduce-scatter.1

commit v6 on v5

--- a/solution.py
+++ b/solution.py
@@ -9,7 +9,7 @@
 
 K = 8192
 ITERS = 3
-DP = ("x", "y", "core")
+DP = ("x", "yh", "yl", "core")
 LANES = 128
 SUB = 8
 
@@ -57,11 +57,19 @@
     low_ref[...] = low
 
 
-def chunk_kernel(high_ref, low_ref, items_ref, out_ref, sums_ref, xh_ref, xl_ref):
+def chunk_kernel(high_ref, low_ref, items_ref, out_ref, sums_ref, xh_ref, xl_ref, held_ref, sems):
     codes, step = high_ref.shape[0], 256
+    starts = range(0, items_ref.shape[0], step)
+    copies = [
+        pltpu.make_async_copy(items_ref.at[pl.ds(first, step)], held_ref.at[pl.ds(first, step)], sems.at[i])
+        for i, first in enumerate(starts)
+    ]
+    for copy in copies:
+        copy.start()
     folded = [jnp.zeros((step, LANES), jnp.float32) for _ in range(0, codes, step)]
-    for first in range(0, items_ref.shape[0], step):
-        values = items_ref[first:first + step]
+    for copy, first in zip(copies, starts):
+        copy.wait()
+        values = held_ref[first:first + step]
         xh_ref[first:first + step], xl_ref[first:first + step] = split(values)
         item_high, item_low = split(unit_rows(values))
         for k, start in enumerate(range(0, codes, step)):
@@ -72,15 +80,10 @@
             out_ref[start:start + step, first:first + step] = values
             for lane in range(0, step, LANES):
                 folded[k] = folded[k] + values[:, lane:lane + LANES]
-    rows = [lane_sums(total[at:at + LANES]) for total in folded for at in range(0, step, LANES)]
-
-    @pl.when(pl.program_id(0) == 0)
-    def _():
-        sums_ref[...] = jnp.concatenate(rows, axis=0)
-
-    @pl.when(pl.program_id(0) > 0)
-    def _():
-        sums_ref[...] += jnp.concatenate(rows, axis=0)
+    for k, total in enumerate(folded):
+        for part in range(step // LANES):
+            row = k * (step // LANES) + part
+            sums_ref[row:row + 1] = lane_sums(total[part * LANES:(part + 1) * LANES])
 
 
 def load_blocks(refs):
@@ -121,12 +124,12 @@
         out_ref[peer] = tile
 
 
-def numer_kernel(total_items, count, got_ref, *refs):
+def numer_kernel(total_items, count, nx, near, cores, got_ref, *refs):
     high_refs, low_refs, out_ref = refs[count:2 * count], refs[2 * count:3 * count], refs[3 * count]
     scales = row_scales(total_items, got_ref)
     codes, width = refs[0].shape[0], high_refs[0].shape[1]
-    nx = out_ref.shape[0]
     parts = codes // LANES
+    per_x = width // (nx * SUB)
     step = 256
     mass = []
     for start in range(0, codes, step):
@@ -151,15 +154,16 @@
         for part in range(step // LANES):
             mass.append(lane_sums(folded[part * LANES:(part + 1) * LANES]))
             col = start // LANES + part
-            for x in range(nx):
-                for lane in range(x * width // nx, (x + 1) * width // nx, LANES):
-                    turned = sums[part * LANES:(part + 1) * LANES, lane:lane + LANES].T
-                    for group in range(LANES // SUB):
-                        row = (lane - x * width // nx) // SUB + group
-                        out_ref[x, row * parts + col] = turned[group * SUB:(group + 1) * SUB]
+            for lane in range(0, width, LANES):
+                turned = sums[part * LANES:(part + 1) * LANES, lane:lane + LANES].T
+                for group in range(LANES // SUB):
+                    x, rest = divmod(lane // SUB + group, per_x)
+                    y, core = divmod(rest, cores)
+                    row = (y // near) * cores + core
+                    out_ref[x * near + y % near, row * parts + col] = turned[group * SUB:(group + 1) * SUB]
     tile = jnp.concatenate(mass + [jnp.ones((SUB - parts, LANES), jnp.float32)], axis=0)
-    for x in range(nx):
-        out_ref[x, out_ref.shape[1] - 1] = tile
+    for peer in range(out_ref.shape[0]):
+        out_ref[peer, out_ref.shape[1] - 1] = tile
 
 
 def repack_kernel(got_ref, out_ref):
@@ -207,7 +211,9 @@
 def body(items, codewords, assign):
     f32 = jnp.float32
     n = lax.axis_size("code")
-    nx, ny, nc = lax.axis_size("x"), lax.axis_size("y"), lax.axis_size("core")
+    nx, nc = lax.axis_size("x"), lax.axis_size("core")
+    high, low = lax.axis_size("yh"), lax.axis_size("yl")
+    ny = high * low
     local_codes, width = codewords.shape
     own_rows = items.shape[0]
     half = local_codes // nc
@@ -224,29 +230,19 @@
     )
     gathered, named, code_high, code_low = lax.optimization_barrier((gathered, named, code_high, code_low))
     looked = lax.psum_scatter(named, "code", scatter_dimension=0, tiled=True)
-    group, block = gathered.shape[0], 256
+    group = gathered.shape[0]
     part = jax.ShapeDtypeStruct((group, width), jnp.bfloat16)
-    kernel_vals, col_tile, item_high, item_low = pl.pallas_call(
+    kernel_vals, col_tile, item_high, item_low = call(
         chunk_kernel,
-        grid=(group // block,),
-        out_shape=(
+        (
             jax.ShapeDtypeStruct((half, group), f32),
             jax.ShapeDtypeStruct((half // LANES, LANES), f32),
             part,
             part,
         ),
-        in_specs=[
-            pl.BlockSpec((half, width), lambda i: (0, 0)),
-            pl.BlockSpec((half, width), lambda i: (0, 0)),
-            pl.BlockSpec((block, width), lambda i: (i, 0)),
-        ],
-        out_specs=(
-            pl.BlockSpec((half, block), lambda i: (0, i)),
-            pl.BlockSpec((half // LANES, LANES), lambda i: (0, 0)),
-            pl.BlockSpec((block, width), lambda i: (i, 0)),
-            pl.BlockSpec((block, width), lambda i: (i, 0)),
-        ),
-        compiler_params=pltpu.CompilerParams(vmem_limit_bytes=16 * MIB),
+        [VMEM, VMEM, pl.BlockSpec(memory_space=pl.ANY)],
+        [pltpu.VMEM((group, width), f32), pltpu.SemaphoreType.DMA((group // 256,))],
+        grant=16,
     )(code_high, code_low, pltpu.with_memory_space_constraint(gathered, pltpu.HBM))
     blocks, count = [kernel_vals], 1
 
@@ -255,25 +251,25 @@
     operands = [VMEM] * (1 + count)
     cols = jnp.broadcast_to(col_tile[None], col_shape.shape)
     for turn in range(ITERS):
-        got = lax.all_to_all(cols, ("x", "y"), 0, 0)
+        got = lax.all_to_all(cols, ("x", "yh", "yl"), 0, 0)
         rows = call(row_kernel, row_shape, operands)(got, *blocks)
         got = lax.all_to_all(rows, ("core", "code"), 0, 0)
         if turn < ITERS - 1:
             cols = call(functools.partial(col_kernel, total_items), col_shape, operands)(got, *blocks)
 
     per_owner = width // (nx * ny * nc)
-    tiles = ny * nc * (per_owner // SUB) * (half // LANES)
+    tiles = high * nc * (per_owner // SUB) * (half // LANES)
     numer = call(
-        functools.partial(numer_kernel, total_items, count),
-        jax.ShapeDtypeStruct((nx, tiles + 1, SUB, LANES), f32),
+        functools.partial(numer_kernel, total_items, count, nx, low, nc),
+        jax.ShapeDtypeStruct((nx * low, tiles + 1, SUB, LANES), f32),
         operands + [VMEM] * (2 * count),
         grant=16,
     )(got, *blocks, item_high, item_low)
-    got = lax.all_to_all(numer, "x", 0, 0)
+    got = lax.all_to_all(numer, ("x", "yl"), 0, 0)
     got, looked = lax.optimization_barrier((got, looked))
-    peers = ny * nc
+    peers = high * nc
     packed = call(repack_kernel, jax.ShapeDtypeStruct((peers, tiles // peers + 1, SUB, LANES), f32), [VMEM])(got)
-    got = lax.all_to_all(packed, ("y", "core"), 0, 0)
+    got = lax.all_to_all(packed, ("yh", "core"), 0, 0)
     shapes = (jax.ShapeDtypeStruct((per_owner, local_codes), f32), jax.ShapeDtypeStruct(items.shape, f32))
     turned, residual = call(functools.partial(finish_kernel, nc), shapes, [VMEM] * 3)(got, items, looked)
     new_codewords = turned.T
@@ -282,11 +278,11 @@
 
 def solution(mesh):
     cores = 2
-    ny = 8
+    high, low = 4, 2
     dp, code = mesh.devices.shape
     fine = Mesh(
-        mesh.devices.reshape(dp // (ny * cores), ny, cores, code),
-        ("x", "y", "core", "code"),
+        mesh.devices.reshape(dp // (high * low * cores), high, low, cores, code),
+        ("x", "yh", "yl", "core", "code"),
     )
     in_specs = (P(DP + ("code",), None), P("code", None), P(DP))
     out_specs = (P("code", DP), P(DP + ("code",), None))

time: 201 us -> 196 us (0.975)
  blocking collectives: 116 us -> 112 us
    all_to_all x5, blocking collectives: 76.1 us -> 72.2 us  [the longest x3 41.7 us: body(): got = lax.all_to_all(cols, ('x', 'yh', 'yl'), 0, 0)]
where the time goes in v6:
time: 196 us
  blocking collectives  112 us (57%)
  waiting for transfers between devices  45.7 us (23%)
  Pallas kernels  20 us (10%)
  between operations  14.1 us (7%)
  local copies, waits for them, and re-layouts  3.3 us (2%)
    all_gather x1, waiting for transfers between devices, body(): gathered = lax.all_gather(items, ('core', 'code'), axis=0, tiled=True)  45 us
    all_to_all x3, blocking collectives, body(): got = lax.all_to_all(cols, ('x', 'yh', 'yl'), 0, 0)  41.7 us
    all_to_all x3, blocking collectives, body(): got = lax.all_to_all(rows, ('core', 'code'), 0, 0)  40.2 us
    all_to_all x1, blocking collectives, body(): got = lax.all_to_all(numer, ('x', 'yl'), 0, 0)  17.1 us
    all_to_all x1, blocking collectives, body(): got = lax.all_to_all(packed, ('yh', 'core'), 0, 0)  13.5 us
    pallas_call x1, Pallas kernels, body(): call(chunk_kernel, (jax.ShapeDtypeStruct((half, group), f32), jax.ShapeDt...  7.09 us
    pallas_call x1, Pallas kernels, body(): call(lookup_kernel, jax.ShapeDtypeStruct((assign.shape[0], width), f32),...  5.56 us
  transfers between devices with their start and end apart: 2, of which 1 were waited for; matrix products, arithmetic and copies ran while one was open for 0% of the time, Pallas kernels for 10%

profile of v6, /device:TPU:1, one launch (start us, length us, event | category | flops | bytes accessed | tf_op | source)
XLA Modules:
  0.0 195.7 jit_solution(14998943778396742461)
XLA Ops:
  7.2 0.0 copy-start.4
  7.2 0.0 all-gather.2.cloned.1.call-start
  7.2 0.7 all-gather.2.cloned.1.call-update
  7.9 0.0 reduce-scatter.2.cloned.1.call-start
  8.0 0.1 pad_add_fusion.z_ref
  8.0 1.6 copy-done
  9.6 0.8 shard_map.51
  10.5 0.0 copy-done.4
  10.5 0.7 copy-done.1
  11.2 5.6 %shard_map.50 = f32[1024,512]{1,0:T(8,128)} custom-call(s32[2]{0:T(128)S(1)} %pad_add_fusion.z_ref, s32[8,128]{1,0:T(8,128)S(1)} %bitcast.4, f32[1024,512]{1,0:T(8,128)S(1)} %copy-done.1), custom_call_target="tpu_custom_call" | custom-call | tf_op jit(solution)/shard_map/pallas_call | solution.py:228
  16.8 45.0 %all-gather.2.cloned.1.call-done.items_ref = f32[2048,512]{1,0:T(8,128)} async-done(((f32[128,512]{1,0:T(8,128)}), f32[2048,512]{1,0:T(8,128)}) %all-gather.2.cloned.1.call-update) | async-done | bytes 4194320 | tf_op jit(solution)/shard_map/all_gather | solution.py:224
  61.7 0.0 reduce-scatter.2.cloned.1.call-update
  61.8 7.1 %shard_map.52 = (f32[512,2048]{1,0:T(8,128)S(1)}, f32[4,128]{1,0:T(4,128)S(1)}, bf16[2048,512]{1,0:T(8,128)(2,1)S(1)}, bf16[2048,512]{1,0:T(8,128)(2,1)S(1)}) custom-call(bf16[512,512]{1,0:T(8,128)(2,1)S(1)} %get-tuple-element.18.high_ref, bf16[512,512]{1,0:T(8,128)(2,1)S(1)} %get-tuple-element.19.low_ref, f32[2048,512]{1,0:T(8,128)} %all-gather.2.cloned.1.call-done.items_ref), custom_call_target="tpu_custom_call" | custom-call | tf_op jit(solution)/shard_map/pallas_call | solution.py:235
  68.9 18.0 %all_to_all.40.got_ref = f32[32,4,128]{2,1,0:T(4,128)S(1)} all-to-all(f32[32,4,128]{2,1,0:T(4,128)S(1)} %broadcast_in_dim.2), channel_id=1, replica_groups=mesh['x'=4,'yh'=4,'yl'=2,'core'=2,'code'=8] {'x','yh','yl'}, dimensions={0} | all-to-all | bytes 131072 | tf_op jit(solution)/shard_map/all_to_all | solution.py:254
  86.8 0.4 shard_map.53
  87.3 14.6 %all_to_all.41.got_ref = f32[16,16,128]{2,1,0:T(8,128)S(1)} all-to-all(f32[16,16,128]{2,1,0:T(8,128)S(1)} %shard_map.53), channel_id=1, replica_groups=mesh['x'=4,'yh'=4,'yl'=2,'core'=2,'code'=8] {'core','code'}, dimensions={0} | all-to-all | bytes 262144 | tf_op jit(solution)/shard_map/all_to_all | solution.py:256
  101.8 0.4 shard_map.54
  102.2 11.8 %all_to_all.42.got_ref = f32[32,4,128]{2,1,0:T(4,128)S(1)} all-to-all(f32[32,4,128]{2,1,0:T(4,128)S(1)} %shard_map.54), channel_id=1, replica_groups=mesh['x'=4,'yh'=4,'yl'=2,'core'=2,'code'=8] {'x','yh','yl'}, dimensions={0} | all-to-all | bytes 131072 | tf_op jit(solution)/shard_map/all_to_all | solution.py:254
  114.0 0.4 shard_map.55
  114.5 12.8 %all_to_all.43.got_ref = f32[16,16,128]{2,1,0:T(8,128)S(1)} all-to-all(f32[16,16,128]{2,1,0:T(8,128)S(1)} %shard_map.55), channel_id=1, replica_groups=mesh['x'=4,'yh'=4,'yl'=2,'core'=2,'code'=8] {'core','code'}, dimensions={0} | all-to-all | bytes 262144 | tf_op jit(solution)/shard_map/all_to_all | solution.py:256
  127.3 0.4 shard_map.56
  127.6 11.9 %all_to_all.44.got_ref = f32[32,4,128]{2,1,0:T(4,128)S(1)} all-to-all(f32[32,4,128]{2,1,0:T(4,128)S(1)} %shard_map.56), channel_id=1, replica_groups=mesh['x'=4,'yh'=4,'yl'=2,'core'=2,'code'=8] {'x','yh','yl'}, dimensions={0} | all-to-all | bytes 131072 | tf_op jit(solution)/shard_map/all_to_all | solution.py:254
  139.5 0.4 shard_map.57
  139.9 12.9 %all_to_all.45.got_ref = f32[16,16,128]{2,1,0:T(8,128)S(1)} all-to-all(f32[16,16,128]{2,1,0:T(8,128)S(1)} %shard_map.57), channel_id=1, replica_groups=mesh['x'=4,'yh'=4,'yl'=2,'core'=2,'code'=8] {'core','code'}, dimensions={0} | all-to-all | bytes 262144 | tf_op jit(solution)/shard_map/all_to_all | solution.py:256
  152.8 3.7 %shard_map.58 = f32[8,33,8,128]{3,2,1,0:T(8,128)S(1)} custom-call(f32[16,16,128]{2,1,0:T(8,128)S(1)} %all_to_all.45.got_ref, f32[512,2048]{1,0:T(8,128)S(1)} %get-tuple-element.22.refs_0_, bf16[2048,512]{1,0:T(8,128)(2,1)S(1)} %get-tuple-element.23.refs_1_, bf16[2048,512]{1,0:T(8,128)(2,1)S(1)} %get-tuple-element.24.refs_2_), custom_call_target="tpu_custom_call" | custom-call | tf_op jit(solution)/shard_map/pallas_call | solution.py:262
  156.5 0.0 copy-start.2
  156.5 17.1 %all_to_all.46.got_ref = f32[8,33,8,128]{3,2,1,0:T(8,128)S(1)} all-to-all(f32[8,33,8,128]{3,2,1,0:T(8,128)S(1)} %shard_map.58), channel_id=1, replica_groups=mesh['x'=4,'yh'=4,'yl'=2,'core'=2,'code'=8] {'x','yl'}, dimensions={0} | all-to-all | bytes 2162688 | tf_op jit(solution)/shard_map/all_to_all | solution.py:268
  173.6 0.1 shard_map.59
  173.7 13.5 %all_to_all.47.got_ref = f32[8,5,8,128]{3,2,1,0:T(8,128)S(1)} all-to-all(f32[8,5,8,128]{3,2,1,0:T(8,128)S(1)} %shard_map.59), channel_id=1, replica_groups=mesh['x'=4,'yh'=4,'yl'=2,'core'=2,'code'=8] {'yh','core'}, dimensions={0} | all-to-all | bytes 327680 | tf_op jit(solution)/shard_map/all_to_all | solution.py:272
  187.1 0.0 copy-done.2
  187.2 0.9 copy-done.3
  188.1 0.7 shard_map.60
  (5 shorter events, 0.0 us)
Async XLA Ops:
  7.2 3.3 %copy-start.4 = (s32[1024]{0:T(1024)S(1)}, s32[1024]{0:T(1024)}, u32[]{:S(2)}) copy-start(s32[1024]{0:T(1024)} %param.5) | copy-start | bytes 12292
  7.2 54.6 %all-gather.2.cloned.1.call-start = ((), (), s32[]{:S(2)}) async-start(), calls=%async_computation.9 | async-start | bytes 4456448 | tf_op jit(solution)/shard_map/all_gather | solution.py:224
  7.9 165.7 %reduce-scatter.2.cloned.1.call-start = ((), (), s32[]{:S(2)}) async-start(), calls=%async_computation.10 | async-start | bytes 2359296 | tf_op jit(solution)/shard_map/reduce_scatter | solution.py:232
  8.0 1.6 copy-start
  9.6 1.6 copy-start.1
  156.5 30.6 %copy-start.2 = (f32[128,512]{1,0:T(8,128)S(1)}, f32[128,512]{1,0:T(8,128)}, u32[]{:S(2)}) copy-start(f32[128,512]{1,0:T(8,128)} %items_ref.1) | copy-start | bytes 786436
  187.2 1.0 copy-start.3
Sparse Core Ops, SparseCore 0:
  10.1 51.5 all-gather.1
  64.6 41.7 reduce-scatter.1

commit v7 on v6

--- a/solution.py
+++ b/solution.py
@@ -59,27 +59,29 @@
 
 def chunk_kernel(high_ref, low_ref, items_ref, out_ref, sums_ref, xh_ref, xl_ref, held_ref, sems):
     codes, step = high_ref.shape[0], 256
-    starts = range(0, items_ref.shape[0], step)
+    total = items_ref.shape[0]
+    edges = [0, step, total // 2, total]
     copies = [
-        pltpu.make_async_copy(items_ref.at[pl.ds(first, step)], held_ref.at[pl.ds(first, step)], sems.at[i])
-        for i, first in enumerate(starts)
+        pltpu.make_async_copy(items_ref.at[pl.ds(a, b - a)], held_ref.at[pl.ds(a, b - a)], sems.at[i])
+        for i, (a, b) in enumerate(zip(edges, edges[1:]))
     ]
     for copy in copies:
         copy.start()
     folded = [jnp.zeros((step, LANES), jnp.float32) for _ in range(0, codes, step)]
-    for copy, first in zip(copies, starts):
+    for copy, begin, end in zip(copies, edges, edges[1:]):
         copy.wait()
-        values = held_ref[first:first + step]
-        xh_ref[first:first + step], xl_ref[first:first + step] = split(values)
-        item_high, item_low = split(unit_rows(values))
-        for k, start in enumerate(range(0, codes, step)):
-            code_high = high_ref[start:start + step]
-            code_low = low_ref[start:start + step]
-            logits = dot_nt(code_high, item_high) + (dot_nt(code_high, item_low) + dot_nt(code_low, item_high))
-            values = jnp.exp(logits)
-            out_ref[start:start + step, first:first + step] = values
-            for lane in range(0, step, LANES):
-                folded[k] = folded[k] + values[:, lane:lane + LANES]
+        for first in range(begin, end, step):
+            values = held_ref[first:first + step]
+            xh_ref[first:first + step], xl_ref[first:first + step] = split(values)
+            item_high, item_low = split(unit_rows(values))
+            for k, start in enumerate(range(0, codes, step)):
+                code_high = high_ref[start:start + step]
+                code_low = low_ref[start:start + step]
+                logits = dot_nt(code_high, item_high) + (dot_nt(code_high, item_low) + dot_nt(code_low, item_high))
+                values = jnp.exp(logits)
+                out_ref[start:start + step, first:first + step] = values
+                for lane in range(0, step, LANES):
+                    folded[k] = folded[k] + values[:, lane:lane + LANES]
     for k, total in enumerate(folded):
         for part in range(step // LANES):
             row = k * (step // LANES) + part
@@ -241,7 +243,7 @@
             part,
         ),
         [VMEM, VMEM, pl.BlockSpec(memory_space=pl.ANY)],
-        [pltpu.VMEM((group, width), f32), pltpu.SemaphoreType.DMA((group // 256,))],
+        [pltpu.VMEM((group, width), f32), pltpu.SemaphoreType.DMA((3,))],
         grant=16,
     )(code_high, code_low, pltpu.with_memory_space_constraint(gathered, pltpu.HBM))
     blocks, count = [kernel_vals], 1
@@ -265,8 +267,8 @@
         operands + [VMEM] * (2 * count),
         grant=16,
     )(got, *blocks, item_high, item_low)
+    numer, looked = lax.optimization_barrier((numer, looked))
     got = lax.all_to_all(numer, ("x", "yl"), 0, 0)
-    got, looked = lax.optimization_barrier((got, looked))
     peers = high * nc
     packed = call(repack_kernel, jax.ShapeDtypeStruct((peers, tiles // peers + 1, SUB, LANES), f32), [VMEM])(got)
     got = lax.all_to_all(packed, ("yh", "core"), 0, 0)

time: 196 us -> 194 us (0.990)
  transfers between devices with their start and end apart: 2 -> 2, of which waited for: 1 -> 1; matrix products, arithmetic and copies ran while one was open for 0% -> 0% of each run, Pallas kernels for 10% -> 9%
where the time goes in v7:
time: 194 us; the launch traced here: 193 us
  blocking collectives  112 us (58%)
  waiting for transfers between devices  45.7 us (24%)
  Pallas kernels  18.3 us (9%)
  between operations  14.2 us (7%)
  local copies, waits for them, and re-layouts  2.35 us (1%)
    all_gather x1, waiting for transfers between devices, body(): gathered = lax.all_gather(items, ('core', 'code'), axis=0, tiled=True)  45 us
    all_to_all x3, blocking collectives, body(): got = lax.all_to_all(cols, ('x', 'yh', 'yl'), 0, 0)  41.8 us
    all_to_all x3, blocking collectives, body(): got = lax.all_to_all(rows, ('core', 'code'), 0, 0)  40.1 us
    all_to_all x1, blocking collectives, body(): got = lax.all_to_all(numer, ('x', 'yl'), 0, 0)  17.1 us
    all_to_all x1, blocking collectives, body(): got = lax.all_to_all(packed, ('yh', 'core'), 0, 0)  13.5 us
    pallas_call x1, Pallas kernels, body(): call(lookup_kernel, jax.ShapeDtypeStruct((assign.shape[0], width), f32),...  5.56 us
    pallas_call x1, Pallas kernels, body(): call(chunk_kernel, (jax.ShapeDtypeStruct((half, group), f32), jax.ShapeDt...  5.44 us
  transfers between devices with their start and end apart: 2, of which 1 were waited for; matrix products, arithmetic and copies ran while one was open for 0% of the time, Pallas kernels for 9%

profile of v7, /device:TPU:1, one launch (start us, length us, event | category | flops | bytes accessed | tf_op | source)
XLA Modules:
  0.0 193.1 jit_solution(4301741825806576640)
XLA Ops:
  7.2 0.0 copy-start.4
  7.2 0.0 all-gather.2.cloned.1.call-start
  7.2 0.7 all-gather.2.cloned.1.call-update
  7.9 0.0 reduce-scatter.2.cloned.1.call-start
  8.0 0.1 pad_add_fusion.z_ref
  8.0 1.6 copy-done
  9.6 0.8 shard_map.51
  10.5 0.0 copy-done.4
  10.5 0.7 copy-done.1
  11.2 5.6 %shard_map.50 = f32[1024,512]{1,0:T(8,128)} custom-call(s32[2]{0:T(128)S(1)} %pad_add_fusion.z_ref, s32[8,128]{1,0:T(8,128)S(1)} %bitcast.4, f32[1024,512]{1,0:T(8,128)S(1)} %copy-done.1), custom_call_target="tpu_custom_call" | custom-call | tf_op jit(solution)/shard_map/pallas_call | solution.py:230
  16.8 45.0 %all-gather.2.cloned.1.call-done.items_ref = f32[2048,512]{1,0:T(8,128)} async-done(((f32[128,512]{1,0:T(8,128)}), f32[2048,512]{1,0:T(8,128)}) %all-gather.2.cloned.1.call-update) | async-done | bytes 4194320 | tf_op jit(solution)/shard_map/all_gather | solution.py:226
  61.7 0.0 reduce-scatter.2.cloned.1.call-update
  61.8 5.4 %shard_map.52 = (f32[512,2048]{1,0:T(8,128)S(1)}, f32[4,128]{1,0:T(4,128)S(1)}, bf16[2048,512]{1,0:T(8,128)(2,1)S(1)}, bf16[2048,512]{1,0:T(8,128)(2,1)S(1)}) custom-call(bf16[512,512]{1,0:T(8,128)(2,1)S(1)} %get-tuple-element.18.high_ref, bf16[512,512]{1,0:T(8,128)(2,1)S(1)} %get-tuple-element.19.low_ref, f32[2048,512]{1,0:T(8,128)} %all-gather.2.cloned.1.call-done.items_ref), custom_call_target="tpu_custom_call" | custom-call | tf_op jit(solution)/shard_map/pallas_call | solution.py:237
  67.2 18.0 %all_to_all.40.got_ref = f32[32,4,128]{2,1,0:T(4,128)S(1)} all-to-all(f32[32,4,128]{2,1,0:T(4,128)S(1)} %broadcast_in_dim.2), channel_id=1, replica_groups=mesh['x'=4,'yh'=4,'yl'=2,'core'=2,'code'=8] {'x','yh','yl'}, dimensions={0} | all-to-all | bytes 131072 | tf_op jit(solution)/shard_map/all_to_all | solution.py:256
  85.2 0.4 shard_map.53
  85.6 14.3 %all_to_all.41.got_ref = f32[16,16,128]{2,1,0:T(8,128)S(1)} all-to-all(f32[16,16,128]{2,1,0:T(8,128)S(1)} %shard_map.53), channel_id=1, replica_groups=mesh['x'=4,'yh'=4,'yl'=2,'core'=2,'code'=8] {'core','code'}, dimensions={0} | all-to-all | bytes 262144 | tf_op jit(solution)/shard_map/all_to_all | solution.py:258
  99.9 0.4 shard_map.54
  100.3 12.0 %all_to_all.42.got_ref = f32[32,4,128]{2,1,0:T(4,128)S(1)} all-to-all(f32[32,4,128]{2,1,0:T(4,128)S(1)} %shard_map.54), channel_id=1, replica_groups=mesh['x'=4,'yh'=4,'yl'=2,'core'=2,'code'=8] {'x','yh','yl'}, dimensions={0} | all-to-all | bytes 131072 | tf_op jit(solution)/shard_map/all_to_all | solution.py:256
  112.3 0.4 shard_map.55
  112.7 12.9 %all_to_all.43.got_ref = f32[16,16,128]{2,1,0:T(8,128)S(1)} all-to-all(f32[16,16,128]{2,1,0:T(8,128)S(1)} %shard_map.55), channel_id=1, replica_groups=mesh['x'=4,'yh'=4,'yl'=2,'core'=2,'code'=8] {'core','code'}, dimensions={0} | all-to-all | bytes 262144 | tf_op jit(solution)/shard_map/all_to_all | solution.py:258
  125.6 0.4 shard_map.56
  126.0 11.9 %all_to_all.44.got_ref = f32[32,4,128]{2,1,0:T(4,128)S(1)} all-to-all(f32[32,4,128]{2,1,0:T(4,128)S(1)} %shard_map.56), channel_id=1, replica_groups=mesh['x'=4,'yh'=4,'yl'=2,'core'=2,'code'=8] {'x','yh','yl'}, dimensions={0} | all-to-all | bytes 131072 | tf_op jit(solution)/shard_map/all_to_all | solution.py:256
  137.9 0.4 shard_map.57
  138.3 12.9 %all_to_all.45.got_ref = f32[16,16,128]{2,1,0:T(8,128)S(1)} all-to-all(f32[16,16,128]{2,1,0:T(8,128)S(1)} %shard_map.57), channel_id=1, replica_groups=mesh['x'=4,'yh'=4,'yl'=2,'core'=2,'code'=8] {'core','code'}, dimensions={0} | all-to-all | bytes 262144 | tf_op jit(solution)/shard_map/all_to_all | solution.py:258
  151.2 3.7 %shard_map.58 = f32[8,33,8,128]{3,2,1,0:T(8,128)S(1)} custom-call(f32[16,16,128]{2,1,0:T(8,128)S(1)} %all_to_all.45.got_ref, f32[512,2048]{1,0:T(8,128)S(1)} %get-tuple-element.22.refs_0_, bf16[2048,512]{1,0:T(8,128)(2,1)S(1)} %get-tuple-element.23.refs_1_, bf16[2048,512]{1,0:T(8,128)(2,1)S(1)} %get-tuple-element.24.refs_2_), custom_call_target="tpu_custom_call" | custom-call | tf_op jit(solution)/shard_map/pallas_call | solution.py:264
  154.9 0.0 copy-start.2
  154.9 0.0 reduce-scatter.2.cloned.1.call-done.looked_ref
  154.9 17.1 %all_to_all.46.got_ref = f32[8,33,8,128]{3,2,1,0:T(8,128)S(1)} all-to-all(f32[8,33,8,128]{3,2,1,0:T(8,128)S(1)} %shard_map.58), channel_id=1, replica_groups=mesh['x'=4,'yh'=4,'yl'=2,'core'=2,'code'=8] {'x','yl'}, dimensions={0} | all-to-all | bytes 2162688 | tf_op jit(solution)/shard_map/all_to_all | solution.py:271
  172.0 0.1 shard_map.59
  172.0 13.5 %all_to_all.47.got_ref = f32[8,5,8,128]{3,2,1,0:T(8,128)S(1)} all-to-all(f32[8,5,8,128]{3,2,1,0:T(8,128)S(1)} %shard_map.59), channel_id=1, replica_groups=mesh['x'=4,'yh'=4,'yl'=2,'core'=2,'code'=8] {'yh','core'}, dimensions={0} | all-to-all | bytes 327680 | tf_op jit(solution)/shard_map/all_to_all | solution.py:274
  185.5 0.0 copy-done.2
  185.5 0.7 shard_map.60
  (5 shorter events, 0.0 us)
Async XLA Ops:
  7.2 3.3 %copy-start.4 = (s32[1024]{0:T(1024)S(1)}, s32[1024]{0:T(1024)}, u32[]{:S(2)}) copy-start(s32[1024]{0:T(1024)} %param.5) | copy-start | bytes 12292
  7.2 54.6 %all-gather.2.cloned.1.call-start = ((), (), s32[]{:S(2)}) async-start(), calls=%async_computation.9 | async-start | bytes 4456448 | tf_op jit(solution)/shard_map/all_gather | solution.py:226
  7.9 147.0 %reduce-scatter.2.cloned.1.call-start = ((), (), s32[]{:S(2)}) async-start(), calls=%async_computation.10 | async-start | bytes 2359296 | tf_op jit(solution)/shard_map/reduce_scatter | solution.py:234
  8.0 1.6 copy-start
  9.6 1.6 copy-start.1
  154.9 30.7 %copy-start.2 = (f32[128,512]{1,0:T(8,128)S(1)}, f32[128,512]{1,0:T(8,128)}, u32[]{:S(2)}) copy-start(f32[128,512]{1,0:T(8,128)} %items_ref.1) | copy-start | bytes 786436
  154.9 30.6 %copy-start.3 = (f32[128,512]{1,0:T(8,128)S(1)}, f32[128,512]{1,0:T(8,128)}, u32[]{:S(2)}) copy-start(f32[128,512]{1,0:T(8,128)} %reduce-scatter.2.cloned.1.call-done.looked_ref) | copy-start | bytes 786436
Sparse Core Ops, SparseCore 0:
  10.1 51.5 all-gather.1
  64.6 41.7 reduce-scatter.1

commit v8 on v7

--- a/solution.py
+++ b/solution.py
@@ -161,8 +161,8 @@
                 for group in range(LANES // SUB):
                     x, rest = divmod(lane // SUB + group, per_x)
                     y, core = divmod(rest, cores)
-                    row = (y // near) * cores + core
-                    out_ref[x * near + y % near, row * parts + col] = turned[group * SUB:(group + 1) * SUB]
+                    row = core * (per_x // (near * cores)) + y // near
+                    out_ref[(y % near) * nx + x, row * parts + col] = turned[group * SUB:(group + 1) * SUB]
     tile = jnp.concatenate(mass + [jnp.ones((SUB - parts, LANES), jnp.float32)], axis=0)
     for peer in range(out_ref.shape[0]):
         out_ref[peer, out_ref.shape[1] - 1] = tile
@@ -202,8 +202,9 @@
     residual_ref[...] = items_ref[...] - looked_ref[...]
     peers, parts = got_ref.shape[0], got_ref.shape[1] - 1
     for core in range(cores):
-        summed = got_ref[core]
-        for peer in range(core + cores, peers, cores):
+        first = core * (peers // cores)
+        summed = got_ref[first]
+        for peer in range(first + 1, first + peers // cores):
             summed = summed + got_ref[peer]
         for b in range(parts):
             lane = (core * parts + b) * LANES
@@ -253,7 +254,7 @@
     operands = [VMEM] * (1 + count)
     cols = jnp.broadcast_to(col_tile[None], col_shape.shape)
     for turn in range(ITERS):
-        got = lax.all_to_all(cols, ("x", "yh", "yl"), 0, 0)
+        got = lax.all_to_all(cols, ("yh", "yl", "x"), 0, 0)
         rows = call(row_kernel, row_shape, operands)(got, *blocks)
         got = lax.all_to_all(rows, ("core", "code"), 0, 0)
         if turn < ITERS - 1:
@@ -268,10 +269,10 @@
         grant=16,
     )(got, *blocks, item_high, item_low)
     numer, looked = lax.optimization_barrier((numer, looked))
-    got = lax.all_to_all(numer, ("x", "yl"), 0, 0)
+    got = lax.all_to_all(numer, ("yl", "x"), 0, 0)
     peers = high * nc
     packed = call(repack_kernel, jax.ShapeDtypeStruct((peers, tiles // peers + 1, SUB, LANES), f32), [VMEM])(got)
-    got = lax.all_to_all(packed, ("yh", "core"), 0, 0)
+    got = lax.all_to_all(packed, ("core", "yh"), 0, 0)
     shapes = (jax.ShapeDtypeStruct((per_owner, local_codes), f32), jax.ShapeDtypeStruct(items.shape, f32))
     turned, residual = call(functools.partial(finish_kernel, nc), shapes, [VMEM] * 3)(got, items, looked)
     new_codewords = turned.T

time: 194 us -> 194 us (level)
  no operation moved by 1% of the time
where the time goes in v8:
time: 194 us; the launch traced here: 193 us
  blocking collectives  113 us (58%)
  waiting for transfers between devices  45.7 us (24%)
  Pallas kernels  18.3 us (9%)
  between operations  14.2 us (7%)
  local copies, waits for them, and re-layouts  2.35 us (1%)
    all_gather x1, waiting for transfers between devices, body(): gathered = lax.all_gather(items, ('core', 'code'), axis=0, tiled=True)  45 us
    all_to_all x3, blocking collectives, body(): got = lax.all_to_all(cols, ('yh', 'yl', 'x'), 0, 0)  41.7 us
    all_to_all x3, blocking collectives, body(): got = lax.all_to_all(rows, ('core', 'code'), 0, 0)  40 us
    all_to_all x1, blocking collectives, body(): got = lax.all_to_all(numer, ('yl', 'x'), 0, 0)  17.1 us
    all_to_all x1, blocking collectives, body(): got = lax.all_to_all(packed, ('core', 'yh'), 0, 0)  13.9 us
    pallas_call x1, Pallas kernels, body(): call(lookup_kernel, jax.ShapeDtypeStruct((assign.shape[0], width), f32),...  5.56 us
    pallas_call x1, Pallas kernels, body(): call(chunk_kernel, (jax.ShapeDtypeStruct((half, group), f32), jax.ShapeDt...  5.44 us
  transfers between devices with their start and end apart: 2, of which 1 were waited for; matrix products, arithmetic and copies ran while one was open for 0% of the time, Pallas kernels for 9%

profile of v8, /device:TPU:1, one launch (start us, length us, event | category | flops | bytes accessed | tf_op | source)
XLA Modules:
  0.0 193.3 jit_solution(13718803418588796725)
XLA Ops:
  7.2 0.0 copy-start.4
  7.2 0.0 all-gather.2.cloned.1.call-start
  7.2 0.7 all-gather.2.cloned.1.call-update
  7.9 0.0 reduce-scatter.2.cloned.1.call-start
  8.0 0.1 pad_add_fusion.z_ref
  8.0 1.6 copy-done
  9.6 0.8 shard_map.51
  10.5 0.7 copy-done.1
  11.2 5.6 %shard_map.50 = f32[1024,512]{1,0:T(8,128)} custom-call(s32[2]{0:T(128)S(1)} %pad_add_fusion.z_ref, s32[8,128]{1,0:T(8,128)S(1)} %bitcast.4, f32[1024,512]{1,0:T(8,128)S(1)} %copy-done.1), custom_call_target="tpu_custom_call" | custom-call | tf_op jit(solution)/shard_map/pallas_call | solution.py:231
  16.8 45.0 %all-gather.2.cloned.1.call-done.items_ref = f32[2048,512]{1,0:T(8,128)} async-done(((f32[128,512]{1,0:T(8,128)}), f32[2048,512]{1,0:T(8,128)}) %all-gather.2.cloned.1.call-update) | async-done | bytes 4194320 | tf_op jit(solution)/shard_map/all_gather | solution.py:227
  61.7 0.0 reduce-scatter.2.cloned.1.call-update
  61.8 5.4 %shard_map.52 = (f32[512,2048]{1,0:T(8,128)S(1)}, f32[4,128]{1,0:T(4,128)S(1)}, bf16[2048,512]{1,0:T(8,128)(2,1)S(1)}, bf16[2048,512]{1,0:T(8,128)(2,1)S(1)}) custom-call(bf16[512,512]{1,0:T(8,128)(2,1)S(1)} %get-tuple-element.18.high_ref, bf16[512,512]{1,0:T(8,128)(2,1)S(1)} %get-tuple-element.19.low_ref, f32[2048,512]{1,0:T(8,128)} %all-gather.2.cloned.1.call-done.items_ref), custom_call_target="tpu_custom_call" | custom-call | tf_op jit(solution)/shard_map/pallas_call | solution.py:238
  67.2 17.9 %all_to_all.40.got_ref = f32[32,4,128]{2,1,0:T(4,128)S(1)} all-to-all(f32[32,4,128]{2,1,0:T(4,128)S(1)} %broadcast_in_dim.2), channel_id=1, replica_groups=mesh['x'=4,'yh'=4,'yl'=2,'core'=2,'code'=8] {'yh','yl','x'}, dimensions={0} | all-to-all | bytes 131072 | tf_op jit(solution)/shard_map/all_to_all | solution.py:257
  85.2 0.4 shard_map.53
  85.6 14.3 %all_to_all.41.got_ref = f32[16,16,128]{2,1,0:T(8,128)S(1)} all-to-all(f32[16,16,128]{2,1,0:T(8,128)S(1)} %shard_map.53), channel_id=1, replica_groups=mesh['x'=4,'yh'=4,'yl'=2,'core'=2,'code'=8] {'core','code'}, dimensions={0} | all-to-all | bytes 262144 | tf_op jit(solution)/shard_map/all_to_all | solution.py:259
  99.9 0.4 shard_map.54
  100.3 11.9 %all_to_all.42.got_ref = f32[32,4,128]{2,1,0:T(4,128)S(1)} all-to-all(f32[32,4,128]{2,1,0:T(4,128)S(1)} %shard_map.54), channel_id=1, replica_groups=mesh['x'=4,'yh'=4,'yl'=2,'core'=2,'code'=8] {'yh','yl','x'}, dimensions={0} | all-to-all | bytes 131072 | tf_op jit(solution)/shard_map/all_to_all | solution.py:257
  112.2 0.4 shard_map.55
  112.6 12.9 %all_to_all.43.got_ref = f32[16,16,128]{2,1,0:T(8,128)S(1)} all-to-all(f32[16,16,128]{2,1,0:T(8,128)S(1)} %shard_map.55), channel_id=1, replica_groups=mesh['x'=4,'yh'=4,'yl'=2,'core'=2,'code'=8] {'core','code'}, dimensions={0} | all-to-all | bytes 262144 | tf_op jit(solution)/shard_map/all_to_all | solution.py:259
  125.5 0.4 shard_map.56
  125.9 11.8 %all_to_all.44.got_ref = f32[32,4,128]{2,1,0:T(4,128)S(1)} all-to-all(f32[32,4,128]{2,1,0:T(4,128)S(1)} %shard_map.56), channel_id=1, replica_groups=mesh['x'=4,'yh'=4,'yl'=2,'core'=2,'code'=8] {'yh','yl','x'}, dimensions={0} | all-to-all | bytes 131072 | tf_op jit(solution)/shard_map/all_to_all | solution.py:257
  137.7 0.4 shard_map.57
  138.1 12.8 %all_to_all.45.got_ref = f32[16,16,128]{2,1,0:T(8,128)S(1)} all-to-all(f32[16,16,128]{2,1,0:T(8,128)S(1)} %shard_map.57), channel_id=1, replica_groups=mesh['x'=4,'yh'=4,'yl'=2,'core'=2,'code'=8] {'core','code'}, dimensions={0} | all-to-all | bytes 262144 | tf_op jit(solution)/shard_map/all_to_all | solution.py:259
  151.0 3.7 %shard_map.58 = f32[8,33,8,128]{3,2,1,0:T(8,128)S(1)} custom-call(f32[16,16,128]{2,1,0:T(8,128)S(1)} %all_to_all.45.got_ref, f32[512,2048]{1,0:T(8,128)S(1)} %get-tuple-element.22.refs_0_, bf16[2048,512]{1,0:T(8,128)(2,1)S(1)} %get-tuple-element.23.refs_1_, bf16[2048,512]{1,0:T(8,128)(2,1)S(1)} %get-tuple-element.24.refs_2_), custom_call_target="tpu_custom_call" | custom-call | tf_op jit(solution)/shard_map/pallas_call | solution.py:265
  154.7 0.0 copy-start.2
  154.7 0.0 reduce-scatter.2.cloned.1.call-done.looked_ref
  154.7 0.0 copy-start.3
  154.7 17.1 %all_to_all.46.got_ref = f32[8,33,8,128]{3,2,1,0:T(8,128)S(1)} all-to-all(f32[8,33,8,128]{3,2,1,0:T(8,128)S(1)} %shard_map.58), channel_id=1, replica_groups=mesh['x'=4,'yh'=4,'yl'=2,'core'=2,'code'=8] {'yl','x'}, dimensions={0} | all-to-all | bytes 2162688 | tf_op jit(solution)/shard_map/all_to_all | solution.py:272
  171.8 0.1 shard_map.59
  171.8 13.9 %all_to_all.47.got_ref = f32[8,5,8,128]{3,2,1,0:T(8,128)S(1)} all-to-all(f32[8,5,8,128]{3,2,1,0:T(8,128)S(1)} %shard_map.59), channel_id=1, replica_groups=mesh['x'=4,'yh'=4,'yl'=2,'core'=2,'code'=8] {'core','yh'}, dimensions={0} | all-to-all | bytes 327680 | tf_op jit(solution)/shard_map/all_to_all | solution.py:275
  185.8 0.0 copy-done.2
  185.8 0.7 shard_map.60
  (5 shorter events, 0.0 us)
Async XLA Ops:
  7.2 3.3 %copy-start.4 = (s32[1024]{0:T(1024)S(1)}, s32[1024]{0:T(1024)}, u32[]{:S(2)}) copy-start(s32[1024]{0:T(1024)} %param.5) | copy-start | bytes 12292
  7.2 54.6 %all-gather.2.cloned.1.call-start = ((), (), s32[]{:S(2)}) async-start(), calls=%async_computation.9 | async-start | bytes 4456448 | tf_op jit(solution)/shard_map/all_gather | solution.py:227
  7.9 146.8 %reduce-scatter.2.cloned.1.call-start = ((), (), s32[]{:S(2)}) async-start(), calls=%async_computation.10 | async-start | bytes 2359296 | tf_op jit(solution)/shard_map/reduce_scatter | solution.py:235
  8.0 1.6 copy-start
  9.6 1.6 copy-start.1
  154.7 31.1 %copy-start.2 = (f32[128,512]{1,0:T(8,128)S(1)}, f32[128,512]{1,0:T(8,128)}, u32[]{:S(2)}) copy-start(f32[128,512]{1,0:T(8,128)} %items_ref.1) | copy-start | bytes 786436
  154.7 31.0 %copy-start.3 = (f32[128,512]{1,0:T(8,128)S(1)}, f32[128,512]{1,0:T(8,128)}, u32[]{:S(2)}) copy-start(f32[128,512]{1,0:T(8,128)} %reduce-scatter.2.cloned.1.call-done.looked_ref) | copy-start | bytes 786436
Sparse Core Ops, SparseCore 0:
  10.1 51.5 all-gather.1
  64.6 41.7 reduce-scatter.1

commit v9 on v8

--- a/solution.py
+++ b/solution.py
@@ -60,32 +60,28 @@
 def chunk_kernel(high_ref, low_ref, items_ref, out_ref, sums_ref, xh_ref, xl_ref, held_ref, sems):
     codes, step = high_ref.shape[0], 256
     total = items_ref.shape[0]
-    edges = [0, step, total // 2, total]
+    edges = [0, step, 2 * step, total // 2, total]
     copies = [
         pltpu.make_async_copy(items_ref.at[pl.ds(a, b - a)], held_ref.at[pl.ds(a, b - a)], sems.at[i])
         for i, (a, b) in enumerate(zip(edges, edges[1:]))
     ]
     for copy in copies:
         copy.start()
-    folded = [jnp.zeros((step, LANES), jnp.float32) for _ in range(0, codes, step)]
+    code_high, code_low = high_ref[...], low_ref[...]
+    folded = jnp.zeros((codes, LANES), jnp.float32)
     for copy, begin, end in zip(copies, edges, edges[1:]):
         copy.wait()
         for first in range(begin, end, step):
             values = held_ref[first:first + step]
             xh_ref[first:first + step], xl_ref[first:first + step] = split(values)
             item_high, item_low = split(unit_rows(values))
-            for k, start in enumerate(range(0, codes, step)):
-                code_high = high_ref[start:start + step]
-                code_low = low_ref[start:start + step]
-                logits = dot_nt(code_high, item_high) + (dot_nt(code_high, item_low) + dot_nt(code_low, item_high))
-                values = jnp.exp(logits)
-                out_ref[start:start + step, first:first + step] = values
-                for lane in range(0, step, LANES):
-                    folded[k] = folded[k] + values[:, lane:lane + LANES]
-    for k, total in enumerate(folded):
-        for part in range(step // LANES):
-            row = k * (step // LANES) + part
-            sums_ref[row:row + 1] = lane_sums(total[part * LANES:(part + 1) * LANES])
+            logits = dot_nt(code_high, item_high) + (dot_nt(code_high, item_low) + dot_nt(code_low, item_high))
+            values = jnp.exp(logits)
+            out_ref[:, first:first + step] = values
+            for lane in range(0, step, LANES):
+                folded = folded + values[:, lane:lane + LANES]
+    for row in range(codes // LANES):
+        sums_ref[row:row + 1] = lane_sums(folded[row * LANES:(row + 1) * LANES])
 
 
 def load_blocks(refs):
@@ -132,27 +128,28 @@
     codes, width = refs[0].shape[0], high_refs[0].shape[1]
     parts = codes // LANES
     per_x = width // (nx * SUB)
-    step = 256
+    step = codes
     mass = []
     for start in range(0, codes, step):
         folded = jnp.zeros((step, LANES), jnp.float32)
         sums, at = None, 0
         for ref, xh_ref, xl_ref in zip(refs[:count], high_refs, low_refs):
-            highs, lows = [], []
-            for lane in range(0, ref.shape[1], LANES):
-                weights = ref[start:start + step, lane:lane + LANES] * scales[at]
-                folded = folded + weights
-                high, low = split(weights)
-                highs.append(high)
-                lows.append(low)
-                at += 1
-            high, low = jnp.concatenate(highs, axis=1), jnp.concatenate(lows, axis=1)
-            xh, xl = xh_ref[...], xl_ref[...]
-            more = jnp.dot(high, xh, preferred_element_type=jnp.float32) + (
-                jnp.dot(low, xh, preferred_element_type=jnp.float32)
-                + jnp.dot(high, xl, preferred_element_type=jnp.float32)
-            )
-            sums = more if sums is None else sums + more
+            for first in range(0, ref.shape[1], 512):
+                highs, lows = [], []
+                for lane in range(first, first + 512, LANES):
+                    weights = ref[start:start + step, lane:lane + LANES] * scales[at]
+                    folded = folded + weights
+                    high, low = split(weights)
+                    highs.append(high)
+                    lows.append(low)
+                    at += 1
+                high, low = jnp.concatenate(highs, axis=1), jnp.concatenate(lows, axis=1)
+                xh, xl = xh_ref[first:first + 512], xl_ref[first:first + 512]
+                more = jnp.dot(high, xh, preferred_element_type=jnp.float32) + (
+                    jnp.dot(low, xh, preferred_element_type=jnp.float32)
+                    + jnp.dot(high, xl, preferred_element_type=jnp.float32)
+                )
+                sums = more if sums is None else sums + more
         for part in range(step // LANES):
             mass.append(lane_sums(folded[part * LANES:(part + 1) * LANES]))
             col = start // LANES + part
@@ -244,7 +241,7 @@
             part,
         ),
         [VMEM, VMEM, pl.BlockSpec(memory_space=pl.ANY)],
-        [pltpu.VMEM((group, width), f32), pltpu.SemaphoreType.DMA((3,))],
+        [pltpu.VMEM((group, width), f32), pltpu.SemaphoreType.DMA((4,))],
         grant=16,
     )(code_high, code_low, pltpu.with_memory_space_constraint(gathered, pltpu.HBM))
     blocks, count = [kernel_vals], 1

time: 194 us -> 195 us (level)
  transfers between devices with their start and end apart: 2 -> 2, of which waited for: 1 -> 1; matrix products, arithmetic and copies ran while one was open for 0% -> 0% of each run, Pallas kernels for 9% -> 10%
where the time goes in v9:
time: 195 us
  blocking collectives  113 us (58%)
  waiting for transfers between devices  45.7 us (23%)
  Pallas kernels  19.6 us (10%)
  between operations  14.2 us (7%)
  local copies, waits for them, and re-layouts  2.35 us (1%)
    all_gather x1, waiting for transfers between devices, body(): gathered = lax.all_gather(items, ('core', 'code'), axis=0, tiled=True)  45 us
    all_to_all x3, blocking collectives, body(): got = lax.all_to_all(cols, ('yh', 'yl', 'x'), 0, 0)  41.8 us
    all_to_all x3, blocking collectives, body(): got = lax.all_to_all(rows, ('core', 'code'), 0, 0)  39.9 us
    all_to_all x1, blocking collectives, body(): got = lax.all_to_all(numer, ('yl', 'x'), 0, 0)  17.1 us
    all_to_all x1, blocking collectives, body(): got = lax.all_to_all(packed, ('core', 'yh'), 0, 0)  13.9 us
    pallas_call x1, Pallas kernels, body(): call(chunk_kernel, (jax.ShapeDtypeStruct((half, group), f32), jax.ShapeDt...  6.72 us
    pallas_call x1, Pallas kernels, body(): call(lookup_kernel, jax.ShapeDtypeStruct((assign.shape[0], width), f32),...  5.56 us
  transfers between devices with their start and end apart: 2, of which 1 were waited for; matrix products, arithmetic and copies ran while one was open for 0% of the time, Pallas kernels for 10%

profile of v9, /device:TPU:1, one launch (start us, length us, event | category | flops | bytes accessed | tf_op | source)
XLA Modules:
  0.0 194.5 jit_solution(2068094579854289624)
XLA Ops:
  7.2 0.0 copy-start.4
  7.2 0.0 all-gather.2.cloned.1.call-start
  7.2 0.7 all-gather.2.cloned.1.call-update
  7.9 0.0 reduce-scatter.2.cloned.1.call-start
  8.0 0.1 pad_add_fusion.z_ref
  8.0 1.6 copy-done
  9.6 0.8 shard_map.51
  10.5 0.0 copy-done.4
  10.5 0.7 copy-done.1
  11.2 5.6 %shard_map.50 = f32[1024,512]{1,0:T(8,128)} custom-call(s32[2]{0:T(128)S(1)} %pad_add_fusion.z_ref, s32[8,128]{1,0:T(8,128)S(1)} %bitcast.4, f32[1024,512]{1,0:T(8,128)S(1)} %copy-done.1), custom_call_target="tpu_custom_call" | custom-call | tf_op jit(solution)/shard_map/pallas_call | solution.py:228
  16.8 45.0 %all-gather.2.cloned.1.call-done.items_ref = f32[2048,512]{1,0:T(8,128)} async-done(((f32[128,512]{1,0:T(8,128)}), f32[2048,512]{1,0:T(8,128)}) %all-gather.2.cloned.1.call-update) | async-done | bytes 4194320 | tf_op jit(solution)/shard_map/all_gather | solution.py:224
  61.7 0.0 reduce-scatter.2.cloned.1.call-update
  61.8 6.7 %shard_map.52 = (f32[512,2048]{1,0:T(8,128)S(1)}, f32[4,128]{1,0:T(4,128)S(1)}, bf16[2048,512]{1,0:T(8,128)(2,1)S(1)}, bf16[2048,512]{1,0:T(8,128)(2,1)S(1)}) custom-call(bf16[512,512]{1,0:T(8,128)(2,1)S(1)} %get-tuple-element.18.high_ref, bf16[512,512]{1,0:T(8,128)(2,1)S(1)} %get-tuple-element.19.low_ref, f32[2048,512]{1,0:T(8,128)} %all-gather.2.cloned.1.call-done.items_ref), custom_call_target="tpu_custom_call" | custom-call | tf_op jit(solution)/shard_map/pallas_call | solution.py:235
  68.5 17.9 %all_to_all.40.got_ref = f32[32,4,128]{2,1,0:T(4,128)S(1)} all-to-all(f32[32,4,128]{2,1,0:T(4,128)S(1)} %broadcast_in_dim.2), channel_id=1, replica_groups=mesh['x'=4,'yh'=4,'yl'=2,'core'=2,'code'=8] {'yh','yl','x'}, dimensions={0} | all-to-all | bytes 131072 | tf_op jit(solution)/shard_map/all_to_all | solution.py:254
  86.4 0.4 shard_map.53
  86.9 14.1 %all_to_all.41.got_ref = f32[16,16,128]{2,1,0:T(8,128)S(1)} all-to-all(f32[16,16,128]{2,1,0:T(8,128)S(1)} %shard_map.53), channel_id=1, replica_groups=mesh['x'=4,'yh'=4,'yl'=2,'core'=2,'code'=8] {'core','code'}, dimensions={0} | all-to-all | bytes 262144 | tf_op jit(solution)/shard_map/all_to_all | solution.py:256
  101.0 0.4 shard_map.54
  101.4 12.0 %all_to_all.42.got_ref = f32[32,4,128]{2,1,0:T(4,128)S(1)} all-to-all(f32[32,4,128]{2,1,0:T(4,128)S(1)} %shard_map.54), channel_id=1, replica_groups=mesh['x'=4,'yh'=4,'yl'=2,'core'=2,'code'=8] {'yh','yl','x'}, dimensions={0} | all-to-all | bytes 131072 | tf_op jit(solution)/shard_map/all_to_all | solution.py:254
  113.4 0.4 shard_map.55
  113.8 12.9 %all_to_all.43.got_ref = f32[16,16,128]{2,1,0:T(8,128)S(1)} all-to-all(f32[16,16,128]{2,1,0:T(8,128)S(1)} %shard_map.55), channel_id=1, replica_groups=mesh['x'=4,'yh'=4,'yl'=2,'core'=2,'code'=8] {'core','code'}, dimensions={0} | all-to-all | bytes 262144 | tf_op jit(solution)/shard_map/all_to_all | solution.py:256
  126.7 0.4 shard_map.56
  127.1 11.8 %all_to_all.44.got_ref = f32[32,4,128]{2,1,0:T(4,128)S(1)} all-to-all(f32[32,4,128]{2,1,0:T(4,128)S(1)} %shard_map.56), channel_id=1, replica_groups=mesh['x'=4,'yh'=4,'yl'=2,'core'=2,'code'=8] {'yh','yl','x'}, dimensions={0} | all-to-all | bytes 131072 | tf_op jit(solution)/shard_map/all_to_all | solution.py:254
  138.9 0.4 shard_map.57
  139.3 12.9 %all_to_all.45.got_ref = f32[16,16,128]{2,1,0:T(8,128)S(1)} all-to-all(f32[16,16,128]{2,1,0:T(8,128)S(1)} %shard_map.57), channel_id=1, replica_groups=mesh['x'=4,'yh'=4,'yl'=2,'core'=2,'code'=8] {'core','code'}, dimensions={0} | all-to-all | bytes 262144 | tf_op jit(solution)/shard_map/all_to_all | solution.py:256
  152.2 3.7 %shard_map.58 = f32[8,33,8,128]{3,2,1,0:T(8,128)S(1)} custom-call(f32[16,16,128]{2,1,0:T(8,128)S(1)} %all_to_all.45.got_ref, f32[512,2048]{1,0:T(8,128)S(1)} %get-tuple-element.22.refs_0_, bf16[2048,512]{1,0:T(8,128)(2,1)S(1)} %get-tuple-element.23.refs_1_, bf16[2048,512]{1,0:T(8,128)(2,1)S(1)} %get-tuple-element.24.refs_2_), custom_call_target="tpu_custom_call" | custom-call | tf_op jit(solution)/shard_map/pallas_call | solution.py:262
  155.9 0.0 copy-start.2
  155.9 0.0 reduce-scatter.2.cloned.1.call-done.looked_ref
  155.9 17.1 %all_to_all.46.got_ref = f32[8,33,8,128]{3,2,1,0:T(8,128)S(1)} all-to-all(f32[8,33,8,128]{3,2,1,0:T(8,128)S(1)} %shard_map.58), channel_id=1, replica_groups=mesh['x'=4,'yh'=4,'yl'=2,'core'=2,'code'=8] {'yl','x'}, dimensions={0} | all-to-all | bytes 2162688 | tf_op jit(solution)/shard_map/all_to_all | solution.py:269
  173.0 0.1 shard_map.59
  173.1 13.9 %all_to_all.47.got_ref = f32[8,5,8,128]{3,2,1,0:T(8,128)S(1)} all-to-all(f32[8,5,8,128]{3,2,1,0:T(8,128)S(1)} %shard_map.59), channel_id=1, replica_groups=mesh['x'=4,'yh'=4,'yl'=2,'core'=2,'code'=8] {'core','yh'}, dimensions={0} | all-to-all | bytes 327680 | tf_op jit(solution)/shard_map/all_to_all | solution.py:272
  186.9 0.0 copy-done.3
  186.9 0.7 shard_map.60
  (5 shorter events, 0.0 us)
Async XLA Ops:
  7.2 3.3 %copy-start.4 = (s32[1024]{0:T(1024)S(1)}, s32[1024]{0:T(1024)}, u32[]{:S(2)}) copy-start(s32[1024]{0:T(1024)} %param.5) | copy-start | bytes 12292
  7.2 54.6 %all-gather.2.cloned.1.call-start = ((), (), s32[]{:S(2)}) async-start(), calls=%async_computation.9 | async-start | bytes 4456448 | tf_op jit(solution)/shard_map/all_gather | solution.py:224
  7.9 148.0 %reduce-scatter.2.cloned.1.call-start = ((), (), s32[]{:S(2)}) async-start(), calls=%async_computation.10 | async-start | bytes 2359296 | tf_op jit(solution)/shard_map/reduce_scatter | solution.py:232
  8.0 1.6 copy-start
  9.6 1.6 copy-start.1
  155.9 31.1 %copy-start.2 = (f32[128,512]{1,0:T(8,128)S(1)}, f32[128,512]{1,0:T(8,128)}, u32[]{:S(2)}) copy-start(f32[128,512]{1,0:T(8,128)} %items_ref.1) | copy-start | bytes 786436
  155.9 31.0 %copy-start.3 = (f32[128,512]{1,0:T(8,128)S(1)}, f32[128,512]{1,0:T(8,128)}, u32[]{:S(2)}) copy-start(f32[128,512]{1,0:T(8,128)} %reduce-scatter.2.cloned.1.call-done.looked_ref) | copy-start | bytes 786436
Sparse Core Ops, SparseCore 0:
  10.1 51.5 all-gather.1
  64.6 41.2 reduce-scatter.1

commit v10 on v8

--- a/solution.py
+++ b/solution.py
@@ -15,6 +15,7 @@
 
 epsilon = 1e-05
 inverse_temp = 64.0
+LOG2_E = 1.4426950408889634
 
 VMEM = pl.BlockSpec(memory_space=pltpu.VMEM)
 SMEM = pl.BlockSpec(memory_space=pltpu.SMEM)
@@ -52,12 +53,12 @@
 def scale_kernel(z_ref, codes_ref, high_ref, low_ref):
     half, width = high_ref.shape
     codes = codes_ref[pl.ds(pl.multiple_of(z_ref[0] * half, half), half)]
-    high, low = split(unit_rows(codes) * (inverse_temp / width))
+    high, low = split(unit_rows(codes) * (inverse_temp / width * LOG2_E))
     high_ref[...] = high
     low_ref[...] = low
 
 
-def chunk_kernel(high_ref, low_ref, items_ref, out_ref, sums_ref, xh_ref, xl_ref, held_ref, sems):
+def chunk_kernel(high_ref, low_ref, items_ref, out_ref, sums_ref, xh_ref, xl_ref, norm_ref, held_ref, sems):
     codes, step = high_ref.shape[0], 256
     total = items_ref.shape[0]
     edges = [0, step, total // 2, total]
@@ -72,13 +73,19 @@
         copy.wait()
         for first in range(begin, end, step):
             values = held_ref[first:first + step]
-            xh_ref[first:first + step], xl_ref[first:first + step] = split(values)
-            item_high, item_low = split(unit_rows(values))
+            power = jnp.mean(values * values, axis=-1, keepdims=True) + epsilon
+            inverse = lax.rsqrt(power)
+            item_high, item_low = split(values * inverse)
+            xh_ref[first:first + step], xl_ref[first:first + step] = item_high, item_low
+            norm = power * inverse
+            for at in range(0, step, LANES):
+                row = (first + at) // LANES
+                norm_ref[row:row + 1] = jnp.broadcast_to(norm[at:at + LANES], (LANES, LANES)).T[:1]
             for k, start in enumerate(range(0, codes, step)):
                 code_high = high_ref[start:start + step]
                 code_low = low_ref[start:start + step]
                 logits = dot_nt(code_high, item_high) + (dot_nt(code_high, item_low) + dot_nt(code_low, item_high))
-                values = jnp.exp(logits)
+                values = jnp.exp2(logits)
                 out_ref[start:start + step, first:first + step] = values
                 for lane in range(0, step, LANES):
                     folded[k] = folded[k] + values[:, lane:lane + LANES]
@@ -126,7 +133,7 @@
         out_ref[peer] = tile
 
 
-def numer_kernel(total_items, count, nx, near, cores, got_ref, *refs):
+def numer_kernel(total_items, count, nx, near, cores, got_ref, norm_ref, *refs):
     high_refs, low_refs, out_ref = refs[count:2 * count], refs[2 * count:3 * count], refs[3 * count]
     scales = row_scales(total_items, got_ref)
     codes, width = refs[0].shape[0], high_refs[0].shape[1]
@@ -142,7 +149,7 @@
             for lane in range(0, ref.shape[1], LANES):
                 weights = ref[start:start + step, lane:lane + LANES] * scales[at]
                 folded = folded + weights
-                high, low = split(weights)
+                high, low = split(weights * norm_ref[at:at + 1])
                 highs.append(high)
                 lows.append(low)
                 at += 1
@@ -235,13 +242,14 @@
     looked = lax.psum_scatter(named, "code", scatter_dimension=0, tiled=True)
     group = gathered.shape[0]
     part = jax.ShapeDtypeStruct((group, width), jnp.bfloat16)
-    kernel_vals, col_tile, item_high, item_low = call(
+    kernel_vals, col_tile, item_high, item_low, norms = call(
         chunk_kernel,
         (
             jax.ShapeDtypeStruct((half, group), f32),
             jax.ShapeDtypeStruct((half // LANES, LANES), f32),
             part,
             part,
+            jax.ShapeDtypeStruct((group // LANES, LANES), f32),
         ),
         [VMEM, VMEM, pl.BlockSpec(memory_space=pl.ANY)],
         [pltpu.VMEM((group, width), f32), pltpu.SemaphoreType.DMA((3,))],
@@ -265,9 +273,9 @@
     numer = call(
         functools.partial(numer_kernel, total_items, count, nx, low, nc),
         jax.ShapeDtypeStruct((nx * low, tiles + 1, SUB, LANES), f32),
-        operands + [VMEM] * (2 * count),
+        operands + [VMEM] * (1 + 2 * count),
         grant=16,
-    )(got, *blocks, item_high, item_low)
+    )(got, norms, *blocks, item_high, item_low)
     numer, looked = lax.optimization_barrier((numer, looked))
     got = lax.all_to_all(numer, ("yl", "x"), 0, 0)
     peers = high * nc

time: 194 us -> 194 us (level)
  no operation moved by 1% of the time
where the time goes in v10:
time: 194 us; the launch traced here: 193 us
  blocking collectives  113 us (58%)
  waiting for transfers between devices  45.7 us (24%)
  Pallas kernels  18.4 us (9%)
  between operations  14.2 us (7%)
  local copies, waits for them, and re-layouts  2.35 us (1%)
    all_gather x1, waiting for transfers between devices, body(): gathered = lax.all_gather(items, ('core', 'code'), axis=0, tiled=True)  45 us
    all_to_all x3, blocking collectives, body(): got = lax.all_to_all(cols, ('yh', 'yl', 'x'), 0, 0)  41.6 us
    all_to_all x3, blocking collectives, body(): got = lax.all_to_all(rows, ('core', 'code'), 0, 0)  40 us
    all_to_all x1, blocking collectives, body(): got = lax.all_to_all(numer, ('yl', 'x'), 0, 0)  17.1 us
    all_to_all x1, blocking collectives, body(): got = lax.all_to_all(packed, ('core', 'yh'), 0, 0)  13.9 us
    pallas_call x1, Pallas kernels, body(): call(lookup_kernel, jax.ShapeDtypeStruct((assign.shape[0], width), f32),...  5.56 us
    pallas_call x1, Pallas kernels, body(): call(chunk_kernel, (jax.ShapeDtypeStruct((half, group), f32), jax.ShapeDt...  5.44 us
  transfers between devices with their start and end apart: 2, of which 1 were waited for; matrix products, arithmetic and copies ran while one was open for 0% of the time, Pallas kernels for 9%

profile of v10, /device:TPU:1, one launch (start us, length us, event | category | flops | bytes accessed | tf_op | source)
XLA Modules:
  0.0 193.4 jit_solution(15319390843754953821)
XLA Ops:
  7.2 0.0 copy-start.4
  7.2 0.0 all-gather.2.cloned.1.call-start
  7.2 0.7 all-gather.2.cloned.1.call-update
  7.9 0.0 reduce-scatter.2.cloned.1.call-start
  8.0 0.1 pad_add_fusion.z_ref
  8.0 1.6 copy-done
  9.6 0.8 shard_map.51
  10.5 0.0 copy-done.4
  10.5 0.7 copy-done.1
  11.2 5.6 %shard_map.50 = f32[1024,512]{1,0:T(8,128)} custom-call(s32[2]{0:T(128)S(1)} %pad_add_fusion.z_ref, s32[8,128]{1,0:T(8,128)S(1)} %bitcast.4, f32[1024,512]{1,0:T(8,128)S(1)} %copy-done.1), custom_call_target="tpu_custom_call" | custom-call | tf_op jit(solution)/shard_map/pallas_call | solution.py:238
  16.8 45.0 %all-gather.2.cloned.1.call-done.items_ref = f32[2048,512]{1,0:T(8,128)} async-done(((f32[128,512]{1,0:T(8,128)}), f32[2048,512]{1,0:T(8,128)}) %all-gather.2.cloned.1.call-update) | async-done | bytes 4194320 | tf_op jit(solution)/shard_map/all_gather | solution.py:234
  61.7 0.0 reduce-scatter.2.cloned.1.call-update
  61.8 5.4 %shard_map.52 = (f32[512,2048]{1,0:T(8,128)S(1)}, f32[4,128]{1,0:T(4,128)S(1)}, bf16[2048,512]{1,0:T(8,128)(2,1)S(1)}, bf16[2048,512]{1,0:T(8,128)(2,1)S(1)}, f32[16,128]{1,0:T(8,128)S(1)}) custom-call(bf16[512,512]{1,0:T(8,128)(2,1)S(1)} %get-tuple-element.19.high_ref, bf16[512,512]{1,0:T(8,128)(2,1)S(1)} %get-tuple-element.20.low_ref, ...), custom_call_target="tpu_custom_call" | custom-call | tf_op jit(solution)/shard_map/pallas_call | solution.py:245
  67.2 17.9 %all_to_all.40.got_ref = f32[32,4,128]{2,1,0:T(4,128)S(1)} all-to-all(f32[32,4,128]{2,1,0:T(4,128)S(1)} %broadcast_in_dim.2), channel_id=1, replica_groups=mesh['x'=4,'yh'=4,'yl'=2,'core'=2,'code'=8] {'yh','yl','x'}, dimensions={0} | all-to-all | bytes 131072 | tf_op jit(solution)/shard_map/all_to_all | solution.py:265
  85.2 0.4 shard_map.53
  85.6 14.5 %all_to_all.41.got_ref = f32[16,16,128]{2,1,0:T(8,128)S(1)} all-to-all(f32[16,16,128]{2,1,0:T(8,128)S(1)} %shard_map.53), channel_id=1, replica_groups=mesh['x'=4,'yh'=4,'yl'=2,'core'=2,'code'=8] {'core','code'}, dimensions={0} | all-to-all | bytes 262144 | tf_op jit(solution)/shard_map/all_to_all | solution.py:267
  100.1 0.4 shard_map.54
  100.5 11.8 %all_to_all.42.got_ref = f32[32,4,128]{2,1,0:T(4,128)S(1)} all-to-all(f32[32,4,128]{2,1,0:T(4,128)S(1)} %shard_map.54), channel_id=1, replica_groups=mesh['x'=4,'yh'=4,'yl'=2,'core'=2,'code'=8] {'yh','yl','x'}, dimensions={0} | all-to-all | bytes 131072 | tf_op jit(solution)/shard_map/all_to_all | solution.py:265
  112.3 0.4 shard_map.55
  112.7 12.7 %all_to_all.43.got_ref = f32[16,16,128]{2,1,0:T(8,128)S(1)} all-to-all(f32[16,16,128]{2,1,0:T(8,128)S(1)} %shard_map.55), channel_id=1, replica_groups=mesh['x'=4,'yh'=4,'yl'=2,'core'=2,'code'=8] {'core','code'}, dimensions={0} | all-to-all | bytes 262144 | tf_op jit(solution)/shard_map/all_to_all | solution.py:267
  125.5 0.4 shard_map.56
  125.9 11.8 %all_to_all.44.got_ref = f32[32,4,128]{2,1,0:T(4,128)S(1)} all-to-all(f32[32,4,128]{2,1,0:T(4,128)S(1)} %shard_map.56), channel_id=1, replica_groups=mesh['x'=4,'yh'=4,'yl'=2,'core'=2,'code'=8] {'yh','yl','x'}, dimensions={0} | all-to-all | bytes 131072 | tf_op jit(solution)/shard_map/all_to_all | solution.py:265
  137.7 0.4 shard_map.57
  138.1 12.8 %all_to_all.45.got_ref = f32[16,16,128]{2,1,0:T(8,128)S(1)} all-to-all(f32[16,16,128]{2,1,0:T(8,128)S(1)} %shard_map.57), channel_id=1, replica_groups=mesh['x'=4,'yh'=4,'yl'=2,'core'=2,'code'=8] {'core','code'}, dimensions={0} | all-to-all | bytes 262144 | tf_op jit(solution)/shard_map/all_to_all | solution.py:267
  151.0 3.7 %shard_map.58 = f32[8,33,8,128]{3,2,1,0:T(8,128)S(1)} custom-call(f32[16,16,128]{2,1,0:T(8,128)S(1)} %all_to_all.45.got_ref, f32[16,128]{1,0:T(8,128)S(1)} %get-tuple-element.24.norm_ref, f32[512,2048]{1,0:T(8,128)S(1)} %get-tuple-element.23.refs_0_, bf16[2048,512]{1,0:T(8,128)(2,1)S(1)} %get-tuple-element.25.refs_1_, ...), custom_call_target="tpu_custom_call" | custom-call | tf_op jit(solution)/shard_map/pallas_call | solution.py:273
  154.7 0.0 copy-start.2
  154.7 0.0 reduce-scatter.2.cloned.1.call-done.looked_ref
  154.8 0.0 copy-start.3
  154.8 17.1 %all_to_all.46.got_ref = f32[8,33,8,128]{3,2,1,0:T(8,128)S(1)} all-to-all(f32[8,33,8,128]{3,2,1,0:T(8,128)S(1)} %shard_map.58), channel_id=1, replica_groups=mesh['x'=4,'yh'=4,'yl'=2,'core'=2,'code'=8] {'yl','x'}, dimensions={0} | all-to-all | bytes 2162688 | tf_op jit(solution)/shard_map/all_to_all | solution.py:280
  171.8 0.1 shard_map.59
  171.9 13.9 %all_to_all.47.got_ref = f32[8,5,8,128]{3,2,1,0:T(8,128)S(1)} all-to-all(f32[8,5,8,128]{3,2,1,0:T(8,128)S(1)} %shard_map.59), channel_id=1, replica_groups=mesh['x'=4,'yh'=4,'yl'=2,'core'=2,'code'=8] {'core','yh'}, dimensions={0} | all-to-all | bytes 327680 | tf_op jit(solution)/shard_map/all_to_all | solution.py:283
  185.8 0.7 shard_map.60
  (5 shorter events, 0.0 us)
Async XLA Ops:
  7.2 3.3 %copy-start.4 = (s32[1024]{0:T(1024)S(1)}, s32[1024]{0:T(1024)}, u32[]{:S(2)}) copy-start(s32[1024]{0:T(1024)} %param.5) | copy-start | bytes 12292
  7.2 54.6 %all-gather.2.cloned.1.call-start = ((), (), s32[]{:S(2)}) async-start(), calls=%async_computation.9 | async-start | bytes 4456448 | tf_op jit(solution)/shard_map/all_gather | solution.py:234
  7.9 146.9 %reduce-scatter.2.cloned.1.call-start = ((), (), s32[]{:S(2)}) async-start(), calls=%async_computation.10 | async-start | bytes 2359296 | tf_op jit(solution)/shard_map/reduce_scatter | solution.py:242
  8.0 1.6 copy-start
  9.6 1.6 copy-start.1
  154.7 31.1 %copy-start.2 = (f32[128,512]{1,0:T(8,128)S(1)}, f32[128,512]{1,0:T(8,128)}, u32[]{:S(2)}) copy-start(f32[128,512]{1,0:T(8,128)} %items_ref.1) | copy-start | bytes 786436
  154.8 31.0 %copy-start.3 = (f32[128,512]{1,0:T(8,128)S(1)}, f32[128,512]{1,0:T(8,128)}, u32[]{:S(2)}) copy-start(f32[128,512]{1,0:T(8,128)} %reduce-scatter.2.cloned.1.call-done.looked_ref) | copy-start | bytes 786436
Sparse Core Ops, SparseCore 0:
  10.1 51.5 all-gather.1
  64.6 41.1 reduce-scatter.1
